TPU v7x, 32 devices: a whole 2x2x4 slice. The times are simulated.
32 devices in a mesh: dp: 16 (over z, y, core), tensor: 2 (over x).
Axes of the slice: x: 2, y: 2, z: 4, core: 2. Of those that a mesh axis runs over, the one named last changes fastest.
Arguments:
- tokens: bfloat16 [24576, 896], P('dp'), may hold values from -6 to 6
- cotangent: bfloat16 [24576, 896], P('dp'), may hold values from -6 to 6
- order: int32 [16, 1536], P('dp'), may hold values from 0 to 1535, each once within a row
- lengths: int32 [16, 3], P('dp'), may hold values from 1 to 1024, 1536 in all within a row
- adapter_ids: int32 [16, 3], P('dp'), may hold values from 0 to 7
- norm_gains: bfloat16 [2, 896], replicated, may hold values from 0.099609375 to 1.8984375
- w_query: bfloat16 [896, 896], P(None, 'tensor'), may hold values from -0.25 to 0.25
- w_key: bfloat16 [896, 128], P(None, 'tensor'), may hold values from -0.25 to 0.25
- w_value: bfloat16 [896, 128], P(None, 'tensor'), may hold values from -0.1875 to 0.1875
- b_query: bfloat16 [896], P('tensor'), may hold values from -3 to 3
- b_key: bfloat16 [128], P('tensor'), may hold values from -3 to 3
- b_value: bfloat16 [128], P('tensor'), may hold values from -3 to 3
- w_out: bfloat16 [896, 896], P('tensor'), may hold values from -0.25 to 0.25
- w_gate: bfloat16 [896, 4864], P(None, 'tensor'), may hold values from -0.1875 to 0.1875
- w_up: bfloat16 [896, 4864], P(None, 'tensor'), may hold values from -0.1875 to 0.1875
- w_down: bfloat16 [4864, 896], P('tensor'), may hold values from -0.078125 to 0.078125
- adapters: float32 [22912, 128], P(('dp', 'tensor'))
- first_moment: float32 [22912, 128], P(('dp', 'tensor'))
- second_moment: float32 [22912, 128], P(('dp', 'tensor')), as said below
Outputs:
- layer_output: bfloat16 [24576, 896], P('dp')
- input_grad: bfloat16 [24576, 896], P('dp')
- adapter_grad: float32 [22912, 128], P(('dp', 'tensor'))
- first_moment_new: float32 [22912, 128], P(('dp', 'tensor'))
- second_moment_new: float32 [22912, 128], P(('dp', 'tensor'))
- adapters_new: float32 [22912, 128], P(('dp', 'tensor'))
- adapter_copy: bfloat16 [22912, 128], P(('dp', 'tensor'))
Inputs may be any that keep to these rules, and one draw needn't show every extreme that they name: Each row of order is a permutation of 0 to 1535. Each row of lengths sums to 1536 and holds a sequence of exactly 1024 tokens. `second_moment`: positive.
All inputs are finite; a program needn't handle non-finite values.
Results may differ from a plain program's by a relative error of at most 0.017.
Values may be sent and summed in bfloat16 or wider, within the bound.
A program may use at most 256 MiB of HBM per device.

v0:
```python
import functools

import jax
import jax.numpy as jnp
from jax import lax
from jax.experimental import pallas as pl
from jax.experimental.pallas import tpu as pltpu
from jax.sharding import PartitionSpec as P

HEAD = 64
RANK = 16
STEP = 3

ADAPTER_SCALE = 2.0
NORM_EPS = 1e-06
ROPE_BASE = 1000000.0
BETA_ONE = 0.5
BETA_TWO = 0.6
LEARN_RATE = 0.04
WEIGHT_DECAY = 0.01
ADAM_EPS = 1e-08
MASKED_SCORE = -1e30
PLANES = 4
FLAT_PAD = 64
MESH = pl.DeviceIdType.MESH

LANES = 128
ROW_TILE = 256
QUERY_TILE = 128
KEY_TILE = 256
HIDDEN_TILE = 512

F32 = jnp.float32
BF16 = jnp.bfloat16
I32 = jnp.int32


def nn(left, right):
    return lax.dot_general(left, right, (((1,), (0,)), ((), ())), preferred_element_type=F32)


def nt(left, right):
    return lax.dot_general(left, right, (((1,), (1,)), ((), ())), preferred_element_type=F32)


def tn(left, right):
    return lax.dot_general(left, right, (((0,), (0,)), ((), ())), preferred_element_type=F32)


def lane_iota(shape):
    return lax.broadcasted_iota(I32, shape, 1)


def row_iota(shape):
    return lax.broadcasted_iota(I32, shape, 0)


def whole(array):
    return pl.BlockSpec(array.shape, lambda *_: (0,) * array.ndim)


def row_blocks(array, tile):
    return pl.BlockSpec((tile, array.shape[1]), lambda i, *_: (i, 0))


def rows_from(array, start, count):
    return pl.BlockSpec(
        (pl.Element(count), pl.Element(array.shape[1])), lambda *_: (start, 0)
    )


def lane_table(table):
    return jnp.transpose(jnp.concatenate([table] * (LANES // table.shape[0]), axis=0))


def rank_mask(adapter_col, width):
    return jnp.where(lane_iota((adapter_col.shape[0], width)) // RANK == adapter_col, 1.0, 0.0)


def turn(values):
    lanes = lane_iota(values.shape) % HEAD
    return jnp.where(
        lanes < HEAD // 2,
        -pltpu.roll(values, LANES - HEAD // 2, 1),
        pltpu.roll(values, HEAD // 2, 1),
    )


def rms(values):
    return lax.rsqrt(jnp.mean(values * values, axis=-1, keepdims=True) + NORM_EPS)


def norm_back(values, gain, grad):
    inverse = rms(values)
    weighted = grad * gain
    return inverse * weighted - values * inverse * inverse * inverse * jnp.mean(
        weighted * values, axis=-1, keepdims=True
    )


def pick_rows(place_col, slots):
    hit = place_col == lane_iota((place_col.shape[0], slots))
    return jnp.where(hit, 1.0, 0.0).astype(BF16)


def place_rows(place_row, slots):
    hit = row_iota((slots, place_row.shape[1])) == place_row
    return jnp.where(hit, 1.0, 0.0).astype(BF16)


def params(**more):
    return pltpu.CompilerParams(vmem_limit_bytes=60 * 1024 * 1024, **more)


def cost(flops, moved):
    return pl.CostEstimate(flops=int(flops), bytes_accessed=int(moved), transcendentals=0)


def xor_bit(value, bit):
    size = 2**bit
    return value + size * (1 - 2 * lax.rem(value // size, 2))


def subsets(axes):
    out = [()]
    for axis in axes:
        out += [chosen + (axis,) for chosen in out]
    return out


def flip(place, part, axes):
    for axis in axes:
        if axis == "tensor":
            part = 1 - part
        else:
            place = xor_bit(place, axis)
    return place, part


def front_kernel(
    devices, rows_ref, chunk_ref, wq_ref, wo_ref, got_ref, copies_ref, wq_out, wo_out,
    local_sem, tsend, trecv, csend, crecv, wsend, wrecv,
):
    place, part = lax.axis_index("dp"), lax.axis_index("tensor")
    plane = devices // PLANES
    depth, inside = place // plane, lax.rem(place, plane)
    core = lax.rem(place, 2)
    own = 2 * place + part
    units = chunk_ref.shape[0]

    def rows_of(index):
        return copies_ref.at[pl.ds(index * units, units)]

    barrier = pltpu.get_barrier_semaphore()
    for k in range(1, devices):
        pl.semaphore_signal(
            barrier, inc=1, device_id=(lax.rem(place + k, devices), part), device_id_type=MESH
        )
    pl.semaphore_signal(barrier, inc=1, device_id=(place, 1 - part), device_id_type=MESH)
    pl.semaphore_wait(barrier, devices)

    keep = [
        pltpu.make_async_copy(chunk_ref, rows_of(own), local_sem.at[0]),
        pltpu.make_async_copy(rows_ref.at[place, part], got_ref.at[place], local_sem.at[1]),
    ]
    for copy in keep:
        copy.start()
    sent = []

    def chunk_copy(source, index, number, where):
        return pltpu.make_async_remote_copy(
            src_ref=source,
            dst_ref=rows_of(index),
            send_sem=csend.at[number],
            recv_sem=crecv.at[index],
            device_id=where,
            device_id_type=MESH,
        )

    def send_chunk(source, index, where):
        copy = chunk_copy(source, index, len(sent), where)
        copy.start()
        sent.append(copy)

    def take_chunk(index):
        chunk_copy(chunk_ref, index, 0, (place, 1 - part)).wait_recv()

    def layer(turn):
        return lax.rem(depth + turn, PLANES)

    for turn in (2, 3, 1):
        send_chunk(chunk_ref, own, (layer(turn) * plane + inside, part))

    def weight_copy(ref, out, number, slot, where):
        return pltpu.make_async_remote_copy(
            src_ref=ref.at[slot],
            dst_ref=out.at[slot],
            send_sem=wsend.at[number],
            recv_sem=wrecv.at[number],
            device_id=where,
            device_id_type=MESH,
        )

    direct = [
        weight_copy(wq_ref, wq_out, 0, core, (place, 1 - part)),
        weight_copy(wo_ref, wo_out, 1, core, (place, 1 - part)),
    ]
    for copy in direct:
        copy.start()

    rows_sent = []
    for turn in (2, 3, 1, 0):
        for step in range(plane):
            if turn == 0 and step == 0:
                continue
            target = layer(turn) * plane + lax.rem(inside + step, plane)
            copy = pltpu.make_async_remote_copy(
                src_ref=rows_ref.at[target, part],
                dst_ref=got_ref.at[place],
                send_sem=tsend.at[len(rows_sent)],
                recv_sem=trecv.at[place],
                device_id=(target, part),
                device_id_type=MESH,
            )
            copy.start()
            rows_sent.append((copy, target))

    bits = [2**b for b in range(plane.bit_length() - 1)]
    bits = list(range(len(bits)))[::-1]
    orders = [["tensor"] + bits, bits[:-1] + ["tensor"] + bits[-1:]]
    relayed = []
    for stage in range(len(bits) + 1):
        for turn in (0, 1, 2, 3):
            order = orders[turn % 2]
            origin = layer(turn) * plane + inside
            where = flip(place, part, [order[stage]])
            for chosen in subsets(order[:stage]):
                at, side = flip(origin, part, chosen)
                index = 2 * at + side
                if turn == 0 and not chosen:
                    send_chunk(chunk_ref, index, where)
                    continue
                if stage == 0 or order[stage - 1] in chosen:
                    take_chunk(index)
                send_chunk(rows_of(index), index, where)
        if stage == 0:
            partner = (xor_bit(place, 0), part)
            for number, (ref, out) in enumerate(((wq_ref, wq_out), (wo_ref, wo_out))):
                direct[number].wait_recv()
                copy = weight_copy(out, out, 2 + number, core, partner)
                copy.start()
                relayed.append(copy)
    for turn in (0, 1, 2, 3):
        order = orders[turn % 2]
        origin = layer(turn) * plane + inside
        for chosen in subsets(order):
            if order[-1] in chosen:
                at, side = flip(origin, part, chosen)
                take_chunk(2 * at + side)
    for number, (ref, out) in enumerate(((wq_ref, wq_out), (wo_ref, wo_out))):
        weight_copy(out, out, 2 + number, 1 - core, (place, 1 - part)).wait_recv()
    for copy, source in rows_sent:
        pltpu.make_async_remote_copy(
            src_ref=rows_ref.at[source, part],
            dst_ref=got_ref.at[source],
            send_sem=tsend.at[0],
            recv_sem=trecv.at[source],
            device_id=(source, part),
            device_id_type=MESH,
        ).wait_recv()
    for copy, _ in rows_sent:
        copy.wait_send()
    for copy in sent + direct + relayed:
        copy.wait_send()
    for copy in keep:
        copy.wait()


def front(rows, chunk, wq, wo, devices):
    _, _, piece, width = rows.shape
    anywhere = pl.BlockSpec(memory_space=pl.ANY)
    outs = [
        jax.ShapeDtypeStruct((devices, piece, width), BF16),
        jax.ShapeDtypeStruct((2 * devices * chunk.shape[0],) + chunk.shape[1:], BF16),
        jax.ShapeDtypeStruct(wq.shape, BF16),
        jax.ShapeDtypeStruct(wo.shape, BF16),
    ]
    return pl.pallas_call(
        functools.partial(front_kernel, devices),
        in_specs=[anywhere] * 4,
        out_specs=[anywhere] * 4,
        out_shape=outs,
        scratch_shapes=[
            pltpu.SemaphoreType.DMA((2,)),
            pltpu.SemaphoreType.DMA((devices,)),
            pltpu.SemaphoreType.DMA((devices,)),
            pltpu.SemaphoreType.DMA((2 * devices,)),
            pltpu.SemaphoreType.DMA((2 * devices,)),
            pltpu.SemaphoreType.DMA((4,)),
            pltpu.SemaphoreType.DMA((4,)),
        ],
        compiler_params=pltpu.CompilerParams(collective_id=0, has_side_effects=True),
        cost_estimate=cost(0, 100e6),
        name="front",
    )(rows, chunk, wq, wo)


def in_order(part, mine, theirs, place):
    @pl.when(part == 0)
    def _():
        place(mine, theirs)

    @pl.when(part == 1)
    def _():
        place(theirs, mine)


def project_kernel(
    part_ref, x_ref, meta_ref, turns_ref, sines_ref, gain_ref, mine_ref, theirs_ref, flat_ref,
    n_ref, q_ref, kv_ref, z_ref, cos_ref, sin_ref, w_ref, bias,
):
    width = x_ref.shape[1]
    qw, kw = q_ref.shape[1], kv_ref.shape[1] // 2
    rank = flat_ref.shape[1]
    low = qw + 2 * kw
    a_rows, b_rows = [], []
    cursor = 0
    for size in (qw, kw, kw):
        a_rows.append(slice(cursor, cursor + width))
        b_rows.append(slice(cursor + width, cursor + width + size))
        cursor += width + size

    @pl.when(pl.program_id(0) == 0)
    def _():
        def fill(first, second):
            at, to = 0, 0
            for size in (qw // 2, kw // 2, kw // 2):
                cut = slice(at, at + size)
                both = jnp.concatenate(
                    [first[:width, cut].astype(F32), second[:width, cut].astype(F32)], axis=1
                )
                w_ref[:, to : to + 2 * size] = both.astype(BF16)
                extra = jnp.concatenate(
                    [first[width : width + 8, cut].astype(F32), second[width : width + 8, cut].astype(F32)],
                    axis=1,
                )
                bias[:, to : to + 2 * size] = extra
                at += size
                to += 2 * size

        in_order(part_ref[0], mine_ref, theirs_ref, fill)
        for i, rows in enumerate(a_rows):
            w_ref[:, low + i * rank : low + (i + 1) * rank] = flat_ref[rows, :]

    values = x_ref[...].astype(F32)
    normed = (values * rms(values) * gain_ref[...]).astype(BF16)
    n_ref[...] = normed
    base = nn(normed, w_ref[...])
    mask = rank_mask(meta_ref[:, 0:1], rank)
    lows = [(base[:, low + i * rank : low + (i + 1) * rank] * mask).astype(BF16) for i in range(3)]
    for i in range(3):
        z_ref[:, i * rank : (i + 1) * rank] = lows[i]
    cos, sin = lane_table(turns_ref[...]), lane_table(sines_ref[...])
    cos_ref[...] = cos
    sin_ref[...] = sin
    queries = base[:, :qw] + bias[0:1, :qw] + ADAPTER_SCALE * nt(lows[0], flat_ref[b_rows[0], :])
    for pair in range(qw // LANES):
        part = queries[:, pair * LANES : (pair + 1) * LANES]
        turned = (part * cos + turn(part) * sin) * HEAD**-0.5
        q_ref[:, pair * LANES : (pair + 1) * LANES] = turned.astype(BF16)
    keys = base[:, qw : qw + kw] + bias[0:1, qw : qw + kw] + ADAPTER_SCALE * nt(lows[1], flat_ref[b_rows[1], :])
    kv_ref[:, :kw] = (keys * cos + turn(keys) * sin).astype(BF16)
    vals = base[:, qw + kw : low] + bias[0:1, qw + kw : low] + ADAPTER_SCALE * nt(lows[2], flat_ref[b_rows[2], :])
    kv_ref[:, kw:] = vals.astype(BF16)


def project(part, x, meta, turns, sines, gain, mine, theirs, flat, qw, kw):
    rows, width = x.shape
    rank = flat.shape[1]
    tile = ROW_TILE
    early = 3 * width + qw + 2 * kw
    columns = pl.BlockSpec((turns.shape[0], tile), lambda i, *_: (0, i))
    outs = [
        jax.ShapeDtypeStruct((rows, width), BF16),
        jax.ShapeDtypeStruct((rows, qw), BF16),
        jax.ShapeDtypeStruct((rows, 2 * kw), BF16),
        jax.ShapeDtypeStruct((rows, 3 * rank), BF16),
        jax.ShapeDtypeStruct((rows, LANES), F32),
        jax.ShapeDtypeStruct((rows, LANES), F32),
        jax.ShapeDtypeStruct((width, qw + 2 * kw + 3 * rank), BF16),
    ]
    return pl.pallas_call(
        project_kernel,
        grid_spec=pltpu.PrefetchScalarGridSpec(
            num_scalar_prefetch=1,
            grid=(rows // tile,),
            in_specs=[row_blocks(a, tile) for a in (x, meta)]
            + [columns, columns]
            + [whole(a) for a in (gain, mine, theirs)]
            + [rows_from(flat, 0, early)],
            out_specs=[row_blocks(o, tile) for o in outs[:6]] + [whole(outs[6])],
            scratch_shapes=[pltpu.VMEM((8, qw + 2 * kw), F32)],
        ),
        out_shape=outs,
        compiler_params=params(),
        cost_estimate=cost(2 * rows * width * 1600, 9e6),
        name="project",
    )(part, x, meta, turns, sines, gain, mine, theirs, flat)


def head_groups(heads, kv_heads):
    width = heads // kv_heads
    groups = {}
    for head in range(heads):
        groups.setdefault((head // width, head % 2), []).append(head)
    return [(kv, half, members) for (kv, half), members in sorted(groups.items())]


def spread_heads(tile_f32, kv, half, ones=False):
    lanes = lane_iota(tile_f32.shape)
    moved = tile_f32 if kv % 2 == half else pltpu.roll(tile_f32, HEAD, 1)
    keep = (lanes >= HEAD) if half else (lanes < HEAD)
    rest = jnp.where(lanes == (0 if half else HEAD), 1.0, 0.0) if ones else 0.0
    return jnp.where(keep, moved, rest)


def stack_heads(groups, source, target):
    rows = source.shape[0]
    at = 0
    for _, _, members in groups:
        for head in members:
            pair = slice((head // 2) * LANES, (head // 2 + 1) * LANES)
            target[at : at + rows, :] = source[:, pair]
            at += rows


def attend_kernel(
    heads, kv_heads, bounds_ref, all_ref, meta_ref, metar_ref, place_ref, own_ref, other_ref,
    column_ref,
    q_ref, o_ref, log_ref, merged_ref, slot_ref, keys, values, acc, top, held, stack, scores,
):
    step = pl.program_id(0)
    groups = head_groups(heads, kv_heads)
    rows = q_ref.shape[0]
    q_ref[...] = nn(pick_rows(meta_ref[:, 0:1], all_ref.shape[0]), all_ref[...]).astype(BF16)
    stack_heads(groups, q_ref, stack)

    @pl.when(step == 0)
    def _():
        both = jnp.concatenate([own_ref[...], other_ref[...]], axis=0)
        for start in range(0, keys.shape[1], KEY_TILE):
            span = slice(start, start + KEY_TILE)
            part = nn(pick_rows(column_ref[span, :], both.shape[0]), both)
            merged_ref[span, :] = part.astype(BF16)
            for number, (kv, half, _) in enumerate(groups):
                keys[number, span, :] = spread_heads(part[:, :LANES], kv, half).astype(BF16)
                turned = jnp.transpose(spread_heads(part[:, LANES:], kv, half, True))
                values[number, :, span] = turned.astype(BF16)

    acc[...] = jnp.zeros_like(acc)
    top[...] = jnp.full_like(top, MASKED_SCORE)
    first, last = metar_ref[1:2, :], metar_ref[2:3, :]
    cuts = []
    at = 0
    for _, _, members in groups:
        cuts.append(slice(at * rows, (at + len(members)) * rows))
        at += len(members)

    def find_top(number, carry):
        start = pl.multiple_of(number * KEY_TILE, KEY_TILE)
        span = pl.ds(start, KEY_TILE)
        index = start + row_iota((KEY_TILE, rows))
        bias = jnp.where((index >= first) & (index <= last), 0.0, MASKED_SCORE)
        for group, cut in enumerate(cuts):
            count = (cut.stop - cut.start) // rows
            part = nt(keys[group, span, :], stack[cut, :])
            part = part + jnp.concatenate([bias] * count, axis=1)
            scores[span, cut] = part
            most = jnp.max(part.reshape(KEY_TILE // 8, 8, -1), axis=0)
            top[:, cut] = jnp.maximum(top[:, cut], most)
        return carry

    def weigh(number, carry):
        start = pl.multiple_of(number * KEY_TILE, KEY_TILE)
        span = pl.ds(start, KEY_TILE)
        for group, cut in enumerate(cuts):
            weights = jnp.exp(scores[span, cut] - top[0:1, cut]).astype(BF16)
            acc[:, cut] += nn(values[group, :, span], weights)
        return carry

    lax.fori_loop(bounds_ref[0, step], bounds_ref[1, step], find_top, 0)
    top[0:1, :] = jnp.max(top[...], axis=0, keepdims=True)
    lax.fori_loop(bounds_ref[0, step], bounds_ref[1, step], weigh, 0)
    parts = {}
    at = 0
    for _, half, members in groups:
        for head in members:
            cut = slice(at * rows, (at + 1) * rows)
            at += 1
            block = acc[:, cut]
            sums = block[0:1, :] if half else block[HEAD : HEAD + 1, :]
            log_ref[head : head + 1, :] = top[0:1, cut] + jnp.log(sums)
            parts[head] = block / sums
    low = row_iota((LANES, rows)) < HEAD
    for pair in range(heads // 2):
        both = jnp.where(low, parts[2 * pair], parts[2 * pair + 1])
        o_ref[:, pair * LANES : (pair + 1) * LANES] = jnp.transpose(both).astype(BF16)
    for head in range(heads, log_ref.shape[0]):
        log_ref[head : head + 1, :] = jnp.zeros((1, rows), F32)
    held[pl.ds(pl.multiple_of(step * rows, rows), rows), :] = o_ref[...]

    @pl.when(step == pl.num_programs(0) - 1)
    def _():
        slot_ref[...] = nn(place_rows(place_ref[0:1, :], held.shape[0]), held[...]).astype(BF16)


def attend(bounds, q, meta, meta_rows, own_kv, other_kv, column, heads, kv_heads):
    rows, qw = q.shape
    tile = QUERY_TILE
    keys = 2 * rows
    groups = len(head_groups(heads, kv_heads))
    outs = [
        jax.ShapeDtypeStruct((rows, qw), BF16),
        jax.ShapeDtypeStruct((rows, qw), BF16),
        jax.ShapeDtypeStruct((16, rows), F32),
        jax.ShapeDtypeStruct((keys, own_kv.shape[1]), BF16),
        jax.ShapeDtypeStruct((rows, qw), BF16),
    ]
    return pl.pallas_call(
        functools.partial(attend_kernel, heads, kv_heads),
        grid_spec=pltpu.PrefetchScalarGridSpec(
            num_scalar_prefetch=1,
            grid=(rows // tile,),
            in_specs=[
                whole(q),
                row_blocks(meta, tile),
                pl.BlockSpec((8, tile), lambda i, *_: (0, i)),
                whole(meta_rows),
                whole(own_kv),
                whole(other_kv),
                whole(column),
            ],
            out_specs=[
                row_blocks(outs[0], tile),
                row_blocks(outs[1], tile),
                pl.BlockSpec((16, tile), lambda i, *_: (0, i)),
                whole(outs[3]),
                whole(outs[4]),
            ],
            scratch_shapes=[
                pltpu.VMEM((groups, keys, LANES), BF16),
                pltpu.VMEM((groups, LANES, keys), BF16),
                pltpu.VMEM((LANES, heads * tile), F32),
                pltpu.VMEM((8, heads * tile), F32),
                pltpu.VMEM((rows, qw), BF16),
                pltpu.VMEM((heads * tile, LANES), BF16),
                pltpu.VMEM((keys, heads * tile), F32),
            ],
        ),
        out_shape=outs,
        compiler_params=params(),
        cost_estimate=cost(heads * rows * keys * 2000, 6e6),
        name="attend",
    )(bounds, q, meta, meta_rows, meta_rows, own_kv, other_kv, column)


def attend_back_kernel(
    heads, kv_heads, bounds_ref, q_ref, all_ref, o_ref, log_ref, meta_ref, metar_ref, cos_ref,
    sin_ref, merged_ref, column_ref, place_ref,
    gq_ref, own_ref, other_ref, keys, values, dkeys, dvalues, dq, dots, g_ref, held, stack, grads,
):
    step = pl.program_id(0)
    groups = head_groups(heads, kv_heads)
    rows = q_ref.shape[0]
    g_ref[...] = nn(pick_rows(meta_ref[:, 0:1], all_ref.shape[0]), all_ref[...]).astype(BF16)

    @pl.when(step == 0)
    def _():
        for start in range(0, keys.shape[1], KEY_TILE):
            span = slice(start, start + KEY_TILE)
            part = merged_ref[span, :].astype(F32)
            for number, (kv, half, _) in enumerate(groups):
                keys[number, span, :] = spread_heads(part[:, :LANES], kv, half).astype(BF16)
                values[number, span, :] = spread_heads(part[:, LANES:], kv, half).astype(BF16)
        dkeys[...] = jnp.zeros_like(dkeys)
        dvalues[...] = jnp.zeros_like(dvalues)

    stack_heads(groups, q_ref, stack)
    stack_heads(groups, g_ref, grads)
    dq[...] = jnp.zeros_like(dq)
    for pair in range(heads // 2):
        lanes = slice(pair * LANES, (pair + 1) * LANES)
        product = jnp.transpose(g_ref[:, lanes].astype(F32) * o_ref[:, lanes].astype(F32))
        dots[2 * pair : 2 * pair + 1, :] = jnp.sum(product[:HEAD], axis=0, keepdims=True)
        dots[2 * pair + 1 : 2 * pair + 2, :] = jnp.sum(product[HEAD:], axis=0, keepdims=True)
    first, last = metar_ref[1:2, :], metar_ref[2:3, :]

    def one_tile(number, carry):
        start = pl.multiple_of(number * KEY_TILE, KEY_TILE)
        index = start + row_iota((KEY_TILE, rows))
        bias = jnp.where((index >= first) & (index <= last), 0.0, MASKED_SCORE)
        span = pl.ds(start, KEY_TILE)
        begin = 0
        for group, (_, half, members) in enumerate(groups):
            count = len(members)
            cut = slice(begin * rows, (begin + count) * rows)
            begin += count
            logs = jnp.concatenate([log_ref[h : h + 1, :] for h in members], axis=1)
            drop = jnp.concatenate([dots[h : h + 1, :] for h in members], axis=1)
            key_part = keys[group, span, :]
            scores = nt(key_part, stack[cut, :]) + jnp.concatenate([bias] * count, axis=1)
            weights = jnp.exp(scores - logs)
            change = nt(values[group, span, :], grads[cut, :])
            dscores = (weights * (change - drop)).astype(BF16)
            dvalues[group, span, :] += nn(weights.astype(BF16), grads[cut, :])
            dkeys[group, span, :] += nn(dscores, stack[cut, :])
            back = tn(dscores, key_part)
            for at, head in enumerate(members):
                dq[head // 2, :, :] += back[at * rows : (at + 1) * rows, :]
        return carry

    lax.fori_loop(bounds_ref[0, step], bounds_ref[1, step], one_tile, 0)
    cos, sin = lane_table(cos_ref[...]), lane_table(sin_ref[...])
    for pair in range(heads // 2):
        grad = dq[pair, :, :] * HEAD**-0.5
        grad = grad * cos - turn(grad) * sin
        held[
            pl.ds(pl.multiple_of(step * rows, rows), rows), pair * LANES : (pair + 1) * LANES
        ] = grad.astype(BF16)

    @pl.when(step == pl.num_programs(0) - 1)
    def _():
        gq_ref[...] = nn(place_rows(place_ref[0:1, :], held.shape[0]), held[...]).astype(BF16)
        total = dkeys.shape[1]

        def join(ref):
            out = None
            for group, (kv, half, _) in enumerate(groups):
                part = ref[group, :, :]
                lanes = lane_iota(part.shape)
                part = jnp.where((lanes >= HEAD) if half else (lanes < HEAD), part, 0.0)
                if kv % 2 != half:
                    part = pltpu.roll(part, HEAD, 1)
                out = part if out is None else out + part
            return out.astype(BF16)

        both = jnp.concatenate([join(dkeys), join(dvalues)], axis=1)
        half_rows = own_ref.shape[0]
        for at in range(0, total, KEY_TILE):
            hit = (at + row_iota((KEY_TILE, total))) == column_ref[...]
            part = nn(jnp.where(hit, 1.0, 0.0).astype(BF16), both).astype(BF16)
            if at < half_rows:
                own_ref[at : at + KEY_TILE, :] = part
            else:
                other_ref[at - half_rows : at - half_rows + KEY_TILE, :] = part


def attend_back(
    bounds, q, grad, o, logs, meta, meta_rows, cos, sin, merged, column_row, heads, kv_heads
):
    rows, qw = q.shape
    tile = QUERY_TILE
    keys, kvw = merged.shape
    groups = len(head_groups(heads, kv_heads))
    outs = [
        jax.ShapeDtypeStruct((rows, qw), BF16),
        jax.ShapeDtypeStruct((rows, kvw), BF16),
        jax.ShapeDtypeStruct((rows, kvw), BF16),
    ]
    return pl.pallas_call(
        functools.partial(attend_back_kernel, heads, kv_heads),
        grid_spec=pltpu.PrefetchScalarGridSpec(
            num_scalar_prefetch=1,
            grid=(rows // tile,),
            in_specs=[
                row_blocks(q, tile),
                whole(grad),
                row_blocks(o, tile),
                pl.BlockSpec((16, tile), lambda i, *_: (0, i)),
                row_blocks(meta, tile),
                pl.BlockSpec((8, tile), lambda i, *_: (0, i)),
                pl.BlockSpec((cos.shape[0], tile), lambda i, *_: (0, rows // tile + i)),
                pl.BlockSpec((cos.shape[0], tile), lambda i, *_: (0, rows // tile + i)),
                whole(merged),
                whole(column_row),
                whole(meta_rows),
            ],
            out_specs=[whole(o) for o in outs],
            scratch_shapes=[
                pltpu.VMEM((groups, keys, LANES), BF16),
                pltpu.VMEM((groups, keys, LANES), BF16),
                pltpu.VMEM((groups, keys, LANES), F32),
                pltpu.VMEM((groups, keys, LANES), F32),
                pltpu.VMEM((heads // 2, tile, LANES), F32),
                pltpu.VMEM((16, tile), F32),
                pltpu.VMEM((tile, qw), BF16),
                pltpu.VMEM((rows, qw), BF16),
                pltpu.VMEM((heads * tile, LANES), BF16),
                pltpu.VMEM((heads * tile, LANES), BF16),
            ],
        ),
        out_shape=outs,
        compiler_params=params(),
        cost_estimate=cost(heads * rows * keys * 3000, 9e6),
        name="attend_back",
    )(bounds, q, grad, o, logs, meta, meta_rows, cos, sin, merged, column_row, meta_rows)


def middle_kernel(
    part_ref, o_ref, x_ref, meta_ref, mine_ref, theirs_ref, gain_ref, flat_ref,
    y_ref, n_ref, z_ref, w_ref,
):
    width = x_ref.shape[1]
    rank = flat_ref.shape[1]
    half = mine_ref.shape[0]

    @pl.when(pl.program_id(0) == 0)
    def _():
        def fill(first, second):
            w_ref[:half, :width] = first[...]
            w_ref[half:, :width] = second[...]

        in_order(part_ref[0], mine_ref, theirs_ref, fill)
        w_ref[:, width:] = flat_ref[: 2 * half, :]

    mask = rank_mask(meta_ref[:, 0:1], rank)
    base = nn(o_ref[...], w_ref[...])
    low = (base[:, width:] * mask).astype(BF16)
    z_ref[...] = low
    values = x_ref[...].astype(F32) + (base[:, :width] + ADAPTER_SCALE * nt(low, flat_ref[2 * half :, :]))
    y_ref[...] = values
    n_ref[...] = (values * rms(values) * gain_ref[...]).astype(BF16)


def middle(part, o, x, meta, mine, theirs, gain, flat, start):
    rows, width = x.shape
    rank = flat.shape[1]
    tile = ROW_TILE
    rest = (mine, theirs, gain)
    outs = [
        jax.ShapeDtypeStruct((rows, width), F32),
        jax.ShapeDtypeStruct((rows, width), BF16),
        jax.ShapeDtypeStruct((rows, rank), BF16),
        jax.ShapeDtypeStruct((o.shape[1], width + rank), BF16),
    ]
    return pl.pallas_call(
        middle_kernel,
        grid_spec=pltpu.PrefetchScalarGridSpec(
            num_scalar_prefetch=1,
            grid=(rows // tile,),
            in_specs=[row_blocks(a, tile) for a in (o, x, meta)]
            + [whole(a) for a in rest]
            + [rows_from(flat, start, o.shape[1] + width)],
            out_specs=[row_blocks(a, tile) for a in outs[:3]] + [whole(outs[3])],
        ),
        out_shape=outs,
        compiler_params=params(),
        cost_estimate=cost(2 * rows * width * 1100, 12e6),
        name="middle",
    )(part, o, x, meta, *rest, flat)


class Windows:
    def __init__(self, devices, own_rows):
        self.devices = devices
        self.own_rows = own_rows
        self.plane = devices // PLANES
        self.axes = list(range(self.plane.bit_length() - 1)) + ["tensor"]
        self.rows = 16 * ((own_rows + 30) // 16)
        self.last = 16 * (((2 * devices - 1) * own_rows) // 16) + self.rows

    def start(self, zz, at, side):
        row = (2 * (zz * self.plane + at) + side) * self.own_rows
        return pl.multiple_of((row // 16) * 16, 16)

    def span(self, zz, at, side):
        return pl.ds(self.start(zz, at, side), self.rows)

    def boxes(self, stage):
        return 2 ** (len(self.axes) - 1 - stage)

    def box(self, stage, at, side):
        index = 0
        for order, axis in enumerate(self.axes[stage + 1 :]):
            bit = side if axis == "tensor" else lax.rem(at // 2**axis, 2)
            index = index + bit * 2**order
        return index

    def leaving(self, stage, inside, part):
        for chosen in subsets(self.axes[stage + 1 :]):
            yield flip(inside, part, [self.axes[stage]] + list(chosen))

    def staying(self, stage, inside, part):
        for chosen in subsets(self.axes[stage + 1 :]):
            yield flip(inside, part, list(chosen))


def middle_back_kernel(
    plan, first_b, da_ref, db_ref, y1_ref, dy_ref, o_ref, z_ref, meta_ref, copies_ref, w_ref,
    gain_ref, flat_ref,
    dy1_ref, dar_ref, grad_ref, on_ref, kept_ref, acc_bo, acc_ao, mine, inbox, b_ref, msem, ssem,
    rsem, bsem,
):
    step = pl.program_id(0)
    b_load = pltpu.make_async_copy(
        copies_ref.at[pl.ds(first_b, b_ref.shape[0]), :], b_ref, bsem.at[0]
    )
    rank = b_ref.shape[1]
    qw = o_ref.shape[1]
    place, part = lax.axis_index("dp"), lax.axis_index("tensor")
    inside = lax.rem(place, plan.plane)
    partner = flip(place, part, [plan.axes[0]])
    boxes = plan.boxes(0)

    def moves():
        local, remote = [], []
        for zz in range(1, PLANES):
            for at, side in plan.leaving(0, inside, part):
                index = (zz - 1) * boxes + plan.box(0, at, side)
                remote.append(
                    pltpu.make_async_remote_copy(
                        src_ref=flat_ref.at[plan.span(zz, at, side), :],
                        dst_ref=inbox.at[index],
                        send_sem=ssem.at[len(remote)],
                        recv_sem=rsem.at[index],
                        device_id=partner,
                        device_id_type=MESH,
                    )
                )
            for at, side in plan.staying(0, inside, part):
                index = (zz - 1) * boxes + plan.box(0, at, side)
                local.append(
                    pltpu.make_async_copy(
                        flat_ref.at[plan.span(zz, at, side), :], mine.at[index], msem.at[len(local)]
                    )
                )
        return local, remote

    @pl.when(step == 0)
    def _():
        acc_bo[...] = jnp.zeros_like(acc_bo)
        acc_ao[...] = jnp.zeros_like(acc_ao)
        b_load.start()
        barrier = pltpu.get_barrier_semaphore()
        pl.semaphore_signal(barrier, inc=1, device_id=partner, device_id_type=MESH)
        pl.semaphore_wait(barrier, 1)
        local, remote = moves()
        for copy in remote + local:
            copy.start()
        b_load.wait()

    mask = rank_mask(meta_ref[:, 0:1], rank)
    grad = da_ref[...] + db_ref[...].astype(F32)
    dy1 = dy_ref[...].astype(F32) + norm_back(y1_ref[...], gain_ref[...], grad)
    dy1_ref[...] = dy1
    low_grad = dy1.astype(BF16)
    back_out = (ADAPTER_SCALE * nn(low_grad, b_ref[...]) * mask).astype(BF16)
    both = jnp.concatenate([low_grad, back_out], axis=1)
    dar_ref[...] = nt(both, w_ref[...]).astype(BF16)
    acc_bo[...] += ADAPTER_SCALE * tn(low_grad, z_ref[...])
    acc_ao[...] += tn(o_ref[...], back_out)

    @pl.when(step == pl.num_programs(0) - 1)
    def _():
        grad_ref[:qw, :] = acc_ao[...].astype(BF16)
        grad_ref[qw:, :] = acc_bo[...].astype(BF16)
        local, remote = moves()
        for copy in local:
            copy.wait()
        for copy in remote:
            copy.wait_recv()
        later = plan.boxes(1)

        def total(zz, at, side):
            index = (zz - 1) * boxes + plan.box(0, at, side)
            return mine[index].astype(F32) + inbox[index].astype(F32)

        for zz in range(1, PLANES):
            for at, side in plan.leaving(1, inside, part):
                on_ref[(zz - 1) * later + plan.box(1, at, side)] = total(zz, at, side).astype(BF16)
            for at, side in plan.staying(1, inside, part):
                kept_ref[(zz - 1) * later + plan.box(1, at, side)] = total(zz, at, side)
        for copy in remote:
            copy.wait_send()


def middle_back(
    devices, own_rows, d_first, d_second, y1, dy, o, z, meta, copies, start, w_out, gain, flat
):
    rows, width = y1.shape
    rank = copies.shape[1]
    qw = o.shape[1]
    tile = ROW_TILE
    plan = Windows(devices, own_rows)
    first, second = (PLANES - 1) * plan.boxes(0), (PLANES - 1) * plan.boxes(1)
    outs = [
        jax.ShapeDtypeStruct((rows, width), F32),
        jax.ShapeDtypeStruct((rows, qw), BF16),
        jax.ShapeDtypeStruct((qw + width, rank), BF16),
        jax.ShapeDtypeStruct((second, plan.rows, rank), BF16),
        jax.ShapeDtypeStruct((second, plan.rows, rank), F32),
    ]
    return pl.pallas_call(
        functools.partial(middle_back_kernel, plan, start),
        grid=(rows // tile,),
        in_specs=[row_blocks(a, tile) for a in (d_first, d_second, y1, dy, o, z, meta)]
        + [pl.BlockSpec(memory_space=pl.ANY)]
        + [whole(a) for a in (w_out, gain)]
        + [pl.BlockSpec(memory_space=pl.ANY)],
        out_specs=[row_blocks(a, tile) for a in outs[:2]] + [whole(a) for a in outs[2:]],
        out_shape=outs,
        scratch_shapes=[
            pltpu.VMEM((width, rank), F32),
            pltpu.VMEM((qw, rank), F32),
            pltpu.VMEM((first, plan.rows, rank), BF16),
            pltpu.VMEM((first, plan.rows, rank), BF16),
            pltpu.VMEM((width, rank), BF16),
            pltpu.SemaphoreType.DMA((first,)),
            pltpu.SemaphoreType.DMA((first,)),
            pltpu.SemaphoreType.DMA((first,)),
            pltpu.SemaphoreType.DMA((1,)),
        ],
        compiler_params=params(collective_id=3, has_side_effects=True),
        cost_estimate=cost(2 * rows * width * 1500, 20e6),
        name="middle_back",
    )(d_first, d_second, y1, dy, o, z, meta, copies, w_out, gain, flat)


def own_tile(step, tiles):
    return jnp.maximum(step - tiles, 0)


def their_tile(step, tiles):
    return jnp.clip(step - 1, 0, tiles - 1)


def feed_kernel(
    n_ref, n_hbm, dy_ref, dyt_ref, meta_ref, metat_ref, wg_hbm, wu_hbm,
    wd_hbm, copies,
    y_ref, d_ref, y_got, d_got, last_ref, flat_ref,
    wga, wua, wda, raw, grads, extras, xg, xu, dya, yacc, dacc, mask_s, n_got, held_d, held_y,
    packed, blank, ap_ref, bd_ref, wsem, gsem, nsend, nrecv, dsend, drecv, ysend, yrecv,
):
    step = pl.program_id(0)
    steps = pl.num_programs(0)
    tiles_each = n_got.shape[0]
    width, half = wg_hbm.shape
    rank = bd_ref.shape[1]
    rows = n_ref.shape[0]
    place, part = lax.axis_index("dp"), lax.axis_index("tensor")
    theirs = (step >= 1) & (step <= tiles_each)
    number_t = their_tile(step, tiles_each)
    tile = HIDDEN_TILE
    tiles = pl.cdiv(half, tile)
    lap = tiles * tile - half
    a_gate = copies.shape[0] - 3 * width - 6 * half
    a_up = a_gate + width + 2 * half
    a_down = a_up + width + 2 * half
    b_down = a_down + 2 * half

    def loads(number):
        at = pl.multiple_of(jnp.minimum(number * tile, half - tile), LANES)
        to = pl.multiple_of(number * tile, tile)
        here, there = pl.ds(at, tile), pl.ds(to, tile)

        def own_half(base):
            return copies.at[pl.ds(pl.multiple_of(base + part * half + at, 16), tile), :]

        top, side = pl.ds(0, width), pl.ds(width, rank)
        pairs = [
            (wg_hbm.at[:, here], wga.at[top, there]),
            (wu_hbm.at[:, here], wua.at[top, there]),
            (wd_hbm.at[here, :], wda.at[there, top]),
            (own_half(a_gate + width), raw.at[0, there, :]),
            (own_half(a_up + width), raw.at[1, there, :]),
            (own_half(a_down), wda.at[there, side]),
        ]
        return [
            pltpu.make_async_copy(source, target, wsem.at[number, at])
            for at, (source, target) in enumerate(pairs)
        ]

    def swap(source, target, sends, recvs, number):
        return pltpu.make_async_remote_copy(
            src_ref=source,
            dst_ref=target.at[number],
            send_sem=sends.at[number],
            recv_sem=recvs.at[number],
            device_id=(place, 1 - part),
            device_id_type=MESH,
        )

    def send_n(number):
        return swap(n_hbm.at[pl.ds(number * rows, rows), :], n_got, nsend, nrecv, number)

    def send_d(number):
        return swap(held_d.at[number], d_got, dsend, drecv, number)

    def send_y(number):
        return swap(held_y.at[number], y_got, ysend, yrecv, number)

    thin_loads = [
        pltpu.make_async_copy(copies.at[pl.ds(base, width), :], target, gsem.at[at])
        for at, (base, target) in enumerate(
            (
                (a_gate, ap_ref.at[:, pl.ds(0, rank)]),
                (a_up, ap_ref.at[:, pl.ds(rank, rank)]),
                (b_down, bd_ref),
            )
        )
    ]

    @pl.when(step == 0)
    def _():
        for copy in thin_loads:
            copy.start()
        for number in range(tiles):
            for copy in loads(number):
                copy.start()
        barrier = pltpu.get_barrier_semaphore()
        pl.semaphore_signal(barrier, inc=1, device_id=(place, 1 - part), device_id_type=MESH)
        pl.semaphore_wait(barrier, 1)
        for number in range(tiles_each):
            send_n(number).start()
        grads[...] = jnp.zeros_like(grads)
        extras[...] = jnp.zeros_like(extras)
        for copy in thin_loads:
            copy.wait()

    def prepare(normed, dy, adapter):
        mask = rank_mask(adapter, rank)
        mask_s[...] = mask
        lows = nn(normed, ap_ref[...])
        xg[:, :width] = normed
        xu[:, :width] = normed
        xg[:, width:] = (lows[:, :rank] * mask).astype(BF16)
        xu[:, width:] = (lows[:, rank:] * mask).astype(BF16)
        dya[:, :width] = dy
        dya[:, width:] = (ADAPTER_SCALE * nn(dy, bd_ref[...]) * mask).astype(BF16)

    @pl.when(jnp.logical_not(theirs))
    def _():
        prepare(n_ref[...], dy_ref[...], meta_ref[:, 0:1])

    @pl.when(theirs)
    def _():
        send_n(number_t).wait_recv()
        prepare(n_got[number_t], dyt_ref[...], metat_ref[:, 0:1])

    yacc[...] = jnp.zeros_like(yacc)
    dacc[...] = jnp.zeros_like(dacc)

    def hidden(number, carry):
        span = pl.ds(pl.multiple_of(number * tile, tile), tile)

        @pl.when(step == 0)
        def _():
            for copy in loads(number):
                copy.wait()
            for at, target in enumerate((wga, wua)):
                turned = jnp.transpose(raw[at, span, :].astype(F32) * ADAPTER_SCALE)
                target[width:, span] = turned.astype(BF16)
            if lap:

                @pl.when(number == tiles - 1)
                def _():
                    edge = slice((tiles - 1) * tile, (tiles - 1) * tile + lap)
                    wga[:, edge] = jnp.zeros((width + rank, lap), BF16)
                    wua[:, edge] = jnp.zeros((width + rank, lap), BF16)
                    wda[edge, :] = jnp.zeros((lap, width + rank), BF16)

        gate = nn(xg[...], wga[:, span])
        up = nn(xu[...], wua[:, span])
        dhid = nt(dya[...], wda[span, :])
        sig = 1.0 / (1.0 + jnp.exp(-gate))
        silu = gate * sig
        hid = (silu * up).astype(BF16)
        dg = (dhid * up * (sig * (1.0 + gate * (1.0 - sig)))).astype(BF16)
        du = (dhid * silu).astype(BF16)
        yacc[...] += nn(hid, wda[span, :])
        dga = nt(dg, wga[:, span])
        dua = nt(du, wua[:, span])
        dacc[:, :width] += dga[:, :width] + dua[:, :width]
        dacc[:, width : width + rank] += dga[:, width:]
        dacc[:, width + rank :] += dua[:, width:]
        grads[0, span, :] += ADAPTER_SCALE * tn(dg, xg[:, width:])
        grads[1, span, :] += ADAPTER_SCALE * tn(du, xu[:, width:])
        grads[2, span, :] += tn(hid, dya[:, width:])
        return carry

    lax.fori_loop(0, tiles, hidden, 0)
    mask = mask_s[...]
    low = (yacc[:, width:] * mask).astype(BF16)
    result = yacc[:, :width] + ADAPTER_SCALE * nt(low, bd_ref[...])
    back = (dacc[:, width:] * jnp.concatenate([mask, mask], axis=1)).astype(BF16)
    change = dacc[:, :width] + nt(back, ap_ref[...])
    pair = tn(xg[:, :width], back)
    extras[0] += pair[:, :rank]
    extras[1] += pair[:, rank:]
    extras[2] += ADAPTER_SCALE * tn(dya[:, :width], low)

    @pl.when(jnp.logical_not(theirs))
    def _():
        y_ref[...] = result
        d_ref[...] = change

    @pl.when(theirs)
    def _():
        held_d[number_t] = change.astype(BF16)
        send_d(number_t).start()

        @pl.when(number_t < tiles_each - 1)
        def _():
            held_y[number_t] = result.astype(BF16)

        @pl.when(number_t == tiles_each - 1)
        def _():
            last_ref[...] = result.astype(BF16)
            for number in range(tiles_each - 1):
                send_y(number).start()

    @pl.when(step == steps - 1)
    def _():
        last = (tiles - 1) * tile
        for at in range(3):
            packed[at, :last, :] = grads[at, :last, :].astype(BF16)
            packed[at, last:half, :] = grads[at, last + lap : tiles * tile, :].astype(BF16)
            packed[at, half:, :] = extras[at].astype(BF16)
        blank[...] = jnp.zeros_like(blank)
        moves = []
        for at, base in enumerate((a_gate + width, a_up + width, a_down)):
            mine = pl.multiple_of(base + part * half, 16)
            other = pl.multiple_of(base + (1 - part) * half, 16)
            moves.append((packed.at[at, pl.ds(0, half), :], flat_ref.at[pl.ds(mine, half), :]))
            moves.append((blank, flat_ref.at[pl.ds(other, half), :]))
        for at, base in enumerate((a_gate, a_up, b_down)):
            moves.append((packed.at[at, pl.ds(half, width), :], flat_ref.at[pl.ds(base, width), :]))
        moves = [
            pltpu.make_async_copy(source, target, gsem.at[at])
            for at, (source, target) in enumerate(moves)
        ]
        for copy in moves:
            copy.start()
        for copy in moves:
            copy.wait()
        for number in range(tiles_each):
            send_n(number).wait_send()
            send_d(number).wait_send()
            send_d(number).wait_recv()
        for number in range(tiles_each - 1):
            send_y(number).wait_send()
            send_y(number).wait_recv()


def feed(n2, dy, dy_theirs, meta, meta_theirs, w_gate, w_up, w_down, copies):
    rows, width = n2.shape
    half = w_down.shape[0]
    total, rank = copies.shape
    tile = ROW_TILE
    count = rows // tile
    tiles = pl.cdiv(half, HIDDEN_TILE)
    padded = tiles * HIDDEN_TILE
    anywhere = pl.BlockSpec(memory_space=pl.ANY)
    wide, deep = width + rank, width + 2 * rank

    def own_rows(array):
        return pl.BlockSpec((tile, array.shape[1]), lambda i: (own_tile(i, count), 0))

    def their_rows(array):
        return pl.BlockSpec((tile, array.shape[1]), lambda i: (their_tile(i, count), 0))

    dma = pltpu.SemaphoreType.DMA
    outs = [
        jax.ShapeDtypeStruct((rows, width), F32),
        jax.ShapeDtypeStruct((rows, width), F32),
        jax.ShapeDtypeStruct((count - 1, tile, width), BF16),
        jax.ShapeDtypeStruct((count, tile, width), BF16),
        jax.ShapeDtypeStruct((tile, width), BF16),
        jax.ShapeDtypeStruct((total + FLAT_PAD, rank), BF16),
    ]
    return pl.pallas_call(
        feed_kernel,
        grid=(2 * count,),
        in_specs=[
            own_rows(n2), anywhere, own_rows(dy), their_rows(dy_theirs), own_rows(meta),
            their_rows(meta_theirs),
        ]
        + [anywhere] * 4,
        out_specs=[own_rows(outs[0]), own_rows(outs[1]), anywhere, anywhere, whole(outs[4]), anywhere],
        out_shape=outs,
        scratch_shapes=[
            pltpu.VMEM((wide, padded), BF16),
            pltpu.VMEM((wide, padded), BF16),
            pltpu.VMEM((padded, wide), BF16),
            pltpu.VMEM((2, padded, rank), BF16),
            pltpu.VMEM((3, padded, rank), F32),
            pltpu.VMEM((3, width, rank), F32),
            pltpu.VMEM((tile, wide), BF16),
            pltpu.VMEM((tile, wide), BF16),
            pltpu.VMEM((tile, wide), BF16),
            pltpu.VMEM((tile, wide), F32),
            pltpu.VMEM((tile, deep), F32),
            pltpu.VMEM((tile, rank), F32),
            pltpu.VMEM((count, tile, width), BF16),
            pltpu.VMEM((count, tile, width), BF16),
            pltpu.VMEM((count - 1, tile, width), BF16),
            pltpu.VMEM((3, half + width, rank), BF16),
            pltpu.VMEM((half, rank), BF16),
            pltpu.VMEM((width, 2 * rank), BF16),
            pltpu.VMEM((width, rank), BF16),
            dma((tiles, 6)),
            dma((9,)),
            dma((count,)),
            dma((count,)),
            dma((count,)),
            dma((count,)),
            dma((count - 1,)),
            dma((count - 1,)),
        ],
        compiler_params=params(collective_id=1, has_side_effects=True),
        cost_estimate=cost(4 * rows * half * (6 * width + 9 * rank), 40e6),
        name="feed",
    )(
        n2, n2, dy, dy_theirs, meta, meta_theirs, w_gate, w_up, w_down, copies
    )


def tail_kernel(plan, early, key_width, direct, *refs):
    sources = refs[:9]
    other_ref, w_hbm, b_ref, gain_ref, flat_ref, out_grad_ref, kept_hbm, gots_hbm = refs[9:17]
    out_ref, sum_ref = refs[17:19]
    held = refs[19:28]
    w, grads, dxs, acc_a, acc_b, outbox, last_in, got_s, kept, gots, *rest = refs[28:]
    inboxes = rest[:-13]
    (
        load_sem, grad_sem, dsend, drecv, fsend, frecv, rsend, rrecv, zrecv, keep_sem, ksend, krecv,
        hsem,
    ) = rest[-13:]
    gq_s, own_s, x_s, n_s, z_s, dy1_s, meta_s, cos_s, sin_s = held
    place, part = lax.axis_index("dp"), lax.axis_index("tensor")
    devices, plane, axes = plan.devices, plan.plane, plan.axes
    depth, inside = place // plane, lax.rem(place, plane)
    count = len(axes)
    tile = x_s.shape[1]
    rank = b_ref.shape[1]
    width = x_s.shape[2]
    qw, kw = gq_s.shape[2], key_width
    over = (place, 1 - part)

    def layer(hop):
        return lax.rem(depth + hop, PLANES)

    def turn_of(number):
        return lax.rem(number + 2, PLANES)

    def rows_at(number):
        return pl.ds(pl.multiple_of(layer(turn_of(number)) * tile, 16), tile)

    def tile_loads(number):
        return [
            pltpu.make_async_copy(
                source.at[rows_at(number), :], target.at[number], load_sem.at[number, which]
            )
            for which, (source, target) in enumerate(zip(sources, held))
        ]

    sums_loads = [
        pltpu.make_async_copy(kept_hbm, kept, grad_sem.at[3]),
        pltpu.make_async_copy(gots_hbm, gots, grad_sem.at[4]),
    ]
    w_load = pltpu.make_async_copy(w_hbm, w, grad_sem.at[0])
    middle = out_grad_ref.shape[0]
    late_rows = grads.shape[0] - early - middle
    grad_loads = [
        pltpu.make_async_copy(out_grad_ref, grads.at[pl.ds(early, middle), :], grad_sem.at[1]),
        pltpu.make_async_copy(
            flat_ref.at[pl.ds(early + middle, late_rows), :],
            grads.at[pl.ds(early + middle, late_rows), :],
            grad_sem.at[2],
        ),
    ]
    for copy in sums_loads + [w_load]:
        copy.start()
    for number in range(PLANES):
        for copy in tile_loads(number):
            copy.start()
    for copy in grad_loads:
        copy.start()

    barrier = pltpu.get_barrier_semaphore()
    for k in range(1, devices):
        pl.semaphore_signal(
            barrier, inc=1, device_id=(lax.rem(place + k, devices), part), device_id_type=MESH
        )
    pl.semaphore_signal(barrier, inc=1, device_id=over, device_id_type=MESH)
    pl.semaphore_wait(barrier, devices)

    def key_copy(number):
        return pltpu.make_async_remote_copy(
            src_ref=other_ref.at[rows_at(number), :],
            dst_ref=got_s.at[number],
            send_sem=ksend.at[number],
            recv_sem=krecv.at[number],
            device_id=over,
            device_id_type=MESH,
        )

    for number in range(PLANES):
        key_copy(number).start()

    bases = []
    cursor = 0
    for stage in range(count):
        bases.append(cursor)
        cursor += plan.boxes(stage) * (1 if stage < 2 else PLANES)

    def box_of(stage, zz, at, side):
        return plan.box(stage, at, side) + (0 if stage < 2 else zz * plan.boxes(stage))

    def window_sum(stages, zz, at, side):
        if zz == 0:
            total = grads[plan.span(0, at, side), :].astype(F32)
            for stage in range(min(2, stages)):
                total = total + inboxes[stage][box_of(stage, 0, at, side)].astype(F32)
        else:
            index = (zz - 1) * plan.boxes(1) + plan.box(1, at, side)
            total = kept[index] + gots[index].astype(F32)
        for stage in range(2, stages):
            total = total + inboxes[stage][box_of(stage, zz, at, side)].astype(F32)
        return total

    def take(stages, zz, at, side):
        for stage in range(0 if zz == 0 else 2, stages):
            index = box_of(stage, zz, at, side)
            pltpu.make_async_remote_copy(
                src_ref=inboxes[stage].at[index],
                dst_ref=inboxes[stage].at[index],
                send_sem=rsend.at[0],
                recv_sem=rrecv.at[bases[stage] + index],
                device_id=over,
                device_id_type=MESH,
            ).wait_recv()

    sent = []
    posted = [0]

    def pass_on(stage, zz, source_of):
        partner = flip(place, part, [axes[stage]])
        for at, side in plan.leaving(stage, inside, part):
            index = box_of(stage, zz, at, side)
            copy = pltpu.make_async_remote_copy(
                src_ref=source_of(at, side),
                dst_ref=inboxes[stage].at[index],
                send_sem=rsend.at[len(sent)],
                recv_sem=rrecv.at[bases[stage] + index],
                device_id=partner,
                device_id_type=MESH,
            )
            copy.start()
            sent.append(copy)

    def post(total):
        slot = posted[0]
        posted[0] += 1
        outbox[slot] = total.astype(BF16)
        return outbox.at[slot]

    def stage_sends(stage, zz):
        def source_of(at, side):
            take(stage, zz, at, side)
            return post(window_sum(stage, zz, at, side))

        pass_on(stage, zz, source_of)

    for copy in sums_loads:
        copy.wait()
    for zz in range(1, PLANES):
        stage_sends(2, zz)

    def step_at(step):
        return lax.rem(inside + step, plane)

    acc_a[...] = jnp.zeros_like(acc_a)
    acc_b[...] = jnp.zeros_like(acc_b)
    w_load.wait()

    def piece_copy(number, step, where, target):
        return pltpu.make_async_remote_copy(
            src_ref=dxs.at[number, step_at(step)],
            dst_ref=target,
            send_sem=dsend.at[number, step],
            recv_sem=drecv.at[place],
            device_id=where,
            device_id_type=MESH,
        )

    def one_tile(number, carry):
        for copy in tile_loads(number):
            copy.wait()
        key_copy(number).wait_recv()
        mask = rank_mask(meta_s[number][:, 0:1], rank)
        both = own_s[number].astype(F32) + got_s[number].astype(F32)
        cos, sin = cos_s[number], sin_s[number]
        dk = both[:, :kw]
        gq = gq_s[number]
        gk = (dk * cos - turn(dk) * sin).astype(BF16)
        gv = both[:, kw:].astype(BF16)
        at_k, at_v = 2 * width + qw, 3 * width + qw + kw
        b_parts = (
            b_ref[width : width + qw, :],
            b_ref[at_k : at_k + kw, :],
            b_ref[at_v : at_v + kw, :],
        )
        backs = [
            (ADAPTER_SCALE * nn(g, b) * mask).astype(BF16) for g, b in zip((gq, gk, gv), b_parts)
        ]
        dn = nt(jnp.concatenate([gq, gk, gv] + backs, axis=1), w[...])
        values = x_s[number].astype(F32)
        dx = (dy1_s[number] + norm_back(values, gain_ref[...], dn)).astype(BF16)
        acc_a[...] += tn(n_s[number], jnp.concatenate(backs, axis=1))
        low = z_s[number]
        acc_b[:qw, :] += tn(gq, low[:, :rank])
        acc_b[qw : qw + kw, :] += tn(gk, low[:, rank : 2 * rank])
        acc_b[qw + kw :, :] += tn(gv, low[:, 2 * rank :])
        turn_now = turn_of(number)
        if not direct:
            dxs[number] = dx
            copy = pltpu.make_async_copy(
                dxs.at[number], out_ref.at[rows_at(number), :], keep_sem.at[0]
            )
            copy.start()
            copy.wait()
            return carry
        dxs[number] = dx.reshape(dxs.shape[1:])
        for step in range(plane):
            target = layer(turn_now) * plane + step_at(step)
            if step > 0:
                piece_copy(number, step, (target, part), out_ref.at[place, part]).start()
                continue

            @pl.when(turn_now == 0)
            def _():
                pltpu.make_async_copy(
                    dxs.at[number, inside], out_ref.at[place, part], keep_sem.at[0]
                ).start()

            @pl.when(turn_now > 0)
            def _():
                piece_copy(number, 0, (target, part), out_ref.at[place, part]).start()

        return carry

    lax.fori_loop(0, PLANES, one_tile, 0)
    for copy in grad_loads:
        copy.wait()

    at = 0
    for order, size in enumerate((qw, kw, kw)):
        grads[at : at + width, :] = acc_a[:, order * rank : (order + 1) * rank].astype(BF16)
        base = (0, qw, qw + kw)[order]
        grads[at + width : at + width + size, :] = (
            ADAPTER_SCALE * acc_b[base : base + size, :]
        ).astype(BF16)
        at += width + size
    pass_on(0, 0, lambda at, side: grads.at[plan.span(0, at, side), :])

    forwards = []

    def forward(back):
        source = layer(back)
        for step in range(plane):
            at = source * plane + step_at(step)
            if step > 0 or back > 0:
                pltpu.make_async_remote_copy(
                    src_ref=out_ref.at[at, part],
                    dst_ref=out_ref.at[at, part],
                    send_sem=hsem.at[0],
                    recv_sem=drecv.at[at],
                    device_id=over,
                    device_id_type=MESH,
                ).wait_recv()
            else:
                pltpu.make_async_copy(
                    out_ref.at[place, part], out_ref.at[place, part], keep_sem.at[0]
                ).wait()
        copy = forward_copy(source, part, len(forwards))
        copy.start()
        forwards.append(copy)

    def forward_copy(source, side, number):
        span = pl.ds(source * plane, plane)
        return pltpu.make_async_remote_copy(
            src_ref=out_ref.at[span, side],
            dst_ref=out_ref.at[span, side],
            send_sem=fsend.at[number],
            recv_sem=frecv.at[source],
            device_id=over,
            device_id_type=MESH,
        )

    zsends = []

    def across_planes(zz):
        take(count, zz, inside, part)
        total = window_sum(count, zz, inside, part)
        slot = posted[0]
        posted[0] += 1
        number = len(sent) + len(zsends)
        copy = pltpu.make_async_remote_copy(
            src_ref=outbox.at[slot],
            dst_ref=last_in.at[depth],
            send_sem=rsend.at[number],
            recv_sem=zrecv.at[depth],
            device_id=(zz * plane + inside, part),
            device_id_type=MESH,
        )
        zsends.append((zz, copy))

        @pl.when(depth != zz)
        def _():
            outbox[slot] = total.astype(BF16)
            copy.start()

        @pl.when(depth == zz)
        def _():
            sum_ref[...] = total

    if direct:
        forward(0)
    for stage in range(3, count):
        for zz in (1, 2, 3):
            stage_sends(stage, zz)
    for zz in (1, 2, 3):
        across_planes(zz)
    stage_sends(1, 0)
    if direct:
        forward(3)
        forward(1)
    for stage in range(2, count):
        stage_sends(stage, 0)
    across_planes(0)
    if direct:
        forward(2)
    for hop in (1, 2, 3):
        source = layer(hop)
        pltpu.make_async_remote_copy(
            src_ref=last_in.at[source],
            dst_ref=last_in.at[source],
            send_sem=hsem.at[0],
            recv_sem=zrecv.at[source],
            device_id=over,
            device_id_type=MESH,
        ).wait_recv()
        sum_ref[...] += last_in[source].astype(F32)

    if direct:
        for back in range(PLANES):
            forward_copy(layer(back), 1 - part, 0).wait_recv()
        for copy in forwards:
            copy.wait_send()
        for number in range(PLANES):
            for step in range(plane):
                if step == 0 and (number + 2) % PLANES == 0:
                    continue
                piece_copy(number, step, over, out_ref.at[place, part]).wait_send()
    for copy in sent:
        copy.wait_send()
    for zz, copy in zsends:

        @pl.when(depth != zz)
        def _():
            copy.wait_send()

    for number in range(PLANES):
        key_copy(number).wait_send()


def tail(
    devices, own_rows, early, rows_in, other, w_cat, b_rows, gain, flat, grad_out, kept, gots,
    key_width, piece,
):
    gq, _, x = rows_in[:3]
    rows, width = x.shape
    plan = Windows(devices, own_rows)
    plane, count, window = plan.plane, len(plan.axes), plan.rows
    rank = flat.shape[1]
    tile = rows // PLANES
    direct = piece % 16 == 0
    anywhere = pl.BlockSpec(memory_space=pl.ANY)
    boxes = [plan.boxes(stage) * (1 if stage < 2 else PLANES) for stage in range(count)]
    sends = sum(boxes) + PLANES
    qw = gq.shape[1]
    first_plane = 16 * (((2 * plane - 1) * own_rows) // 16) + window
    dma = pltpu.SemaphoreType.DMA
    if direct:
        shape = (devices, 2, piece, width)
        held = (plane, piece, width)
    else:
        shape = (rows, width)
        held = (tile, width)
    outs = [jax.ShapeDtypeStruct(shape, BF16)]
    outs.append(jax.ShapeDtypeStruct((window, rank), F32))
    scratch = [pltpu.VMEM((PLANES, tile, a.shape[1]), a.dtype) for a in rows_in]
    scratch += [
        pltpu.VMEM(w_cat.shape, BF16),
        pltpu.VMEM((first_plane, rank), BF16),
        pltpu.VMEM((PLANES,) + held, BF16),
        pltpu.VMEM((width, 3 * rank), F32),
        pltpu.VMEM((qw + 2 * key_width, rank), F32),
        pltpu.VMEM((sends, window, rank), BF16),
        pltpu.VMEM((PLANES, window, rank), BF16),
        pltpu.VMEM((PLANES, tile, other.shape[1]), BF16),
        pltpu.VMEM(kept.shape, F32),
        pltpu.VMEM(gots.shape, BF16),
    ]
    scratch += [pltpu.VMEM((size, window, rank), BF16) for size in boxes]
    scratch += [
        dma((PLANES, len(rows_in))),
        dma((5,)),
        dma((PLANES, plane)),
        dma((devices,)),
        dma((PLANES,)),
        dma((PLANES,)),
        dma((sends,)),
        dma((sum(boxes),)),
        dma((PLANES,)),
        dma((1,)),
        dma((PLANES,)),
        dma((PLANES,)),
        dma((1,)),
    ]
    return pl.pallas_call(
        functools.partial(tail_kernel, plan, early, key_width, direct),
        grid=(1,),
        in_specs=[anywhere] * 11
        + [pl.BlockSpec((early, rank), lambda i: (0, 0)), whole(gain)]
        + [anywhere] * 4,
        out_specs=[anywhere, whole(outs[1])],
        out_shape=outs,
        scratch_shapes=scratch,
        compiler_params=params(collective_id=2, has_side_effects=True),
        cost_estimate=cost(2 * rows * width * 2900, 200e6),
        name="tail",
    )(*rows_in, other, w_cat, b_rows, gain, flat, grad_out, kept, gots)


def row_tables(order_row, lengths_row, adapter_row, part, parts, each):
    total = order_row.shape[0]
    piece = each // parts
    local = total // parts
    places = jnp.arange(total, dtype=I32)
    own = (order_row % each) // piece == part
    slot = (order_row // each) * piece + order_row % piece
    column = jnp.where(own, slot, local + slot)
    upto = jnp.sum((own[None, :] & (places[None, :] <= places[:, None])).astype(I32), axis=1)
    rank = jnp.where(own, upto - 1, total)
    picks = rank[None, :] == jnp.arange(local, dtype=I32)[:, None]
    sorted_place = jnp.sum(jnp.where(picks, places[None, :], 0), axis=1)
    sorted_slot = jnp.sum(jnp.where(picks, slot[None, :], 0), axis=1)
    slot_place = jnp.sum(jnp.where(column[None, :] == places[:, None], places[None, :], 0), axis=1)
    ends = jnp.cumsum(lengths_row)
    starts = ends - lengths_row
    both = jnp.concatenate([slot_place, sorted_place])
    member = (both[:, None] >= starts[None, :]) & (both[:, None] < ends[None, :])
    first = jnp.sum(jnp.where(member, starts[None, :], 0), axis=1)
    chosen = jnp.sum(jnp.where(member, adapter_row[None, :], 0), axis=1)
    position = both - first
    sorted_first = first[total:]
    bounds = jnp.stack(
        [
            sorted_first[::QUERY_TILE] // KEY_TILE,
            sorted_place[QUERY_TILE - 1 :: QUERY_TILE] // KEY_TILE + 1,
        ]
    )
    blank = jnp.zeros_like(sorted_place)
    meta_sorted = jnp.stack([sorted_slot, sorted_first, sorted_place] + [blank] * 5, axis=1)
    meta_rows = jnp.stack([sorted_slot, sorted_first, sorted_place] + [blank] * 5, axis=0)
    meta_own = jnp.broadcast_to(chosen[:local, None], (local, 8))
    meta_other = jnp.broadcast_to(chosen[local:total, None], (local, 8))
    slot_position = position[:local]
    return (
        meta_own, meta_other, meta_sorted, meta_rows, slot_position, position[total:], column, bounds,
    )


def rope_tables(position):
    freq_index = jnp.arange(HEAD // 2, dtype=F32)
    inv_freq = jnp.power(jnp.float32(ROPE_BASE), -2.0 * freq_index / HEAD)
    angles = position.astype(F32)[None, :] * inv_freq[:, None]
    return jnp.cos(angles), jnp.sin(angles)


def per_device(
    tokens, cotangent, order, lengths, adapter_ids, norm_gains, w_query, w_key, w_value,
    b_query, b_key, b_value, w_out, w_gate, w_up, w_down, adapters, first_moment, second_moment,
):
    parts = lax.axis_size("tensor")
    part = lax.axis_index("tensor")
    devices = lax.axis_size("dp")
    place = lax.axis_index("dp")
    total, width = tokens.shape
    each = total // devices
    piece = each // parts
    local = total // parts
    rank = adapters.shape[1]
    own_rows = adapters.shape[0]
    swap = [(i, parts - 1 - i) for i in range(parts)]
    first_part = part == 0

    def across(values):
        return lax.ppermute(values, "tensor", swap)

    def pair(mine, theirs, axis):
        return jnp.concatenate(
            [jnp.where(first_part, mine, theirs), jnp.where(first_part, theirs, mine)], axis=axis
        )

    def give_back(values):
        got = lax.all_to_all(
            values.reshape(devices, piece, width), "dp", split_axis=0, concat_axis=0, tiled=True
        )
        theirs = across(got)
        return pair(got[:, None], theirs[:, None], 1).reshape(total, width)

    qh, kh, half = w_query.shape[1], w_key.shape[1], w_gate.shape[1]
    qw, kw, hidden = parts * qh, parts * kh, parts * half
    heads, kv_heads = qw // HEAD, kw // HEAD
    mine_qkv = jnp.concatenate(
        [
            jnp.concatenate([w_query, w_key, w_value], axis=1),
            jnp.broadcast_to(
                jnp.concatenate([b_query, b_key, b_value])[None], (32, qh + 2 * kh)
            ),
        ],
        axis=0,
    )
    lines = mine_qkv.shape[0]
    unit = 4 if own_rows % 4 == 0 else 1
    moved, copies, their_qkv, their_out = front(
        tokens.reshape(devices, parts, piece, width),
        adapters.astype(BF16).reshape(own_rows // unit, unit, rank),
        mine_qkv.reshape(2, lines // 2, -1),
        w_out.reshape(2, w_out.shape[0] // 2, width),
        devices,
    )
    cotangent, moved = lax.optimization_barrier((cotangent, moved))
    moved = moved.reshape(local, width)
    dy_all = lax.all_to_all(
        cotangent.reshape(devices, each, width), "dp", split_axis=0, concat_axis=0, tiled=True
    ).reshape(devices, parts, piece, width)

    def half_of(which):
        return lax.dynamic_index_in_dim(dy_all, which, 1, keepdims=False).reshape(local, width)

    dy = half_of(part)
    dy_theirs = half_of(parts - 1 - part)

    early = 3 * width + qw + 2 * kw
    flat = copies.reshape(2 * devices * own_rows, rank)
    meta_own, meta_other, meta_sorted, meta_rows, slot_position, sorted_position, column, bounds = (
        row_tables(order[0], lengths[0], adapter_ids[0], part, parts, each)
    )
    turns, sines = rope_tables(jnp.concatenate([slot_position, sorted_position]))
    gain_one = norm_gains[0:1].astype(F32)
    gain_two = norm_gains[1:2].astype(F32)
    side = jnp.reshape(part, (1,)).astype(I32)

    n1, q, kv, z, cos, sin, w_cat = project(
        side, moved, meta_own, turns, sines, gain_one, mine_qkv, their_qkv.reshape(mine_qkv.shape),
        flat, qw, kw,
    )
    other_kv = across(kv)
    q_sorted, o_sorted, logs, merged, o = attend(
        bounds, q, meta_sorted, meta_rows, kv, other_kv, column[:, None], heads, kv_heads
    )
    y1, n2, z_out, w_out_cat = middle(
        side, o, moved, meta_own, w_out, their_out.reshape(w_out.shape), gain_two, flat, early
    )
    y_own, d_own, y_got, d_got, y_last, flat_grads = feed(
        n2, dy, dy_theirs, meta_own, meta_other, w_gate, w_up, w_down, flat
    )
    y_got = jnp.concatenate([y_got, across(y_last)[None]], axis=0).reshape(local, width)
    dy1, dar, grad_out, on_sums, kept_sums = middle_back(
        devices, own_rows, d_own, d_got.reshape(local, width), y1, dy, o, z_out, meta_own, flat,
        early + qw, w_out_cat, gain_two, flat_grads,
    )
    got_sums = lax.ppermute(on_sums, "dp", [(i, i ^ 2) for i in range(devices)])
    layer_rows = (y1 + (y_own + y_got.astype(F32))).astype(BF16).reshape(devices, 1, piece, width)
    layer_rows = jnp.broadcast_to(layer_rows, (devices, parts, piece, width))
    layer_rows, dar = lax.optimization_barrier((layer_rows, dar))
    layer_out = lax.all_to_all(
        layer_rows.reshape(devices * parts, piece, width),
        ("dp", "tensor"), split_axis=0, concat_axis=0, tiled=True,
    ).reshape(total, width)
    gq, dkv_own, dkv_other = attend_back(
        bounds, q_sorted, dar, o_sorted, logs, meta_sorted, meta_rows, turns, sines,
        merged, column[None, :], heads, kv_heads,
    )
    dx, window = tail(
        devices, own_rows, early,
        (gq, dkv_own, moved, n1, z, dy1, meta_own, cos, sin),
        dkv_other, w_cat, flat, gain_one, flat_grads, grad_out, kept_sums,
        got_sums, kw, piece,
    )
    if dx.ndim == 4:
        input_grad = dx.reshape(total, width)
    else:
        input_grad = give_back(dx)
    offset = lax.rem((2 * place + part) * own_rows, 16)
    reduced = lax.dynamic_slice_in_dim(window, offset, own_rows, 0)
    moment_one = BETA_ONE * first_moment + (1.0 - BETA_ONE) * reduced
    moment_two = BETA_TWO * second_moment + (1.0 - BETA_TWO) * reduced * reduced
    corrected_one = moment_one / (1.0 - BETA_ONE**STEP)
    corrected_two = moment_two / (1.0 - BETA_TWO**STEP)
    updated = adapters - LEARN_RATE * (
        corrected_one / (jnp.sqrt(corrected_two) + ADAM_EPS) + WEIGHT_DECAY * adapters
    )
    return (
        layer_out,
        input_grad,
        reduced,
        moment_one,
        moment_two,
        updated,
        updated.astype(BF16),
    )


def solution(mesh):
    both = P(("dp", "tensor"), None)
    rows = P("dp", None)
    return jax.shard_map(
        per_device,
        mesh=mesh,
        in_specs=(rows, rows, rows, rows, rows, P())
        + (P(None, "tensor"),) * 3
        + (P("tensor"),) * 3
        + (P("tensor", None), P(None, "tensor"), P(None, "tensor"), P("tensor", None))
        + (both,) * 3,
        out_specs=(rows, rows) + (both,) * 5,
        check_vma=False,
    )
```

profile of v0, /device:TPU:1, one launch (start us, length us, event | category | flops | bytes accessed | tf_op | source)
XLA Modules:
  0.0 399.4 jit_solution(14867787024991466505)
XLA Ops:
  0.7 1.0 convert_element_type.32
  2.5 1.1 copy.63
  3.5 1.1 copy.64
  4.6 1.5 copy.62
  6.2 1.3 pad_maximum_fusion.1.mine_ref
  7.5 58.0 %front.1 = (bf16[16,48,896]{2,1,0:T(8,128)(2,1)}, bf16[5728,4,128]{2,1,0:T(4,128)(2,1)}, bf16[2,464,576]{2,1,0:T(8,128)(2,1)}, bf16[2,224,896]{2,1,0:T(8,128)(2,1)}) custom-call(bf16[16,2,48,896]{3,2,1,0:T(8,128)(2,1)} %bitcast.57, bf16[179,4,128]{2,1,0:T(4,128)(2,1)} %reshape.246.chunk_ref, bf16[2,464,576]{2,1,0:T(8,128)(2,1)} %bitcast.52, ...), custom_call_target="tpu_custom_call" | custom-call | bytes 100000000 | tf_op jit(solution)/shard_map/front/pallas_call | solution.py:288
  65.6 12.4 %all-to-all-start = ((bf16[16,96,896]{2,1,0:T(8,128)(2,1)}), bf16[16,96,896]{2,1,0:T(8,128)(2,1)S(1)}, u32[]{:S(2)}, u32[]{:S(2)}) async-start(bf16[16,96,896]{2,1,0:T(8,128)(2,1)} %bitcast.58), calls=%async_computation | async-start | bytes 5505024 | tf_op jit(solution)/shard_map/all_to_all | solution.py:1748
  79.5 1.0 select_reduce_fusion
  80.9 1.4 select_reduce_fusion.1
  83.1 1.5 multiply_sine_fusion
  85.5 10.1 %project.1 = (bf16[768,896]{1,0:T(8,128)(2,1)}, bf16[768,896]{1,0:T(8,128)(2,1)}, bf16[768,256]{1,0:T(8,128)(2,1)}, bf16[768,384]{1,0:T(8,128)(2,1)}, f32[768,12...) custom-call(s32[1]{0:T(128)} %bitcast.part_ref, bf16[768,896]{1,0:T(8,128)(2,1)} %bitcast.46, ...), custom_call_target="tpu_custom_call" | custom-call | flops 2202009600 | bytes 9000000 | tf_op jit(solution)/shard_map/project/pallas_call | solution.py:392
  95.6 1.3 collective-permute-start
  100.0 1.0 copy.69
  102.9 1.2 copy.65
  104.1 1.2 copy.72
  105.3 1.3 stack.51.metar_ref.place_ref
  107.9 3.4 add_select_fusion.column_ref
  111.3 25.4 %attend.1 = (bf16[768,896]{1,0:T(8,128)(2,1)}, bf16[768,896]{1,0:T(8,128)(2,1)}, f32[16,768]{1,0:T(8,128)}, bf16[1536,256]{1,0:T(8,128)(2,1)}, bf16[768,896]{1,0:T(8,128)(2,1)}) custom-call(s32[2,6]{1,0:T(2,128)} %pad_add_fusion.1.bounds_ref, bf16[768,896]{1,0:T(8,128)(2,1)} %get-tuple-element.51.all_ref, s32[768,8]{1,0:T(8,128)} %copy.76.meta_ref, ...), custom_call_target="tpu_custom_call" | custom-call | flops 33030144000 | bytes 6000000 | tf_op jit(solution)/shard_map/attend/pallas_call | solution.py:529
  136.7 7.1 %middle.1 = (f32[768,896]{1,0:T(8,128)}, bf16[768,896]{1,0:T(8,128)(2,1)}, bf16[768,128]{1,0:T(8,128)(2,1)}, bf16[896,1024]{1,0:T(8,128)(2,1)}) custom-call(s32[1]{0:T(128)} %bitcast.part_ref, bf16[768,896]{1,0:T(8,128)(2,1)} %get-tuple-element.53.o_ref, bf16[768,896]{1,0:T(8,128)(2,1)} %bitcast.47, s32[768,8]{1,0:T(8,128)} %broadcast_in_dim.113.meta_ref.refs_6_, ...), custom_call_target="tpu_custom_call" | custom-call | flops 1513881600 | bytes 12000000 | tf_op jit(solution)/shard_map/middle/pallas_call | solution.py:746
  143.8 1.8 constant_dynamic-slice_fusion.1
  146.5 89.3 %feed.1 = (f32[768,896]{1,0:T(8,128)}, f32[768,896]{1,0:T(8,128)}, bf16[2,256,896]{2,1,0:T(8,128)(2,1)}, bf16[3,256,896]{2,1,0:T(8,128)(2,1)}, bf16[256,896]{1,0:T(8,128)(2,1)}, /*index=5*/bf16[22976,128]{1,0:T(8,128)(2,1)}) custom-call(bf16[768,896]{1,0:T(8,128)(2,1)} %get-tuple-element.56.n_ref.n_hbm, bf16[768,896]{1,0:T(8,128)(2,1)} %get-tuple-element.56.n_ref.n_hbm, ...), custom_call_target="tpu_custom_call" | custom-call | flops 48771366912 | bytes 40000000 | tf_op jit(solution)/shard_map/feed/pallas_call | solution.py:1181
  235.9 13.1 %middle_back.1 = (f32[768,896]{1,0:T(8,128)}, bf16[768,896]{1,0:T(8,128)(2,1)}, bf16[1792,128]{1,0:T(8,128)(2,1)}, bf16[6,736,128]{2,1,0:T(8,128)(2,1)}, f32[6,736,128]{2,1,0:T(8,128)}) custom-call(f32[768,896]{1,0:T(8,128)} %get-tuple-element.61.da_ref, bf16[768,896]{1,0:T(8,128)(2,1)} %bitcast.61, f32[768,896]{1,0:T(8,128)} %get-tuple-element.55.y1_ref, ...), custom_call_target="tpu_custom_call" | custom-call | flops 2064384000 | bytes 20000000 | tf_op jit(solution)/shard_map/middle_back/pallas_call | solution.py:903
  249.0 5.2 %collective-permute-start.2 = (bf16[6,736,128]{2,1,0:T(8,128)(2,1)}, bf16[6,736,128]{2,1,0:T(8,128)(2,1)}, u32[]{:S(2)}, u32[]{:S(2)}) collective-permute-start(bf16[6,736,128]{2,1,0:T(8,128)(2,1)} %get-tuple-element.84), channel_id=1, source_target_pairs={{0,4},{2,6},{4,0},{6,2},{8,12},{10,14},{12,8},{14,10},{16,20},{18,... | collective-permute-start | bytes 3391496 | tf_op jit(solution)/shard_map/ppermute | solution.py:1787
  255.0 1.7 broadcast_in_dim.119
  256.7 4.1 %all-to-all-start.1 = ((bf16[32,48,896]{2,1,0:T(8,128)(2,1)}), bf16[32,48,896]{2,1,0:T(8,128)(2,1)S(1)}, u32[]{:S(2)}, u32[]{:S(2)}) async-start(bf16[32,48,896]{2,1,0:T(8,128)(2,1)} %bitcast.51), calls=%async_computation.1 | async-start | bytes 5505024 | tf_op jit(solution)/shard_map/all_to_all | solution.py:1791
  260.9 38.7 %attend_back.1 = (bf16[768,896]{1,0:T(8,128)(2,1)}, bf16[768,256]{1,0:T(8,128)(2,1)}, bf16[768,256]{1,0:T(8,128)(2,1)}) custom-call(s32[2,6]{1,0:T(2,128)} %pad_add_fusion.1.bounds_ref, bf16[768,896]{1,0:T(8,128)(2,1)} %get-tuple-element.68.q_ref, bf16[768,896]{1,0:T(8,128)(2,1)} %get-tuple-element.69.all_ref, bf16[768,896]{1,0:T(8,128)(2,1)} %get-tuple-element.70.o_ref, ...), custom_call_target="tpu_custom_call" | custom-call | flops 49545216000 | bytes 9000000 | tf_op jit(solution)/shard_map/attend_back/pallas_call | solution.py:670
  299.5 2.3 collective-permute-done.2.refs_16_
  301.8 90.0 %tail.1 = (bf16[16,2,48,896]{3,2,1,0:T(8,128)(2,1)}, f32[736,128]{1,0:T(8,128)}) custom-call(bf16[768,896]{1,0:T(8,128)(2,1)} %get-tuple-element.73.refs_0_, bf16[768,256]{1,0:T(8,128)(2,1)} %get-tuple-element.74.refs_1_, bf16[768,896]{1,0:T(8,128)(2,1)} %bitcast.48, bf16[768,896]{1,0:T(8,128)(2,1)} %get-tuple-element.75.refs_3_, ...), custom_call_target="tpu_custom_call" | custom-call | flops 3991142400 | bytes 200000000 | tf_op jit(solution)/shard_map/tail/pallas_call | solution.py:1632
  391.9 2.3 fusion.14
  395.1 1.5 copy.80
  396.6 1.2 copy-done.2
  397.8 1.5 copy.81
  (77 shorter events, 13.4 us)
Async XLA Ops:
  0.6 5.4 %copy-start.12 = (bf16[64]{0:T(256)(128)(2,1)S(1)}, bf16[64]{0:T(256)(128)(2,1)}, u32[]{:S(2)}) copy-start(bf16[64]{0:T(256)(128)(2,1)} %param.30) | copy-start | bytes 388
  0.6 5.4 %copy-start.13 = (bf16[64]{0:T(256)(128)(2,1)S(1)}, bf16[64]{0:T(256)(128)(2,1)}, u32[]{:S(2)}) copy-start(bf16[64]{0:T(256)(128)(2,1)} %param.29) | copy-start | bytes 388
  0.7 5.4 %copy-start.10 = (bf16[448]{0:T(512)(128)(2,1)S(1)}, bf16[448]{0:T(512)(128)(2,1)}, u32[]{:S(2)}) copy-start(bf16[448]{0:T(512)(128)(2,1)} %param.28) | copy-start | bytes 2692
  65.5 12.5 %copy-start.14 = (s32[1,3]{1,0:T(1,128)S(1)}, s32[1,3]{1,0:T(1,128)}, u32[]{:S(2)}) copy-start(s32[1,3]{1,0:T(1,128)} %param.22) | copy-start | bytes 40
  65.5 12.6 %copy-start.9 = (bf16[2,896]{1,0:T(2,128)(2,1)S(1)}, bf16[2,896]{1,0:T(2,128)(2,1)}, u32[]{:S(2)}) copy-start(bf16[2,896]{1,0:T(2,128)(2,1)} %param.24) | copy-start | bytes 10756
  65.5 13.2 %copy-start.7 = (s32[1,1536]{1,0:T(1,128)S(1)}, s32[1,1536]{1,0:T(1,128)}, u32[]{:S(2)}) copy-start(s32[1,1536]{1,0:T(1,128)} %param.21) | copy-start | bytes 18436
  65.5 16.8 %copy-start.11 = (s32[1,3]{1,0:T(1,128)S(1)}, s32[1,3]{1,0:T(1,128)}, u32[]{:S(2)}) copy-start(s32[1,3]{1,0:T(1,128)} %param.23) | copy-start | bytes 40
  65.6 78.3 %all-to-all-start = ((bf16[16,96,896]{2,1,0:T(8,128)(2,1)}), bf16[16,96,896]{2,1,0:T(8,128)(2,1)S(1)}, u32[]{:S(2)}, u32[]{:S(2)}) async-start(bf16[16,96,896]{2,1,0:T(8,128)(2,1)} %bitcast.58), calls=%async_computation | async-start | bytes 5505024 | tf_op jit(solution)/shard_map/all_to_all | solution.py:1748
  95.6 15.7 %collective-permute-start = (bf16[768,256]{1,0:T(8,128)(2,1)}, bf16[768,256]{1,0:T(8,128)(2,1)}, u32[]{:S(2)}, u32[]{:S(2)}) collective-permute-start(bf16[768,256]{1,0:T(8,128)(2,1)} %get-tuple-element.52.own_ref), channel_id=1, source_target_pairs={{0,1},{1,0},{2,3},{3,2},{4,5},{5,4},{6,7},{7,6},{8,9},{9,8},{10,11... | collective-permute-start | bytes 1179656 | tf_op jit(solution)/shard_map/ppermute | solution.py:1711
  143.8 1.8 copy-start.8
  235.8 18.4 %collective-permute-start.1 = (bf16[256,896]{1,0:T(8,128)(2,1)}, bf16[256,896]{1,0:T(8,128)(2,1)S(1)}, u32[]{:S(2)}, u32[]{:S(2)}) collective-permute-start(bf16[256,896]{1,0:T(8,128)(2,1)} %get-tuple-element.60), channel_id=1, source_target_pairs={{0,1},{1,0},{2,3},{3,2},{4,5},{5,4},{6,7},{7,6},{8,9},{9,8},{10,11... | collective-permute-start | bytes 1376264 | tf_op jit(solution)/shard_map/ppermute | solution.py:1711
  235.9 18.3 %copy-start.6 = (bf16[2,256,896]{2,1,0:T(8,128)(2,1)S(1)}, bf16[2,256,896]{2,1,0:T(8,128)(2,1)}, u32[]{:S(2)}) copy-start(bf16[2,256,896]{2,1,0:T(8,128)(2,1)} %get-tuple-element.59) | copy-start | bytes 2752516
  235.9 18.4 %copy-start.1 = (f32[768,896]{1,0:T(8,128)S(1)}, f32[768,896]{1,0:T(8,128)}, u32[]{:S(2)}) copy-start(f32[768,896]{1,0:T(8,128)} %get-tuple-element.58) | copy-start | bytes 8257540
  249.0 5.4 %copy-start = (f32[768,896]{1,0:T(8,128)S(1)}, f32[768,896]{1,0:T(8,128)}, u32[]{:S(2)}) copy-start(f32[768,896]{1,0:T(8,128)} %get-tuple-element.55.y1_ref) | copy-start | bytes 8257540
  249.0 52.8 %collective-permute-start.2 = (bf16[6,736,128]{2,1,0:T(8,128)(2,1)}, bf16[6,736,128]{2,1,0:T(8,128)(2,1)}, u32[]{:S(2)}, u32[]{:S(2)}) collective-permute-start(bf16[6,736,128]{2,1,0:T(8,128)(2,1)} %get-tuple-element.84), channel_id=1, source_target_pairs={{0,4},{2,6},{4,0},{6,2},{8,12},{10,14},{12,8},{14,10},{16,20},{18,... | collective-permute-start | bytes 3391496 | tf_op jit(solution)/shard_map/ppermute | solution.py:1787
  256.7 138.3 %all-to-all-start.1 = ((bf16[32,48,896]{2,1,0:T(8,128)(2,1)}), bf16[32,48,896]{2,1,0:T(8,128)(2,1)S(1)}, u32[]{:S(2)}, u32[]{:S(2)}) async-start(bf16[32,48,896]{2,1,0:T(8,128)(2,1)} %bitcast.51), calls=%async_computation.1 | async-start | bytes 5505024 | tf_op jit(solution)/shard_map/all_to_all | solution.py:1791
  301.8 90.0 %copy-start.3 = (f32[716,128]{1,0:T(8,128)S(1)}, f32[716,128]{1,0:T(8,128)}, u32[]{:S(2)}) copy-start(f32[716,128]{1,0:T(8,128)} %param.35) | copy-start | bytes 1099780
  301.8 90.0 %copy-start.4 = (f32[716,128]{1,0:T(8,128)S(1)}, f32[716,128]{1,0:T(8,128)}, u32[]{:S(2)}) copy-start(f32[716,128]{1,0:T(8,128)} %param.36) | copy-start | bytes 1099780
  394.2 2.4 copy-start.5
  395.1 2.8 copy-start.2
where the time goes:
time: 401 us; the launch traced here: 399 us
  Pallas kernels  332 us (83%)
  local copies, waits for them, and re-layouts  24.4 us (6%)
  starting transfers between devices  23.1 us (6%)
  other arithmetic  16.9 us (4%)
    pallas_call x1, Pallas kernels, tail(): pl.pallas_call(functools.partial(tail_kernel, plan, early, key_width, dir...  90 us
    pallas_call x1, Pallas kernels, feed(): pl.pallas_call(feed_kernel, grid=(2 * count,), in_specs=[own_rows(n2), an...  89.3 us
    pallas_call x1, Pallas kernels, front(): pl.pallas_call(functools.partial(front_kernel, devices), in_specs=[anywhe...  58 us
    pallas_call x1, Pallas kernels, attend_back(): pl.pallas_call(functools.partial(attend_back_kernel, heads, kv_heads), gr...  38.7 us
    pallas_call x1, Pallas kernels, attend(): pl.pallas_call(functools.partial(attend_kernel, heads, kv_heads), grid_sp...  25.4 us
    pallas_call x1, Pallas kernels, middle_back(): pl.pallas_call(functools.partial(middle_back_kernel, plan, start), grid=(...  13.1 us
    all_to_all x1, starting transfers between devices, per_device(): lax.all_to_all(cotangent.reshape(devices, each, width), 'dp', split_axis=...  12.4 us
    pallas_call x1, Pallas kernels, project(): pl.pallas_call(project_kernel, grid_spec=pltpu.PrefetchScalarGridSpec(num...  10.1 us
  transfers between devices with their start and end apart: 5, of which 1 were waited for; matrix products, arithmetic and copies ran while one was open for 7% of the time, Pallas kernels for 46%

commit v1 on v0

--- a/solution.py
+++ b/solution.py
@@ -128,6 +128,15 @@
     return out
 
 
+def flip_fixed(place, part, axes):
+    for axis in axes:
+        if axis == "tensor":
+            part = 1 - part
+        else:
+            place = place ^ 2**axis
+    return place, part
+
+
 def flip(place, part, axes):
     for axis in axes:
         if axis == "tensor":
@@ -138,7 +147,8 @@
 
 
 def front_kernel(
-    devices, rows_ref, chunk_ref, wq_ref, wo_ref, got_ref, copies_ref, wq_out, wo_out,
+    devices, rows_ref, chunk_ref, wq_ref, wk_ref, wv_ref, bias_ref,
+    got_ref, copies_ref, wq_out, wk_out, wv_out, bias_out,
     local_sem, tsend, trecv, csend, crecv, wsend, wrecv,
 ):
     place, part = lax.axis_index("dp"), lax.axis_index("tensor")
@@ -146,26 +156,22 @@
     depth, inside = place // plane, lax.rem(place, plane)
     core = lax.rem(place, 2)
     own = 2 * place + part
+    over = (place, 1 - part)
     units = chunk_ref.shape[0]
 
     def rows_of(index):
         return copies_ref.at[pl.ds(index * units, units)]
+
+    def layer(hop):
+        return lax.rem(depth + hop, PLANES)
 
     barrier = pltpu.get_barrier_semaphore()
     for k in range(1, devices):
         pl.semaphore_signal(
             barrier, inc=1, device_id=(lax.rem(place + k, devices), part), device_id_type=MESH
         )
-    pl.semaphore_signal(barrier, inc=1, device_id=(place, 1 - part), device_id_type=MESH)
+    pl.semaphore_signal(barrier, inc=1, device_id=over, device_id_type=MESH)
     pl.semaphore_wait(barrier, devices)
-
-    keep = [
-        pltpu.make_async_copy(chunk_ref, rows_of(own), local_sem.at[0]),
-        pltpu.make_async_copy(rows_ref.at[place, part], got_ref.at[place], local_sem.at[1]),
-    ]
-    for copy in keep:
-        copy.start()
-    sent = []
 
     def chunk_copy(source, index, number, where):
         return pltpu.make_async_remote_copy(
@@ -177,19 +183,28 @@
             device_id_type=MESH,
         )
 
-    def send_chunk(source, index, where):
-        copy = chunk_copy(source, index, len(sent), where)
-        copy.start()
-        sent.append(copy)
-
-    def take_chunk(index):
-        chunk_copy(chunk_ref, index, 0, (place, 1 - part)).wait_recv()
-
-    def layer(turn):
-        return lax.rem(depth + turn, PLANES)
-
-    for turn in (2, 3, 1):
-        send_chunk(chunk_ref, own, (layer(turn) * plane + inside, part))
+    def chain(hop, way):
+        origin = depth - way * hop
+        index = 2 * (origin * plane + inside) + part
+        target = ((depth + way) * plane + inside, part)
+        source = chunk_ref if hop == 0 else rows_of(index)
+        number = 2 * hop + (0 if way > 0 else 1)
+        inner = (origin >= 0) & (origin < PLANES)
+        ahead = (depth + way >= 0) & (depth + way < PLANES)
+        return chunk_copy(source, index, number, target), inner, ahead
+
+    keep = [
+        pltpu.make_async_copy(chunk_ref, rows_of(own), local_sem.at[0]),
+        pltpu.make_async_copy(rows_ref.at[place, part], got_ref.at[place], local_sem.at[1]),
+    ]
+    for way in (1, -1):
+        copy, _, ahead = chain(0, way)
+
+        @pl.when(ahead)
+        def _():
+            copy.start()
+
+    weights = ((wq_ref, wq_out), (wk_ref, wk_out), (wv_ref, wv_out))
 
     def weight_copy(ref, out, number, slot, where):
         return pltpu.make_async_remote_copy(
@@ -202,18 +217,20 @@
         )
 
     direct = [
-        weight_copy(wq_ref, wq_out, 0, core, (place, 1 - part)),
-        weight_copy(wo_ref, wo_out, 1, core, (place, 1 - part)),
+        weight_copy(ref, out, number, core, over) for number, (ref, out) in enumerate(weights)
     ]
+    for slot in range(2):
+        direct.append(weight_copy(bias_ref, bias_out, 6 + slot, slot, over))
     for copy in direct:
         copy.start()
 
     rows_sent = []
-    for turn in (2, 3, 1, 0):
+
+    def send_rows(hop):
         for step in range(plane):
-            if turn == 0 and step == 0:
+            if hop == 0 and step == 0:
                 continue
-            target = layer(turn) * plane + lax.rem(inside + step, plane)
+            target = layer(hop) * plane + lax.rem(inside + step, plane)
             copy = pltpu.make_async_remote_copy(
                 src_ref=rows_ref.at[target, part],
                 dst_ref=got_ref.at[place],
@@ -225,41 +242,72 @@
             copy.start()
             rows_sent.append((copy, target))
 
-    bits = [2**b for b in range(plane.bit_length() - 1)]
-    bits = list(range(len(bits)))[::-1]
+    send_rows(0)
+    for copy in keep:
+        copy.start()
+    for hop in range(1, PLANES):
+        for way in (1, -1):
+            copy, inner, ahead = chain(hop, way)
+
+            @pl.when(inner)
+            def _():
+                copy.wait_recv()
+
+            if hop < PLANES - 1:
+
+                @pl.when(inner & ahead)
+                def _():
+                    copy.start()
+
+    for hop in (2, 3, 1):
+        send_rows(hop)
+
+    sent = []
+
+    def send_chunk(source, index, where):
+        copy = chunk_copy(source, index, 2 * PLANES + len(sent), where)
+        copy.start()
+        sent.append(copy)
+
+    def take_chunk(index):
+        chunk_copy(chunk_ref, index, 0, over).wait_recv()
+
+    bits = list(range(plane.bit_length() - 1))[::-1]
     orders = [["tensor"] + bits, bits[:-1] + ["tensor"] + bits[-1:]]
     relayed = []
     for stage in range(len(bits) + 1):
-        for turn in (0, 1, 2, 3):
-            order = orders[turn % 2]
-            origin = layer(turn) * plane + inside
+        for hop in range(PLANES):
+            order = orders[hop % 2]
+            origin = layer(hop) * plane + inside
             where = flip(place, part, [order[stage]])
             for chosen in subsets(order[:stage]):
                 at, side = flip(origin, part, chosen)
                 index = 2 * at + side
-                if turn == 0 and not chosen:
+                if hop == 0 and not chosen:
                     send_chunk(chunk_ref, index, where)
                     continue
-                if stage == 0 or order[stage - 1] in chosen:
+                if stage > 0 and order[stage - 1] in chosen:
                     take_chunk(index)
                 send_chunk(rows_of(index), index, where)
         if stage == 0:
             partner = (xor_bit(place, 0), part)
-            for number, (ref, out) in enumerate(((wq_ref, wq_out), (wo_ref, wo_out))):
+            for number, (ref, out) in enumerate(weights):
                 direct[number].wait_recv()
-                copy = weight_copy(out, out, 2 + number, core, partner)
+                copy = weight_copy(out, out, 3 + number, core, partner)
                 copy.start()
                 relayed.append(copy)
-    for turn in (0, 1, 2, 3):
-        order = orders[turn % 2]
-        origin = layer(turn) * plane + inside
+    for hop in range(PLANES):
+        order = orders[hop % 2]
+        origin = layer(hop) * plane + inside
         for chosen in subsets(order):
             if order[-1] in chosen:
                 at, side = flip(origin, part, chosen)
                 take_chunk(2 * at + side)
-    for number, (ref, out) in enumerate(((wq_ref, wq_out), (wo_ref, wo_out))):
-        weight_copy(out, out, 2 + number, 1 - core, (place, 1 - part)).wait_recv()
-    for copy, source in rows_sent:
+    for number, (ref, out) in enumerate(weights):
+        weight_copy(out, out, 3 + number, 1 - core, over).wait_recv()
+    for copy in direct[len(weights) :]:
+        copy.wait_recv()
+    for _, source in rows_sent:
         pltpu.make_async_remote_copy(
             src_ref=rows_ref.at[source, part],
             dst_ref=got_ref.at[source],
@@ -270,39 +318,46 @@
         ).wait_recv()
     for copy, _ in rows_sent:
         copy.wait_send()
+    for hop in range(PLANES - 1):
+        for way in (1, -1):
+            copy, inner, ahead = chain(hop, way)
+
+            @pl.when(inner & ahead)
+            def _():
+                copy.wait_send()
+
     for copy in sent + direct + relayed:
         copy.wait_send()
     for copy in keep:
         copy.wait()
 
 
-def front(rows, chunk, wq, wo, devices):
+def front(rows, chunk, wq, wk, wv, bias, devices):
     _, _, piece, width = rows.shape
     anywhere = pl.BlockSpec(memory_space=pl.ANY)
     outs = [
         jax.ShapeDtypeStruct((devices, piece, width), BF16),
         jax.ShapeDtypeStruct((2 * devices * chunk.shape[0],) + chunk.shape[1:], BF16),
-        jax.ShapeDtypeStruct(wq.shape, BF16),
-        jax.ShapeDtypeStruct(wo.shape, BF16),
-    ]
+    ] + [jax.ShapeDtypeStruct(a.shape, BF16) for a in (wq, wk, wv, bias)]
+    dma = pltpu.SemaphoreType.DMA
     return pl.pallas_call(
         functools.partial(front_kernel, devices),
-        in_specs=[anywhere] * 4,
-        out_specs=[anywhere] * 4,
+        in_specs=[anywhere] * 6,
+        out_specs=[anywhere] * 6,
         out_shape=outs,
         scratch_shapes=[
-            pltpu.SemaphoreType.DMA((2,)),
-            pltpu.SemaphoreType.DMA((devices,)),
-            pltpu.SemaphoreType.DMA((devices,)),
-            pltpu.SemaphoreType.DMA((2 * devices,)),
-            pltpu.SemaphoreType.DMA((2 * devices,)),
-            pltpu.SemaphoreType.DMA((4,)),
-            pltpu.SemaphoreType.DMA((4,)),
+            dma((2,)),
+            dma((devices,)),
+            dma((devices,)),
+            dma((2 * PLANES + 2 * devices,)),
+            dma((2 * devices,)),
+            dma((8,)),
+            dma((8,)),
         ],
         compiler_params=pltpu.CompilerParams(collective_id=0, has_side_effects=True),
         cost_estimate=cost(0, 100e6),
         name="front",
-    )(rows, chunk, wq, wo)
+    )(rows, chunk, wq, wk, wv, bias)
 
 
 def in_order(part, mine, theirs, place):
@@ -316,11 +371,26 @@
 
 
 def project_kernel(
-    part_ref, x_ref, meta_ref, turns_ref, sines_ref, gain_ref, mine_ref, theirs_ref, flat_ref,
-    n_ref, q_ref, kv_ref, z_ref, cos_ref, sin_ref, w_ref, bias,
+    x_ref, meta_ref, turns_ref, sines_ref, gain_ref, mq_ref, mk_ref, mv_ref, mb_ref,
+    tq_ref, tk_ref, tv_ref, tb_ref, flat_ref,
+    n_ref, q_ref, kv_ref, z_ref, cos_ref, sin_ref, w_ref, other_ref, bias, held, ksend, krecv,
 ):
+    place, part = lax.axis_index("dp"), lax.axis_index("tensor")
+    here = pl.program_id(0)
+    tiles = held.shape[0]
     width = x_ref.shape[1]
     qw, kw = q_ref.shape[1], kv_ref.shape[1] // 2
+
+    def swap(number):
+        return pltpu.make_async_remote_copy(
+            src_ref=held.at[number],
+            dst_ref=other_ref.at[number],
+            send_sem=ksend.at[number],
+            recv_sem=krecv.at[number],
+            device_id=(place, 1 - part),
+            device_id_type=MESH,
+        )
+
     rank = flat_ref.shape[1]
     low = qw + 2 * kw
     a_rows, b_rows = [], []
@@ -334,47 +404,76 @@
     def _():
         def fill(first, second):
             at, to = 0, 0
-            for size in (qw // 2, kw // 2, kw // 2):
-                cut = slice(at, at + size)
-                both = jnp.concatenate(
-                    [first[:width, cut].astype(F32), second[:width, cut].astype(F32)], axis=1
-                )
-                w_ref[:, to : to + 2 * size] = both.astype(BF16)
-                extra = jnp.concatenate(
-                    [first[width : width + 8, cut].astype(F32), second[width : width + 8, cut].astype(F32)],
+            for order, size in enumerate((qw // 2, kw // 2, kw // 2)):
+                w_ref[to : to + size, :] = first[order][...]
+                w_ref[to + size : to + 2 * size, :] = second[order][...]
+                bias[:, to : to + 2 * size] = jnp.concatenate(
+                    [
+                        first[3][:8, at : at + size].astype(F32),
+                        second[3][:8, at : at + size].astype(F32),
+                    ],
                     axis=1,
                 )
-                bias[:, to : to + 2 * size] = extra
                 at += size
                 to += 2 * size
 
-        in_order(part_ref[0], mine_ref, theirs_ref, fill)
+        barrier = pltpu.get_barrier_semaphore()
+        pl.semaphore_signal(barrier, inc=1, device_id=(place, 1 - part), device_id_type=MESH)
+        in_order(
+            part, (mq_ref, mk_ref, mv_ref, mb_ref), (tq_ref, tk_ref, tv_ref, tb_ref), fill
+        )
         for i, rows in enumerate(a_rows):
-            w_ref[:, low + i * rank : low + (i + 1) * rank] = flat_ref[rows, :]
+            turned = jnp.transpose(flat_ref[rows, :].astype(F32)).astype(BF16)
+            w_ref[low + i * rank : low + (i + 1) * rank, :] = turned
+        pl.semaphore_wait(barrier, 1)
 
     values = x_ref[...].astype(F32)
     normed = (values * rms(values) * gain_ref[...]).astype(BF16)
     n_ref[...] = normed
-    base = nn(normed, w_ref[...])
+    base = nt(normed, w_ref[qw:, :])
     mask = rank_mask(meta_ref[:, 0:1], rank)
-    lows = [(base[:, low + i * rank : low + (i + 1) * rank] * mask).astype(BF16) for i in range(3)]
+    lows = [
+        (base[:, low - qw + i * rank : low - qw + (i + 1) * rank] * mask).astype(BF16)
+        for i in range(3)
+    ]
     for i in range(3):
         z_ref[:, i * rank : (i + 1) * rank] = lows[i]
     cos, sin = lane_table(turns_ref[...]), lane_table(sines_ref[...])
     cos_ref[...] = cos
     sin_ref[...] = sin
-    queries = base[:, :qw] + bias[0:1, :qw] + ADAPTER_SCALE * nt(lows[0], flat_ref[b_rows[0], :])
+    keys = (
+        base[:, :kw]
+        + bias[0:1, qw : qw + kw]
+        + ADAPTER_SCALE * nt(lows[1], flat_ref[b_rows[1], :])
+    )
+    vals = (
+        base[:, kw : 2 * kw]
+        + bias[0:1, qw + kw : low]
+        + ADAPTER_SCALE * nt(lows[2], flat_ref[b_rows[2], :])
+    )
+    both = jnp.concatenate([keys * cos + turn(keys) * sin, vals], axis=1).astype(BF16)
+    held[here] = both
+    kv_ref[...] = both
+    swap(here).start()
+    queries = (
+        nt(normed, w_ref[:qw, :])
+        + bias[0:1, :qw]
+        + ADAPTER_SCALE * nt(lows[0], flat_ref[b_rows[0], :])
+    )
     for pair in range(qw // LANES):
-        part = queries[:, pair * LANES : (pair + 1) * LANES]
-        turned = (part * cos + turn(part) * sin) * HEAD**-0.5
+        some = queries[:, pair * LANES : (pair + 1) * LANES]
+        turned = (some * cos + turn(some) * sin) * HEAD**-0.5
         q_ref[:, pair * LANES : (pair + 1) * LANES] = turned.astype(BF16)
-    keys = base[:, qw : qw + kw] + bias[0:1, qw : qw + kw] + ADAPTER_SCALE * nt(lows[1], flat_ref[b_rows[1], :])
-    kv_ref[:, :kw] = (keys * cos + turn(keys) * sin).astype(BF16)
-    vals = base[:, qw + kw : low] + bias[0:1, qw + kw : low] + ADAPTER_SCALE * nt(lows[2], flat_ref[b_rows[2], :])
-    kv_ref[:, kw:] = vals.astype(BF16)
-
-
-def project(part, x, meta, turns, sines, gain, mine, theirs, flat, qw, kw):
+
+    @pl.when(here == tiles - 1)
+    def _():
+        for number in range(tiles):
+            swap(number).wait_send()
+        for number in range(tiles):
+            swap(number).wait_recv()
+
+
+def project(x, meta, turns, sines, gain, mine, theirs, flat, qw, kw):
     rows, width = x.shape
     rank = flat.shape[1]
     tile = ROW_TILE
@@ -387,25 +486,30 @@
         jax.ShapeDtypeStruct((rows, 3 * rank), BF16),
         jax.ShapeDtypeStruct((rows, LANES), F32),
         jax.ShapeDtypeStruct((rows, LANES), F32),
-        jax.ShapeDtypeStruct((width, qw + 2 * kw + 3 * rank), BF16),
+        jax.ShapeDtypeStruct((qw + 2 * kw + 3 * rank, width), BF16),
+        jax.ShapeDtypeStruct((rows // tile, tile, 2 * kw), BF16),
     ]
+    dma = pltpu.SemaphoreType.DMA
     return pl.pallas_call(
         project_kernel,
-        grid_spec=pltpu.PrefetchScalarGridSpec(
-            num_scalar_prefetch=1,
-            grid=(rows // tile,),
-            in_specs=[row_blocks(a, tile) for a in (x, meta)]
-            + [columns, columns]
-            + [whole(a) for a in (gain, mine, theirs)]
-            + [rows_from(flat, 0, early)],
-            out_specs=[row_blocks(o, tile) for o in outs[:6]] + [whole(outs[6])],
-            scratch_shapes=[pltpu.VMEM((8, qw + 2 * kw), F32)],
-        ),
+        grid=(rows // tile,),
+        in_specs=[row_blocks(a, tile) for a in (x, meta)]
+        + [columns, columns]
+        + [whole(a) for a in (gain, *mine, *theirs)]
+        + [pl.BlockSpec((early, rank), lambda i: (0, 0))],
+        out_specs=[row_blocks(o, tile) for o in outs[:6]]
+        + [whole(outs[6]), pl.BlockSpec(memory_space=pl.ANY)],
         out_shape=outs,
-        compiler_params=params(),
+        scratch_shapes=[
+            pltpu.VMEM((8, qw + 2 * kw), F32),
+            pltpu.VMEM((rows // tile, tile, 2 * kw), BF16),
+            dma((rows // tile,)),
+            dma((rows // tile,)),
+        ],
+        compiler_params=params(collective_id=4, has_side_effects=True),
         cost_estimate=cost(2 * rows * width * 1600, 9e6),
         name="project",
-    )(part, x, meta, turns, sines, gain, mine, theirs, flat)
+    )(x, meta, turns, sines, gain, *mine, *theirs, flat)
 
 
 def head_groups(heads, kv_heads):
@@ -450,7 +554,7 @@
         both = jnp.concatenate([own_ref[...], other_ref[...]], axis=0)
         for start in range(0, keys.shape[1], KEY_TILE):
             span = slice(start, start + KEY_TILE)
-            part = nn(pick_rows(column_ref[span, :], both.shape[0]), both)
+            part = nn(pick_rows(column_ref[span, 0:1], both.shape[0]), both)
             merged_ref[span, :] = part.astype(BF16)
             for number, (kv, half, _) in enumerate(groups):
                 keys[number, span, :] = spread_heads(part[:, :LANES], kv, half).astype(BF16)
@@ -647,7 +751,7 @@
         both = jnp.concatenate([join(dkeys), join(dvalues)], axis=1)
         half_rows = own_ref.shape[0]
         for at in range(0, total, KEY_TILE):
-            hit = (at + row_iota((KEY_TILE, total))) == column_ref[...]
+            hit = (at + row_iota((KEY_TILE, total))) == column_ref[0:1, :]
             part = nn(jnp.where(hit, 1.0, 0.0).astype(BF16), both).astype(BF16)
             if at < half_rows:
                 own_ref[at : at + KEY_TILE, :] = part
@@ -869,17 +973,17 @@
             copy.wait()
         for copy in remote:
             copy.wait_recv()
-        later = plan.boxes(1)
-
         def total(zz, at, side):
             index = (zz - 1) * boxes + plan.box(0, at, side)
             return mine[index].astype(F32) + inbox[index].astype(F32)
 
         for zz in range(1, PLANES):
-            for at, side in plan.leaving(1, inside, part):
-                on_ref[(zz - 1) * later + plan.box(1, at, side)] = total(zz, at, side).astype(BF16)
-            for at, side in plan.staying(1, inside, part):
-                kept_ref[(zz - 1) * later + plan.box(1, at, side)] = total(zz, at, side)
+            for peer, chosen in enumerate(subsets(plan.axes[1:])):
+                at, side = flip(inside, part, chosen)
+                if peer == 0:
+                    kept_ref[zz - 1] = total(zz, at, side)
+                else:
+                    on_ref[peer - 1, zz - 1] = total(zz, at, side).astype(BF16)
         for copy in remote:
             copy.wait_send()
 
@@ -892,13 +996,13 @@
     qw = o.shape[1]
     tile = ROW_TILE
     plan = Windows(devices, own_rows)
-    first, second = (PLANES - 1) * plan.boxes(0), (PLANES - 1) * plan.boxes(1)
+    first = (PLANES - 1) * plan.boxes(0)
     outs = [
         jax.ShapeDtypeStruct((rows, width), F32),
         jax.ShapeDtypeStruct((rows, qw), BF16),
         jax.ShapeDtypeStruct((qw + width, rank), BF16),
-        jax.ShapeDtypeStruct((second, plan.rows, rank), BF16),
-        jax.ShapeDtypeStruct((second, plan.rows, rank), F32),
+        jax.ShapeDtypeStruct((plan.boxes(0) - 1, PLANES - 1, plan.rows, rank), BF16),
+        jax.ShapeDtypeStruct((PLANES - 1, plan.rows, rank), F32),
     ]
     return pl.pallas_call(
         functools.partial(middle_back_kernel, plan, start),
@@ -1227,10 +1331,13 @@
 
 def tail_kernel(plan, early, key_width, direct, *refs):
     sources = refs[:9]
-    other_ref, w_hbm, b_ref, gain_ref, flat_ref, out_grad_ref, kept_hbm, gots_hbm = refs[9:17]
-    out_ref, sum_ref = refs[17:19]
-    held = refs[19:28]
-    w, grads, dxs, acc_a, acc_b, outbox, last_in, got_s, kept, gots, *rest = refs[28:]
+    other_ref, w_hbm, b_ref, gain_ref, flat_ref, out_grad_ref, kept_hbm = refs[9:16]
+    peers = plan.boxes(0) - 1
+    gots_hbm = refs[16 : 16 + peers]
+    refs = refs[16 + peers :]
+    out_ref, sum_ref = refs[:2]
+    held = refs[2:11]
+    w, grads, dxs, acc_a, acc_b, outbox, last_in, got_s, kept, gots, *rest = refs[11:]
     inboxes = rest[:-13]
     (
         load_sem, grad_sem, dsend, drecv, fsend, frecv, rsend, rrecv, zrecv, keep_sem, ksend, krecv,
@@ -1266,7 +1373,9 @@
 
     sums_loads = [
         pltpu.make_async_copy(kept_hbm, kept, grad_sem.at[3]),
-        pltpu.make_async_copy(gots_hbm, gots, grad_sem.at[4]),
+    ] + [
+        pltpu.make_async_copy(got, gots.at[peer], grad_sem.at[4 + peer])
+        for peer, got in enumerate(gots_hbm)
     ]
     w_load = pltpu.make_async_copy(w_hbm, w, grad_sem.at[0])
     middle = out_grad_ref.shape[0]
@@ -1312,26 +1421,22 @@
     cursor = 0
     for stage in range(count):
         bases.append(cursor)
-        cursor += plan.boxes(stage) * (1 if stage < 2 else PLANES)
-
-    def box_of(stage, zz, at, side):
-        return plan.box(stage, at, side) + (0 if stage < 2 else zz * plan.boxes(stage))
+        cursor += plan.boxes(stage)
 
     def window_sum(stages, zz, at, side):
-        if zz == 0:
-            total = grads[plan.span(0, at, side), :].astype(F32)
-            for stage in range(min(2, stages)):
-                total = total + inboxes[stage][box_of(stage, 0, at, side)].astype(F32)
-        else:
-            index = (zz - 1) * plan.boxes(1) + plan.box(1, at, side)
-            total = kept[index] + gots[index].astype(F32)
-        for stage in range(2, stages):
-            total = total + inboxes[stage][box_of(stage, zz, at, side)].astype(F32)
+        if zz:
+            total = kept[zz - 1]
+            for peer in range(peers):
+                total = total + gots[peer, zz - 1].astype(F32)
+            return total
+        total = grads[plan.span(0, at, side), :].astype(F32)
+        for stage in range(stages):
+            total = total + inboxes[stage][plan.box(stage, at, side)].astype(F32)
         return total
 
     def take(stages, zz, at, side):
-        for stage in range(0 if zz == 0 else 2, stages):
-            index = box_of(stage, zz, at, side)
+        for stage in range(0 if zz else stages):
+            index = plan.box(stage, at, side)
             pltpu.make_async_remote_copy(
                 src_ref=inboxes[stage].at[index],
                 dst_ref=inboxes[stage].at[index],
@@ -1344,10 +1449,10 @@
     sent = []
     posted = [0]
 
-    def pass_on(stage, zz, source_of):
+    def pass_on(stage, source_of):
         partner = flip(place, part, [axes[stage]])
         for at, side in plan.leaving(stage, inside, part):
-            index = box_of(stage, zz, at, side)
+            index = plan.box(stage, at, side)
             copy = pltpu.make_async_remote_copy(
                 src_ref=source_of(at, side),
                 dst_ref=inboxes[stage].at[index],
@@ -1365,17 +1470,66 @@
         outbox[slot] = total.astype(BF16)
         return outbox.at[slot]
 
-    def stage_sends(stage, zz):
+    def stage_sends(stage):
         def source_of(at, side):
-            take(stage, zz, at, side)
-            return post(window_sum(stage, zz, at, side))
-
-        pass_on(stage, zz, source_of)
+            take(stage, 0, at, side)
+            return post(window_sum(stage, 0, at, side))
+
+        pass_on(stage, source_of)
+
+    zfirst = sum(plan.boxes(stage) for stage in range(count))
+    zsends = []
+
+    def plane_copy(slot, box, recv, number, zz):
+        return pltpu.make_async_remote_copy(
+            src_ref=outbox.at[slot],
+            dst_ref=last_in.at[box],
+            send_sem=rsend.at[zfirst + number],
+            recv_sem=zrecv.at[recv],
+            device_id=(zz * plane + inside, part),
+            device_id_type=MESH,
+        )
+
+    def near(zz):
+        slot = posted[0]
+        posted[0] += 1
+        copy = plane_copy(slot, zz, zz, zz, xor_bit(depth, 0))
+        moving = lax.rem(depth, 2) != zz % 2
+        zsends.append((moving, copy))
+        take(count, zz, inside, part)
+
+        @pl.when(moving)
+        def _():
+            outbox[slot] = window_sum(count, zz, inside, part).astype(BF16)
+            copy.start()
+
+        return copy
+
+    def far(zz, came):
+        slot = posted[0]
+        posted[0] += 1
+        copy = plane_copy(slot, PLANES, PLANES, PLANES + zz, zz)
+        staying = lax.rem(depth, 2) == zz % 2
+        moving = staying & (depth != zz)
+        zsends.append((moving, copy))
+
+        @pl.when(staying)
+        def _():
+            came.wait_recv()
+            total = window_sum(count, zz, inside, part) + last_in[zz].astype(F32)
+
+            @pl.when(depth == zz)
+            def _():
+                sum_ref[...] = total
+
+            @pl.when(depth != zz)
+            def _():
+                outbox[slot] = total.astype(BF16)
+                copy.start()
 
     for copy in sums_loads:
         copy.wait()
-    for zz in range(1, PLANES):
-        stage_sends(2, zz)
+    came = [near(zz) for zz in range(1, PLANES)]
 
     def step_at(step):
         return lax.rem(inside + step, plane)
@@ -1414,7 +1568,7 @@
         backs = [
             (ADAPTER_SCALE * nn(g, b) * mask).astype(BF16) for g, b in zip((gq, gk, gv), b_parts)
         ]
-        dn = nt(jnp.concatenate([gq, gk, gv] + backs, axis=1), w[...])
+        dn = nn(jnp.concatenate([gq, gk, gv] + backs, axis=1), w[...])
         values = x_s[number].astype(F32)
         dx = (dy1_s[number] + norm_back(values, gain_ref[...], dn)).astype(BF16)
         acc_a[...] += tn(n_s[number], jnp.concatenate(backs, axis=1))
@@ -1462,7 +1616,7 @@
             ADAPTER_SCALE * acc_b[base : base + size, :]
         ).astype(BF16)
         at += width + size
-    pass_on(0, 0, lambda at, side: grads.at[plan.span(0, at, side), :])
+    pass_on(0, lambda at, side: grads.at[plan.span(0, at, side), :])
 
     forwards = []
 
@@ -1498,60 +1652,20 @@
             device_id_type=MESH,
         )
 
-    zsends = []
-
-    def across_planes(zz):
-        take(count, zz, inside, part)
-        total = window_sum(count, zz, inside, part)
-        slot = posted[0]
-        posted[0] += 1
-        number = len(sent) + len(zsends)
-        copy = pltpu.make_async_remote_copy(
-            src_ref=outbox.at[slot],
-            dst_ref=last_in.at[depth],
-            send_sem=rsend.at[number],
-            recv_sem=zrecv.at[depth],
-            device_id=(zz * plane + inside, part),
-            device_id_type=MESH,
-        )
-        zsends.append((zz, copy))
-
-        @pl.when(depth != zz)
-        def _():
-            outbox[slot] = total.astype(BF16)
-            copy.start()
-
-        @pl.when(depth == zz)
-        def _():
-            sum_ref[...] = total
-
+    for zz in range(1, PLANES):
+        far(zz, came[zz - 1])
+    for stage in range(1, count):
+        stage_sends(stage)
+        if direct and stage <= 2:
+            forward((0, 0, 3)[stage])
+    late = near(0)
     if direct:
-        forward(0)
-    for stage in range(3, count):
-        for zz in (1, 2, 3):
-            stage_sends(stage, zz)
-    for zz in (1, 2, 3):
-        across_planes(zz)
-    stage_sends(1, 0)
-    if direct:
-        forward(3)
         forward(1)
-    for stage in range(2, count):
-        stage_sends(stage, 0)
-    across_planes(0)
+    far(0, late)
     if direct:
         forward(2)
-    for hop in (1, 2, 3):
-        source = layer(hop)
-        pltpu.make_async_remote_copy(
-            src_ref=last_in.at[source],
-            dst_ref=last_in.at[source],
-            send_sem=hsem.at[0],
-            recv_sem=zrecv.at[source],
-            device_id=over,
-            device_id_type=MESH,
-        ).wait_recv()
-        sum_ref[...] += last_in[source].astype(F32)
+    plane_copy(0, PLANES, PLANES, 0, depth).wait_recv()
+    sum_ref[...] += last_in[PLANES].astype(F32)
 
     if direct:
         for back in range(PLANES):
@@ -1565,9 +1679,9 @@
                 piece_copy(number, step, over, out_ref.at[place, part]).wait_send()
     for copy in sent:
         copy.wait_send()
-    for zz, copy in zsends:
-
-        @pl.when(depth != zz)
+    for moving, copy in zsends:
+
+        @pl.when(moving)
         def _():
             copy.wait_send()
 
@@ -1587,8 +1701,9 @@
     tile = rows // PLANES
     direct = piece % 16 == 0
     anywhere = pl.BlockSpec(memory_space=pl.ANY)
-    boxes = [plan.boxes(stage) * (1 if stage < 2 else PLANES) for stage in range(count)]
-    sends = sum(boxes) + PLANES
+    boxes = [plan.boxes(stage) for stage in range(count)]
+    peers = boxes[0] - 1
+    sends = sum(boxes) + 2 * PLANES
     qw = gq.shape[1]
     first_plane = 16 * (((2 * plane - 1) * own_rows) // 16) + window
     dma = pltpu.SemaphoreType.DMA
@@ -1608,22 +1723,22 @@
         pltpu.VMEM((width, 3 * rank), F32),
         pltpu.VMEM((qw + 2 * key_width, rank), F32),
         pltpu.VMEM((sends, window, rank), BF16),
-        pltpu.VMEM((PLANES, window, rank), BF16),
+        pltpu.VMEM((PLANES + 1, window, rank), BF16),
         pltpu.VMEM((PLANES, tile, other.shape[1]), BF16),
         pltpu.VMEM(kept.shape, F32),
-        pltpu.VMEM(gots.shape, BF16),
+        pltpu.VMEM((peers,) + gots[0].shape, BF16),
     ]
     scratch += [pltpu.VMEM((size, window, rank), BF16) for size in boxes]
     scratch += [
         dma((PLANES, len(rows_in))),
-        dma((5,)),
+        dma((4 + peers,)),
         dma((PLANES, plane)),
         dma((devices,)),
         dma((PLANES,)),
         dma((PLANES,)),
         dma((sends,)),
         dma((sum(boxes),)),
-        dma((PLANES,)),
+        dma((PLANES + 1,)),
         dma((1,)),
         dma((PLANES,)),
         dma((PLANES,)),
@@ -1634,60 +1749,143 @@
         grid=(1,),
         in_specs=[anywhere] * 11
         + [pl.BlockSpec((early, rank), lambda i: (0, 0)), whole(gain)]
-        + [anywhere] * 4,
+        + [anywhere] * (3 + peers),
         out_specs=[anywhere, whole(outs[1])],
         out_shape=outs,
         scratch_shapes=scratch,
         compiler_params=params(collective_id=2, has_side_effects=True),
         cost_estimate=cost(2 * rows * width * 2900, 200e6),
         name="tail",
-    )(*rows_in, other, w_cat, b_rows, gain, flat, grad_out, kept, gots)
-
-
-def row_tables(order_row, lengths_row, adapter_row, part, parts, each):
-    total = order_row.shape[0]
+    )(*rows_in, other, w_cat, b_rows, gain, flat, grad_out, kept, *gots)
+
+
+def whole_part(values, size):
+    return jnp.floor((values + 0.5) * (1.0 / size))
+
+
+def tables_kernel(
+    parts, each, part_ref, lengths_ref, ids_ref, order_ref, freq_ref,
+    turns_ref, sines_ref, own_ref, other_ref, sorted_ref, rows_ref, column_ref, column_row_ref,
+    bounds_ref,
+):
+    total = order_ref.shape[1]
+    local = total // parts
     piece = each // parts
+    block = 256
+    order = jnp.broadcast_to(order_ref[0:1, :].astype(F32), (8, total))
+    group = whole_part(order, each)
+    rest = order - group * each
+    part_at = whole_part(rest, piece)
+    own = part_at == part_ref[0].astype(F32)
+    slot = group * piece + (rest - part_at * piece)
+    column = jnp.where(own, slot, slot + local)
+    lanes = lane_iota((8, total))
+    upto = jnp.where(own, 1.0, 0.0)
+    shift = 1
+    while shift < total:
+        upto = upto + jnp.where(lanes >= shift, pltpu.roll(upto, shift, 1), 0.0)
+        shift *= 2
+    rank = jnp.where(own, upto - 1.0, 2.0 * total)
+    place = lanes.astype(F32)
+    number = row_iota((8, total))
+    column_row_ref[...] = column.astype(I32)
+    turned = jnp.transpose(jnp.where(number == 0, column, rank))
+    column_ref[...] = turned.astype(I32)
+
+    def halves(values):
+        high = whole_part(values, 256)
+        return high, values - high * 256
+
+    place_high, place_low = halves(place)
+    slot_high, slot_low = halves(slot)
+    left = jnp.where(
+        number == 0, place_high, jnp.where(number == 1, place_low, jnp.where(number == 2, slot_high, slot_low))
+    ).astype(BF16)
+
+    def chosen_by(keys, start):
+        hit = keys == (start + lane_iota((total, block))).astype(F32)
+        found = nn(left, jnp.where(hit, 1.0, 0.0).astype(BF16))
+        return found[0:1] * 256 + found[1:2], found[2:3] * 256 + found[3:4]
+
+    def sequence(places):
+        first = jnp.zeros_like(places)
+        adapter = jnp.zeros_like(places) + ids_ref[0].astype(F32)
+        start = lengths_ref[0].astype(F32)
+        for at in range(1, lengths_ref.shape[0]):
+            inside = places >= start
+            first = jnp.where(inside, start, first)
+            adapter = jnp.where(inside, ids_ref[at].astype(F32), adapter)
+            start = start + lengths_ref[at].astype(F32)
+        return first, adapter
+
+    def rope(position, at):
+        angles = jnp.broadcast_to(position, freq_ref.shape[:1] + position.shape[1:]) * freq_ref[:, 0:1]
+        turns_ref[:, at : at + block] = jnp.cos(angles)
+        sines_ref[:, at : at + block] = jnp.sin(angles)
+
+    def as_columns(*rows):
+        index = row_iota((8, block))
+        out = jnp.zeros((8, block), F32)
+        for at, row in enumerate(rows):
+            out = jnp.where(index == at, jnp.broadcast_to(row, (8, block)), out)
+        return out
+
+    for start in range(0, total, block):
+        places, _ = chosen_by(turned[:, 0:1], start)
+        first, adapter = sequence(places)
+        columns = jnp.transpose(as_columns(adapter)).astype(I32)
+        if start < local:
+            rope(places - first, start)
+            own_ref[start : start + block, :] = columns
+        else:
+            other_ref[start - local : start - local + block, :] = columns
+    for start in range(0, local, block):
+        places, slots = chosen_by(turned[:, 1:2], start)
+        first, _ = sequence(places)
+        rope(places - first, local + start)
+        rows = as_columns(slots, first, places)
+        rows_ref[:, start : start + block] = rows.astype(I32)
+        sorted_ref[start : start + block, :] = jnp.transpose(rows).astype(I32)
+        at_lane = lane_iota((1, block))
+        for tile in range(0, block, QUERY_TILE):
+            low = jnp.max(jnp.where(at_lane == tile, first, 0.0))
+            high = jnp.max(jnp.where(at_lane == tile + QUERY_TILE - 1, places, 0.0))
+            number_at = (start + tile) // QUERY_TILE
+            bounds_ref[0, number_at] = low.astype(I32) // KEY_TILE
+            bounds_ref[1, number_at] = high.astype(I32) // KEY_TILE + 1
+
+
+def row_tables(order, lengths, adapter_ids, part, parts, each):
+    total = order.shape[1]
     local = total // parts
-    places = jnp.arange(total, dtype=I32)
-    own = (order_row % each) // piece == part
-    slot = (order_row // each) * piece + order_row % piece
-    column = jnp.where(own, slot, local + slot)
-    upto = jnp.sum((own[None, :] & (places[None, :] <= places[:, None])).astype(I32), axis=1)
-    rank = jnp.where(own, upto - 1, total)
-    picks = rank[None, :] == jnp.arange(local, dtype=I32)[:, None]
-    sorted_place = jnp.sum(jnp.where(picks, places[None, :], 0), axis=1)
-    sorted_slot = jnp.sum(jnp.where(picks, slot[None, :], 0), axis=1)
-    slot_place = jnp.sum(jnp.where(column[None, :] == places[:, None], places[None, :], 0), axis=1)
-    ends = jnp.cumsum(lengths_row)
-    starts = ends - lengths_row
-    both = jnp.concatenate([slot_place, sorted_place])
-    member = (both[:, None] >= starts[None, :]) & (both[:, None] < ends[None, :])
-    first = jnp.sum(jnp.where(member, starts[None, :], 0), axis=1)
-    chosen = jnp.sum(jnp.where(member, adapter_row[None, :], 0), axis=1)
-    position = both - first
-    sorted_first = first[total:]
-    bounds = jnp.stack(
-        [
-            sorted_first[::QUERY_TILE] // KEY_TILE,
-            sorted_place[QUERY_TILE - 1 :: QUERY_TILE] // KEY_TILE + 1,
-        ]
-    )
-    blank = jnp.zeros_like(sorted_place)
-    meta_sorted = jnp.stack([sorted_slot, sorted_first, sorted_place] + [blank] * 5, axis=1)
-    meta_rows = jnp.stack([sorted_slot, sorted_first, sorted_place] + [blank] * 5, axis=0)
-    meta_own = jnp.broadcast_to(chosen[:local, None], (local, 8))
-    meta_other = jnp.broadcast_to(chosen[local:total, None], (local, 8))
-    slot_position = position[:local]
-    return (
-        meta_own, meta_other, meta_sorted, meta_rows, slot_position, position[total:], column, bounds,
-    )
-
-
-def rope_tables(position):
     freq_index = jnp.arange(HEAD // 2, dtype=F32)
-    inv_freq = jnp.power(jnp.float32(ROPE_BASE), -2.0 * freq_index / HEAD)
-    angles = position.astype(F32)[None, :] * inv_freq[:, None]
-    return jnp.cos(angles), jnp.sin(angles)
+    freq = jnp.power(jnp.float32(ROPE_BASE), -2.0 * freq_index / HEAD)
+    freq = jnp.broadcast_to(freq[:, None], (HEAD // 2, LANES))
+    shapes = [
+        ((HEAD // 2, total), F32),
+        ((HEAD // 2, total), F32),
+        ((local, 8), I32),
+        ((local, 8), I32),
+        ((local, 8), I32),
+        ((8, local), I32),
+        ((total, 8), I32),
+        ((8, total), I32),
+        ((2, local // QUERY_TILE), I32),
+    ]
+    outs = [jax.ShapeDtypeStruct(shape, kind) for shape, kind in shapes]
+    return pl.pallas_call(
+        functools.partial(tables_kernel, parts, each),
+        grid_spec=pltpu.PrefetchScalarGridSpec(
+            num_scalar_prefetch=3,
+            grid=(1,),
+            in_specs=[whole(order), whole(freq)],
+            out_specs=[whole(o) for o in outs[:-1]] + [pl.BlockSpec(memory_space=pltpu.SMEM)],
+        ),
+        out_shape=outs,
+        compiler_params=params(),
+        cost_estimate=cost(1e8, 4e6),
+        name="tables",
+    )(jnp.reshape(part, (1,)).astype(I32), lengths[0], adapter_ids[0], order, freq)
 
 
 def per_device(
@@ -1725,24 +1923,16 @@
     qh, kh, half = w_query.shape[1], w_key.shape[1], w_gate.shape[1]
     qw, kw, hidden = parts * qh, parts * kh, parts * half
     heads, kv_heads = qw // HEAD, kw // HEAD
-    mine_qkv = jnp.concatenate(
-        [
-            jnp.concatenate([w_query, w_key, w_value], axis=1),
-            jnp.broadcast_to(
-                jnp.concatenate([b_query, b_key, b_value])[None], (32, qh + 2 * kh)
-            ),
-        ],
-        axis=0,
-    )
-    lines = mine_qkv.shape[0]
     unit = 4 if own_rows % 4 == 0 else 1
-    moved, copies, their_qkv, their_out = front(
+    bias = jnp.concatenate([b_query, b_key, b_value, jnp.zeros((width - qh - 2 * kh,), BF16)])
+    mine = (w_query.T, w_key.T, w_value.T, jnp.broadcast_to(bias[None], (16, width)))
+    moved, copies, *theirs = front(
         tokens.reshape(devices, parts, piece, width),
         adapters.astype(BF16).reshape(own_rows // unit, unit, rank),
-        mine_qkv.reshape(2, lines // 2, -1),
-        w_out.reshape(2, w_out.shape[0] // 2, width),
+        *[a.reshape(2, a.shape[0] // 2, width) for a in mine],
         devices,
     )
+    theirs = [a.reshape(b.shape) for a, b in zip(theirs, mine)]
     cotangent, moved = lax.optimization_barrier((cotangent, moved))
     moved = moved.reshape(local, width)
     dy_all = lax.all_to_all(
@@ -1757,24 +1947,24 @@
 
     early = 3 * width + qw + 2 * kw
     flat = copies.reshape(2 * devices * own_rows, rank)
-    meta_own, meta_other, meta_sorted, meta_rows, slot_position, sorted_position, column, bounds = (
-        row_tables(order[0], lengths[0], adapter_ids[0], part, parts, each)
-    )
-    turns, sines = rope_tables(jnp.concatenate([slot_position, sorted_position]))
+    (
+        turns, sines, meta_own, meta_other, meta_sorted, meta_rows, column, column_row, bounds,
+    ) = row_tables(order, lengths, adapter_ids, part, parts, each)
     gain_one = norm_gains[0:1].astype(F32)
     gain_two = norm_gains[1:2].astype(F32)
     side = jnp.reshape(part, (1,)).astype(I32)
 
-    n1, q, kv, z, cos, sin, w_cat = project(
-        side, moved, meta_own, turns, sines, gain_one, mine_qkv, their_qkv.reshape(mine_qkv.shape),
-        flat, qw, kw,
+    n1, q, kv, z, cos, sin, w_cat, other_kv = project(
+        moved, meta_own, turns, sines, gain_one, mine, theirs, flat, qw, kw
     )
-    other_kv = across(kv)
+    other_kv = other_kv.reshape(kv.shape)
+    w_out, kv = lax.optimization_barrier((w_out, kv))
+    their_out = across(w_out)
     q_sorted, o_sorted, logs, merged, o = attend(
-        bounds, q, meta_sorted, meta_rows, kv, other_kv, column[:, None], heads, kv_heads
+        bounds, q, meta_sorted, meta_rows, kv, other_kv, column, heads, kv_heads
     )
     y1, n2, z_out, w_out_cat = middle(
-        side, o, moved, meta_own, w_out, their_out.reshape(w_out.shape), gain_two, flat, early
+        side, o, moved, meta_own, w_out, their_out, gain_two, flat, early
     )
     y_own, d_own, y_got, d_got, y_last, flat_grads = feed(
         n2, dy, dy_theirs, meta_own, meta_other, w_gate, w_up, w_down, flat
@@ -1784,7 +1974,16 @@
         devices, own_rows, d_own, d_got.reshape(local, width), y1, dy, o, z_out, meta_own, flat,
         early + qw, w_out_cat, gain_two, flat_grads,
     )
-    got_sums = lax.ppermute(on_sums, "dp", [(i, i ^ 2) for i in range(devices)])
+    got_sums = []
+    for number, chosen in enumerate(subsets(Windows(devices, own_rows).axes[1:])):
+        if number:
+            moves = [
+                (2 * at + side, 2 * to + over)
+                for at in range(devices)
+                for side in range(parts)
+                for to, over in [flip_fixed(at, side, chosen)]
+            ]
+            got_sums.append(lax.ppermute(on_sums[number - 1], ("dp", "tensor"), moves))
     layer_rows = (y1 + (y_own + y_got.astype(F32))).astype(BF16).reshape(devices, 1, piece, width)
     layer_rows = jnp.broadcast_to(layer_rows, (devices, parts, piece, width))
     layer_rows, dar = lax.optimization_barrier((layer_rows, dar))
@@ -1794,7 +1993,7 @@
     ).reshape(total, width)
     gq, dkv_own, dkv_other = attend_back(
         bounds, q_sorted, dar, o_sorted, logs, meta_sorted, meta_rows, turns, sines,
-        merged, column[None, :], heads, kv_heads,
+        merged, column_row, heads, kv_heads,
     )
     dx, window = tail(
         devices, own_rows, early,

time: 401 us -> 383 us (0.955)
  other arithmetic: 16.9 us -> 6.31 us
  local copies, waits for them, and re-layouts: 24.4 us -> 14.1 us
  Pallas kernels: 332 us -> 341 us
  starting transfers between devices: 23.1 us -> 17.8 us
    pallas_call x1, Pallas kernels: 90 us -> 74.1 us  [tail(): pl.pallas_call(functools.partial(tail_kernel, plan, early, key_width, dir...]
    pallas_call x1 -> x2, Pallas kernels: 10.1 us -> 21.9 us  [the longest x1 16.3 us: project(): pl.pallas_call(project_kernel, grid=(rows // tile,), in_specs=[row_blocks...]
    pallas_call x1, Pallas kernels: 58 us -> 65.4 us  [front(): pl.pallas_call(functools.partial(front_kernel, devices), in_specs=[anywhe...]
    all_to_all x1, starting transfers between devices: 12.4 us -> 5.63 us  [per_device(): lax.all_to_all(cotangent.reshape(devices, each, width), 'dp', split_axis=...]
    pallas_call x1, Pallas kernels: 38.7 us -> 43.5 us  [attend_back(): pl.pallas_call(functools.partial(attend_back_kernel, heads, kv_heads), gr...]
    select_n x3 -> x0, other arithmetic: 4.14 us -> none  [the longest x2 4.11 us: row_tables(): column = jnp.where(own, slot, local + slot)]
    another operation x13 -> x0, local copies, waits for them, and re-layouts: 4.05 us -> none  [the longest x6 3.09 us: row_tables(): jnp.stack([sorted_slot, sorted_first, sorted_place] + [blank] * 5, axis=0)]
  transfers between devices with their start and end apart: 5 -> 7, of which waited for: 1 -> 0; matrix products, arithmetic and copies ran while one was open for 7% -> 3% of each run, Pallas kernels for 46% -> 50%
where the time goes in v1:
time: 383 us; the launch traced here: 380 us
  Pallas kernels  341 us (89%)
  starting transfers between devices  17.8 us (5%)
  local copies, waits for them, and re-layouts  14.1 us (4%)
  other arithmetic  6.31 us (2%)
    pallas_call x1, Pallas kernels, feed(): pl.pallas_call(feed_kernel, grid=(2 * count,), in_specs=[own_rows(n2), an...  87.3 us
    pallas_call x1, Pallas kernels, tail(): pl.pallas_call(functools.partial(tail_kernel, plan, early, key_width, dir...  74.1 us
    pallas_call x1, Pallas kernels, front(): pl.pallas_call(functools.partial(front_kernel, devices), in_specs=[anywhe...  65.4 us
    pallas_call x1, Pallas kernels, attend_back(): pl.pallas_call(functools.partial(attend_back_kernel, heads, kv_heads), gr...  43.5 us
    pallas_call x1, Pallas kernels, attend(): pl.pallas_call(functools.partial(attend_kernel, heads, kv_heads), grid_sp...  27.9 us
    pallas_call x1, Pallas kernels, project(): pl.pallas_call(project_kernel, grid=(rows // tile,), in_specs=[row_blocks...  16.3 us
    pallas_call x1, Pallas kernels, middle_back(): pl.pallas_call(functools.partial(middle_back_kernel, plan, start), grid=(...  13.6 us
    all_to_all x1, starting transfers between devices, per_device(): lax.all_to_all(layer_rows.reshape(devices * parts, piece, width), ('dp',...  7.89 us
  transfers between devices with their start and end apart: 7, of which 0 were waited for; matrix products, arithmetic and copies ran while one was open for 3% of the time, Pallas kernels for 50%

profile of v1, /device:TPU:1, one launch (start us, length us, event | category | flops | bytes accessed | tf_op | source)
XLA Modules:
  0.0 379.9 jit_solution(3387102182276063662)
XLA Ops:
  0.6 1.0 convert_element_type.21
  1.6 0.8 reshape.96.chunk_ref
  2.4 0.8 pad_maximum_fusion.1
  3.2 0.6 reshape.100.bias_ref
  3.8 65.4 %front.1 = (bf16[16,48,896]{2,1,0:T(8,128)(2,1)}, bf16[5728,4,128]{2,1,0:T(4,128)(2,1)}, bf16[2,224,896]{2,1,0:T(8,128)(2,1)}, bf16[2,32,896]{2,1,0:T(8,128)(2,1...) custom-call(bf16[16,2,48,896]{3,2,1,0:T(8,128)(2,1)} %bitcast.55, bf16[179,4,128]{2,1,0:T(4,128)(2,1)} %reshape.96.chunk_ref, ...), custom_call_target="tpu_custom_call" | custom-call | bytes 100000000 | tf_op jit(solution)/shard_map/front/pallas_call | solution.py:343
  69.2 5.6 %all-to-all-start = ((bf16[16,96,896]{2,1,0:T(8,128)(2,1)}), bf16[16,96,896]{2,1,0:T(8,128)(2,1)S(1)}, u32[]{:S(2)}, u32[]{:S(2)}) async-start(bf16[16,96,896]{2,1,0:T(8,128)(2,1)} %bitcast.56), calls=%async_computation | async-start | bytes 5505024 | tf_op jit(solution)/shard_map/all_to_all | solution.py:1938
  74.9 0.7 broadcast_in_dim.12.freq_ref
  75.6 5.5 %tables.1 = (f32[32,1536]{1,0:T(8,128)}, f32[32,1536]{1,0:T(8,128)}, s32[768,8]{1,0:T(8,128)}, s32[768,8]{1,0:T(8,128)}, s32[768,8]{1,0:T(8,128)}, /*index=5*/s3...) custom-call(s32[1]{0:T(128)} %bitcast.part_ref, s32[3]{0:T(128)} %bitcast.70, s32[3]{0:T(128)} %bitcast.71, ...), custom_call_target="tpu_custom_call" | custom-call | flops 100000000 | bytes 4000000 | tf_op jit(solution)/shard_map/tables/pallas_call | solution.py:1876
  81.1 0.6 slice_convert_fusion
  81.7 0.6 broadcast_in_dim.27.mb_ref
  82.3 16.3 %project.1 = (bf16[768,896]{1,0:T(8,128)(2,1)}, bf16[768,896]{1,0:T(8,128)(2,1)}, bf16[768,256]{1,0:T(8,128)(2,1)}, bf16[768,384]{1,0:T(8,128)(2,1)}, f32[768,12...) custom-call(bf16[768,896]{1,0:T(8,128)(2,1)} %bitcast.44, ...), custom_call_target="tpu_custom_call" | custom-call | flops 2202009600 | bytes 9000000 | tf_op jit(solution)/shard_map/project/pallas_call | solution.py:493
  98.7 0.9 collective-permute-start
  99.6 27.9 %attend.1 = (bf16[768,896]{1,0:T(8,128)(2,1)}, bf16[768,896]{1,0:T(8,128)(2,1)}, f32[16,768]{1,0:T(8,128)}, bf16[1536,256]{1,0:T(8,128)(2,1)}, bf16[768,896]{1,0:T(8,128)(2,1)}) custom-call(s32[2,6]{1,0:T(2,128)} %get-tuple-element.61.bounds_ref, bf16[768,896]{1,0:T(8,128)(2,1)} %get-tuple-element.72.all_ref, s32[768,8]{1,0:T(8,128)} %get-tuple-element.73.meta_ref, ...), custom_call_target="tpu_custom_call" | custom-call | flops 33030144000 | bytes 6000000 | tf_op jit(solution)/shard_map/attend/pallas_call | solution.py:633
  127.6 7.1 %middle.1 = (f32[768,896]{1,0:T(8,128)}, bf16[768,896]{1,0:T(8,128)(2,1)}, bf16[768,128]{1,0:T(8,128)(2,1)}, bf16[896,1024]{1,0:T(8,128)(2,1)}) custom-call(s32[1]{0:T(128)} %bitcast.part_ref, bf16[768,896]{1,0:T(8,128)(2,1)} %get-tuple-element.79.o_ref, bf16[768,896]{1,0:T(8,128)(2,1)} %bitcast.45, s32[768,8]{1,0:T(8,128)} %get-tuple-element.64.meta_ref.refs_6_, ...), custom_call_target="tpu_custom_call" | custom-call | flops 1513881600 | bytes 12000000 | tf_op jit(solution)/shard_map/middle/pallas_call | solution.py:850
  134.7 1.8 constant_dynamic-slice_fusion.1
  136.5 87.3 %feed.1 = (f32[768,896]{1,0:T(8,128)}, f32[768,896]{1,0:T(8,128)}, bf16[2,256,896]{2,1,0:T(8,128)(2,1)}, bf16[3,256,896]{2,1,0:T(8,128)(2,1)}, bf16[256,896]{1,0:T(8,128)(2,1)}, /*index=5*/bf16[22976,128]{1,0:T(8,128)(2,1)}) custom-call(bf16[768,896]{1,0:T(8,128)(2,1)} %get-tuple-element.82.n_ref.n_hbm, bf16[768,896]{1,0:T(8,128)(2,1)} %get-tuple-element.82.n_ref.n_hbm, ...), custom_call_target="tpu_custom_call" | custom-call | flops 48771366912 | bytes 40000000 | tf_op jit(solution)/shard_map/feed/pallas_call | solution.py:1285
  223.7 0.7 collective-permute-start.1
  224.5 13.6 %middle_back.1 = (f32[768,896]{1,0:T(8,128)}, bf16[768,896]{1,0:T(8,128)(2,1)}, bf16[1792,128]{1,0:T(8,128)(2,1)}, bf16[3,3,736,128]{3,2,1,0:T(8,128)(2,1)}, f32[3,736,128]{2,1,0:T(8,128)}) custom-call(f32[768,896]{1,0:T(8,128)} %get-tuple-element.88.da_ref, bf16[768,896]{1,0:T(8,128)(2,1)} %bitcast.59, f32[768,896]{1,0:T(8,128)} %get-tuple-element.81.y1_ref, ...), custom_call_target="tpu_custom_call" | custom-call | flops 2064384000 | bytes 20000000 | tf_op jit(solution)/shard_map/middle_back/pallas_call | solution.py:1007
  238.1 2.8 slice_bitcast_fusion
  241.1 1.4 collective-permute-start.3
  242.4 1.1 collective-permute-start.2
  243.7 0.6 fusion.1
  244.3 1.7 broadcast_in_dim.30
  246.0 7.9 %all-to-all-start.1 = ((bf16[32,48,896]{2,1,0:T(8,128)(2,1)}), bf16[32,48,896]{2,1,0:T(8,128)(2,1)S(1)}, u32[]{:S(2)}, u32[]{:S(2)}) async-start(bf16[32,48,896]{2,1,0:T(8,128)(2,1)} %bitcast.49), calls=%async_computation.1 | async-start | bytes 5505024 | tf_op jit(solution)/shard_map/all_to_all | solution.py:1990
  253.9 43.5 %attend_back.1 = (bf16[768,896]{1,0:T(8,128)(2,1)}, bf16[768,256]{1,0:T(8,128)(2,1)}, bf16[768,256]{1,0:T(8,128)(2,1)}) custom-call(s32[2,6]{1,0:T(2,128)} %get-tuple-element.61.bounds_ref, bf16[768,896]{1,0:T(8,128)(2,1)} %get-tuple-element.95.q_ref, bf16[768,896]{1,0:T(8,128)(2,1)} %get-tuple-element.96.all_ref, bf16[768,896]{1,0:T(8,128)(2,1)} %get-tuple-element.97.o_ref, ...), custom_call_target="tpu_custom_call" | custom-call | flops 49545216000 | bytes 9000000 | tf_op jit(solution)/shard_map/attend_back/pallas_call | solution.py:774
  297.4 0.8 copy-done.8
  298.3 74.1 %tail.1 = (bf16[16,2,48,896]{3,2,1,0:T(8,128)(2,1)}, f32[736,128]{1,0:T(8,128)}) custom-call(bf16[768,896]{1,0:T(8,128)(2,1)} %get-tuple-element.101.refs_0_, bf16[768,256]{1,0:T(8,128)(2,1)} %get-tuple-element.102.refs_1_, bf16[768,896]{1,0:T(8,128)(2,1)} %bitcast.46, bf16[768,896]{1,0:T(8,128)(2,1)} %get-tuple-element.103.refs_3_, ...), custom_call_target="tpu_custom_call" | custom-call | flops 3991142400 | bytes 200000000 | tf_op jit(solution)/shard_map/tail/pallas_call | solution.py:1747
  372.4 2.3 fusion.3
  374.7 0.9 broadcast_multiply_fusion
  375.6 1.5 copy.28
  377.1 1.2 copy-done.2
  378.4 1.5 copy.29
  (29 shorter events, 0.4 us)
Async XLA Ops:
  69.2 11.9 %copy-start.9 = (bf16[2,896]{1,0:T(2,128)(2,1)S(1)}, bf16[2,896]{1,0:T(2,128)(2,1)}, u32[]{:S(2)}) copy-start(bf16[2,896]{1,0:T(2,128)(2,1)} %param.24) | copy-start | bytes 10756
  69.2 65.5 %all-to-all-start = ((bf16[16,96,896]{2,1,0:T(8,128)(2,1)}), bf16[16,96,896]{2,1,0:T(8,128)(2,1)S(1)}, u32[]{:S(2)}, u32[]{:S(2)}) async-start(bf16[16,96,896]{2,1,0:T(8,128)(2,1)} %bitcast.56), calls=%async_computation | async-start | bytes 5505024 | tf_op jit(solution)/shard_map/all_to_all | solution.py:1938
  82.3 16.4 %copy-start.7 = (bf16[448,896]{1,0:T(8,128)(2,1)S(1)}, bf16[448,896]{1,0:T(8,128)(2,1)}, u32[]{:S(2)}) copy-start(bf16[448,896]{1,0:T(8,128)(2,1)} %mine_ref) | copy-start | bytes 2408452
  98.7 28.9 %collective-permute-start = (bf16[448,896]{1,0:T(8,128)(2,1)S(1)}, bf16[448,896]{1,0:T(8,128)(2,1)}, u32[]{:S(2)}, u32[]{:S(2)}) collective-permute-start(bf16[448,896]{1,0:T(8,128)(2,1)S(1)} %copy-done.7), channel_id=1, source_target_pairs={{0,1},{1,0},{2,3},{3,2},{4,5},{5,4},{6,7},{7,6},{8,9},{9,8},{10,11... | collective-permute-start | bytes 2408456 | tf_op jit(solution)/shard_map/ppermute | solution.py:1909
  223.7 19.8 %collective-permute-start.1 = (bf16[256,896]{1,0:T(8,128)(2,1)}, bf16[256,896]{1,0:T(8,128)(2,1)S(1)}, u32[]{:S(2)}, u32[]{:S(2)}) collective-permute-start(bf16[256,896]{1,0:T(8,128)(2,1)} %get-tuple-element.87), channel_id=1, source_target_pairs={{0,1},{1,0},{2,3},{3,2},{4,5},{5,4},{6,7},{7,6},{8,9},{9,8},{10,11... | collective-permute-start | bytes 1376264 | tf_op jit(solution)/shard_map/ppermute | solution.py:1909
  224.5 19.0 %copy-start.6 = (bf16[2,256,896]{2,1,0:T(8,128)(2,1)S(1)}, bf16[2,256,896]{2,1,0:T(8,128)(2,1)}, u32[]{:S(2)}) copy-start(bf16[2,256,896]{2,1,0:T(8,128)(2,1)} %get-tuple-element.86) | copy-start | bytes 2752516
  238.0 5.6 %copy-start.1 = (f32[768,896]{1,0:T(8,128)S(1)}, f32[768,896]{1,0:T(8,128)}, u32[]{:S(2)}) copy-start(f32[768,896]{1,0:T(8,128)} %get-tuple-element.85) | copy-start | bytes 8257540
  240.8 2.8 copy-start
  240.8 56.6 %collective-permute-start.4 = (bf16[3,736,128]{2,1,0:T(8,128)(2,1)}, bf16[3,736,128]{2,1,0:T(8,128)(2,1)S(1)}, u32[]{:S(2)}, u32[]{:S(2)}) collective-permute-start(bf16[3,736,128]{2,1,0:T(8,128)(2,1)} %get-tuple-element.121), channel_id=1, source_target_pairs={{0,5},{1,4},{2,7},{3,6},{4,1},{5,0},{6,3},{7,2},{8,13},{9,12},{10,... | collective-permute-start | bytes 1695752 | tf_op jit(solution)/shard_map/ppermute | solution.py:1986
  241.1 56.4 %collective-permute-start.3 = (bf16[3,736,128]{2,1,0:T(8,128)(2,1)}, bf16[3,736,128]{2,1,0:T(8,128)(2,1)}, u32[]{:S(2)}, u32[]{:S(2)}) collective-permute-start(bf16[3,736,128]{2,1,0:T(8,128)(2,1)} %get-tuple-element.122), channel_id=1, source_target_pairs={{0,1},{1,0},{2,3},{3,2},{4,5},{5,4},{6,7},{7,6},{8,9},{9,8},{10,11... | collective-permute-start | bytes 1695752 | tf_op jit(solution)/shard_map/ppermute | solution.py:1986
  242.4 55.0 %collective-permute-start.2 = (bf16[3,736,128]{2,1,0:T(8,128)(2,1)}, bf16[3,736,128]{2,1,0:T(8,128)(2,1)}, u32[]{:S(2)}, u32[]{:S(2)}) collective-permute-start(bf16[3,736,128]{2,1,0:T(8,128)(2,1)} %get-tuple-element.123), channel_id=1, source_target_pairs={{0,4},{1,5},{2,6},{3,7},{4,0},{5,1},{6,2},{7,3},{8,12},{9,13},{10,... | collective-permute-start | bytes 1695752 | tf_op jit(solution)/shard_map/ppermute | solution.py:1986
  246.0 129.6 %all-to-all-start.1 = ((bf16[32,48,896]{2,1,0:T(8,128)(2,1)}), bf16[32,48,896]{2,1,0:T(8,128)(2,1)S(1)}, u32[]{:S(2)}, u32[]{:S(2)}) async-start(bf16[32,48,896]{2,1,0:T(8,128)(2,1)} %bitcast.49), calls=%async_computation.1 | async-start | bytes 5505024 | tf_op jit(solution)/shard_map/all_to_all | solution.py:1990
  297.4 0.8 copy-start.8
  298.3 74.1 %copy-start.3 = (f32[716,128]{1,0:T(8,128)S(1)}, f32[716,128]{1,0:T(8,128)}, u32[]{:S(2)}) copy-start(f32[716,128]{1,0:T(8,128)} %param.35) | copy-start | bytes 1099780
  298.3 74.1 %copy-start.4 = (f32[716,128]{1,0:T(8,128)S(1)}, f32[716,128]{1,0:T(8,128)}, u32[]{:S(2)}) copy-start(f32[716,128]{1,0:T(8,128)} %param.36) | copy-start | bytes 1099780
  374.7 2.4 copy-start.5
  375.6 2.8 copy-start.2

commit v2 on v1

--- a/solution.py
+++ b/solution.py
@@ -22,6 +22,7 @@
 MASKED_SCORE = -1e30
 PLANES = 4
 FLAT_PAD = 64
+SWAPPED = 1
 MESH = pl.DeviceIdType.MESH
 
 LANES = 128
@@ -902,10 +903,11 @@
 def middle_back_kernel(
     plan, first_b, da_ref, db_ref, y1_ref, dy_ref, o_ref, z_ref, meta_ref, copies_ref, w_ref,
     gain_ref, flat_ref,
-    dy1_ref, dar_ref, grad_ref, on_ref, kept_ref, acc_bo, acc_ao, mine, inbox, b_ref, msem, ssem,
-    rsem, bsem,
+    dy1_ref, dar_ref, grad_ref, kept_ref, *rest,
 ):
     step = pl.program_id(0)
+    on_refs = rest[: plan.boxes(0) - 1]
+    acc_bo, acc_ao, mine, inbox, b_ref, msem, ssem, rsem, bsem = rest[plan.boxes(0) - 1 :]
     b_load = pltpu.make_async_copy(
         copies_ref.at[pl.ds(first_b, b_ref.shape[0]), :], b_ref, bsem.at[0]
     )
@@ -983,7 +985,7 @@
                 if peer == 0:
                     kept_ref[zz - 1] = total(zz, at, side)
                 else:
-                    on_ref[peer - 1, zz - 1] = total(zz, at, side).astype(BF16)
+                    on_refs[peer - 1][zz - 1] = total(zz, at, side).astype(BF16)
         for copy in remote:
             copy.wait_send()
 
@@ -1001,9 +1003,8 @@
         jax.ShapeDtypeStruct((rows, width), F32),
         jax.ShapeDtypeStruct((rows, qw), BF16),
         jax.ShapeDtypeStruct((qw + width, rank), BF16),
-        jax.ShapeDtypeStruct((plan.boxes(0) - 1, PLANES - 1, plan.rows, rank), BF16),
         jax.ShapeDtypeStruct((PLANES - 1, plan.rows, rank), F32),
-    ]
+    ] + [jax.ShapeDtypeStruct((PLANES - 1, plan.rows, rank), BF16)] * (plan.boxes(0) - 1)
     return pl.pallas_call(
         functools.partial(middle_back_kernel, plan, start),
         grid=(rows // tile,),
@@ -1047,7 +1048,7 @@
 ):
     step = pl.program_id(0)
     steps = pl.num_programs(0)
-    tiles_each = n_got.shape[0]
+    tiles_each, swapped = n_got.shape[0], held_y.shape[0]
     width, half = wg_hbm.shape
     rank = bd_ref.shape[1]
     rows = n_ref.shape[0]
@@ -1213,14 +1214,17 @@
         held_d[number_t] = change.astype(BF16)
         send_d(number_t).start()
 
-        @pl.when(number_t < tiles_each - 1)
+        @pl.when(number_t < swapped)
         def _():
             held_y[number_t] = result.astype(BF16)
 
+        @pl.when(number_t >= swapped)
+        def _():
+            last_ref[number_t - swapped] = result.astype(BF16)
+
         @pl.when(number_t == tiles_each - 1)
         def _():
-            last_ref[...] = result.astype(BF16)
-            for number in range(tiles_each - 1):
+            for number in range(swapped):
                 send_y(number).start()
 
     @pl.when(step == steps - 1)
@@ -1251,7 +1255,7 @@
             send_n(number).wait_send()
             send_d(number).wait_send()
             send_d(number).wait_recv()
-        for number in range(tiles_each - 1):
+        for number in range(swapped):
             send_y(number).wait_send()
             send_y(number).wait_recv()
 
@@ -1277,9 +1281,9 @@
     outs = [
         jax.ShapeDtypeStruct((rows, width), F32),
         jax.ShapeDtypeStruct((rows, width), F32),
-        jax.ShapeDtypeStruct((count - 1, tile, width), BF16),
+        jax.ShapeDtypeStruct((SWAPPED, tile, width), BF16),
         jax.ShapeDtypeStruct((count, tile, width), BF16),
-        jax.ShapeDtypeStruct((tile, width), BF16),
+        jax.ShapeDtypeStruct((count - SWAPPED, tile, width), BF16),
         jax.ShapeDtypeStruct((total + FLAT_PAD, rank), BF16),
     ]
     return pl.pallas_call(
@@ -1307,7 +1311,7 @@
             pltpu.VMEM((tile, rank), F32),
             pltpu.VMEM((count, tile, width), BF16),
             pltpu.VMEM((count, tile, width), BF16),
-            pltpu.VMEM((count - 1, tile, width), BF16),
+            pltpu.VMEM((SWAPPED, tile, width), BF16),
             pltpu.VMEM((3, half + width, rank), BF16),
             pltpu.VMEM((half, rank), BF16),
             pltpu.VMEM((width, 2 * rank), BF16),
@@ -1318,8 +1322,8 @@
             dma((count,)),
             dma((count,)),
             dma((count,)),
-            dma((count - 1,)),
-            dma((count - 1,)),
+            dma((SWAPPED,)),
+            dma((SWAPPED,)),
         ],
         compiler_params=params(collective_id=1, has_side_effects=True),
         cost_estimate=cost(4 * rows * half * (6 * width + 9 * rank), 40e6),
@@ -1621,9 +1625,8 @@
     forwards = []
 
     def forward(back):
-        source = layer(back)
         for step in range(plane):
-            at = source * plane + step_at(step)
+            at = layer(back) * plane + step_at(step)
             if step > 0 or back > 0:
                 pltpu.make_async_remote_copy(
                     src_ref=out_ref.at[at, part],
@@ -1637,39 +1640,41 @@
                 pltpu.make_async_copy(
                     out_ref.at[place, part], out_ref.at[place, part], keep_sem.at[0]
                 ).wait()
-        copy = forward_copy(source, part, len(forwards))
-        copy.start()
-        forwards.append(copy)
+            copy = forward_copy(at, part, len(forwards))
+            copy.start()
+            forwards.append(copy)
 
     def forward_copy(source, side, number):
-        span = pl.ds(source * plane, plane)
         return pltpu.make_async_remote_copy(
-            src_ref=out_ref.at[span, side],
-            dst_ref=out_ref.at[span, side],
+            src_ref=out_ref.at[source, side],
+            dst_ref=out_ref.at[source, side],
             send_sem=fsend.at[number],
             recv_sem=frecv.at[source],
             device_id=over,
             device_id_type=MESH,
         )
 
+    stage_sends(1)
+    if direct:
+        forward(0)
     for zz in range(1, PLANES):
         far(zz, came[zz - 1])
-    for stage in range(1, count):
+    if direct:
+        forward(2)
+    for stage in range(2, count):
         stage_sends(stage)
-        if direct and stage <= 2:
-            forward((0, 0, 3)[stage])
+    if direct:
+        forward(1)
     late = near(0)
     if direct:
-        forward(1)
+        forward(3)
     far(0, late)
-    if direct:
-        forward(2)
     plane_copy(0, PLANES, PLANES, 0, depth).wait_recv()
     sum_ref[...] += last_in[PLANES].astype(F32)
 
     if direct:
-        for back in range(PLANES):
-            forward_copy(layer(back), 1 - part, 0).wait_recv()
+        for source in range(devices):
+            forward_copy(source, 1 - part, 0).wait_recv()
         for copy in forwards:
             copy.wait_send()
         for number in range(PLANES):
@@ -1734,8 +1739,8 @@
         dma((4 + peers,)),
         dma((PLANES, plane)),
         dma((devices,)),
-        dma((PLANES,)),
-        dma((PLANES,)),
+        dma((devices,)),
+        dma((devices,)),
         dma((sends,)),
         dma((sum(boxes),)),
         dma((PLANES + 1,)),
@@ -1969,8 +1974,8 @@
     y_own, d_own, y_got, d_got, y_last, flat_grads = feed(
         n2, dy, dy_theirs, meta_own, meta_other, w_gate, w_up, w_down, flat
     )
-    y_got = jnp.concatenate([y_got, across(y_last)[None]], axis=0).reshape(local, width)
-    dy1, dar, grad_out, on_sums, kept_sums = middle_back(
+    y_got = jnp.concatenate([y_got, across(y_last)], axis=0).reshape(local, width)
+    dy1, dar, grad_out, kept_sums, *on_sums = middle_back(
         devices, own_rows, d_own, d_got.reshape(local, width), y1, dy, o, z_out, meta_own, flat,
         early + qw, w_out_cat, gain_two, flat_grads,
     )

time: 383 us -> 379 us (0.990)
  waiting for transfers between devices: 0.02 us -> 4.53 us
  Pallas kernels: 341 us -> 337 us
    ppermute x2, waiting for transfers between devices: 0.01 us -> 4.52 us  [across(): return lax.ppermute(values, 'tensor', swap)]
    pallas_call x1, Pallas kernels: 87.3 us -> 83.3 us  [feed(): pl.pallas_call(feed_kernel, grid=(2 * count,), in_specs=[own_rows(n2), an...]
  transfers between devices with their start and end apart: 7 -> 7, of which waited for: 0 -> 1; matrix products, arithmetic and copies ran while one was open for 3% -> 2% of each run, Pallas kernels for 50% -> 50%
where the time goes in v2:
time: 379 us; the launch traced here: 378 us
  Pallas kernels  337 us (89%)
  starting transfers between devices  18.8 us (5%)
  local copies, waits for them, and re-layouts  10.6 us (3%)
  other arithmetic  6.35 us (2%)
  waiting for transfers between devices  4.53 us (1%)
    pallas_call x1, Pallas kernels, feed(): pl.pallas_call(feed_kernel, grid=(2 * count,), in_specs=[own_rows(n2), an...  83.3 us
    pallas_call x1, Pallas kernels, tail(): pl.pallas_call(functools.partial(tail_kernel, plan, early, key_width, dir...  76.2 us
    pallas_call x1, Pallas kernels, front(): pl.pallas_call(functools.partial(front_kernel, devices), in_specs=[anywhe...  65.4 us
    pallas_call x1, Pallas kernels, attend_back(): pl.pallas_call(functools.partial(attend_back_kernel, heads, kv_heads), gr...  41.9 us
    pallas_call x1, Pallas kernels, attend(): pl.pallas_call(functools.partial(attend_kernel, heads, kv_heads), grid_sp...  27.1 us
    pallas_call x1, Pallas kernels, project(): pl.pallas_call(project_kernel, grid=(rows // tile,), in_specs=[row_blocks...  16.3 us
    pallas_call x1, Pallas kernels, middle_back(): pl.pallas_call(functools.partial(middle_back_kernel, plan, start), grid=(...  14.2 us
    all_to_all x1, starting transfers between devices, per_device(): lax.all_to_all(layer_rows.reshape(devices * parts, piece, width), ('dp',...  9.42 us
  transfers between devices with their start and end apart: 7, of which 1 were waited for; matrix products, arithmetic and copies ran while one was open for 2% of the time, Pallas kernels for 50%

profile of v2, /device:TPU:1, one launch (start us, length us, event | category | flops | bytes accessed | tf_op | source)
XLA Modules:
  0.0 378.1 jit_solution(2842264397675692018)
XLA Ops:
  0.6 1.0 convert_element_type.21
  1.6 0.8 reshape.96.chunk_ref
  2.4 0.8 pad_maximum_fusion.1
  3.2 0.6 reshape.100.bias_ref
  3.8 65.4 %front.1 = (bf16[16,48,896]{2,1,0:T(8,128)(2,1)}, bf16[5728,4,128]{2,1,0:T(4,128)(2,1)}, bf16[2,224,896]{2,1,0:T(8,128)(2,1)}, bf16[2,32,896]{2,1,0:T(8,128)(2,1...) custom-call(bf16[16,2,48,896]{3,2,1,0:T(8,128)(2,1)} %bitcast.48, bf16[179,4,128]{2,1,0:T(4,128)(2,1)} %reshape.96.chunk_ref, ...), custom_call_target="tpu_custom_call" | custom-call | bytes 100000000 | tf_op jit(solution)/shard_map/front/pallas_call | solution.py:344
  69.2 5.6 %all-to-all-start = ((bf16[16,96,896]{2,1,0:T(8,128)(2,1)}), bf16[16,96,896]{2,1,0:T(8,128)(2,1)S(1)}, u32[]{:S(2)}, u32[]{:S(2)}) async-start(bf16[16,96,896]{2,1,0:T(8,128)(2,1)} %bitcast.49), calls=%async_computation | async-start | bytes 5505024 | tf_op jit(solution)/shard_map/all_to_all | solution.py:1943
  74.9 0.7 broadcast_in_dim.10.freq_ref
  75.6 5.5 %tables.1 = (f32[32,1536]{1,0:T(8,128)}, f32[32,1536]{1,0:T(8,128)}, s32[768,8]{1,0:T(8,128)}, s32[768,8]{1,0:T(8,128)}, s32[768,8]{1,0:T(8,128)}, /*index=5*/s3...) custom-call(s32[1]{0:T(128)} %bitcast.part_ref, s32[3]{0:T(128)} %bitcast.62, s32[3]{0:T(128)} %bitcast.63, ...), custom_call_target="tpu_custom_call" | custom-call | flops 100000000 | bytes 4000000 | tf_op jit(solution)/shard_map/tables/pallas_call | solution.py:1881
  81.1 0.6 slice_convert_fusion
  81.7 0.6 broadcast_in_dim.24.mb_ref
  82.3 16.3 %project.1 = (bf16[768,896]{1,0:T(8,128)(2,1)}, bf16[768,896]{1,0:T(8,128)(2,1)}, bf16[768,256]{1,0:T(8,128)(2,1)}, bf16[768,384]{1,0:T(8,128)(2,1)}, f32[768,12...) custom-call(bf16[768,896]{1,0:T(8,128)(2,1)} %bitcast.37, ...), custom_call_target="tpu_custom_call" | custom-call | flops 2202009600 | bytes 9000000 | tf_op jit(solution)/shard_map/project/pallas_call | solution.py:494
  98.7 1.0 collective-permute-start
  99.6 27.1 %attend.1 = (bf16[768,896]{1,0:T(8,128)(2,1)}, bf16[768,896]{1,0:T(8,128)(2,1)}, f32[16,768]{1,0:T(8,128)}, bf16[1536,256]{1,0:T(8,128)(2,1)}, bf16[768,896]{1,0:T(8,128)(2,1)}) custom-call(s32[2,6]{1,0:T(2,128)} %get-tuple-element.63.bounds_ref, bf16[768,896]{1,0:T(8,128)(2,1)} %get-tuple-element.74.all_ref, s32[768,8]{1,0:T(8,128)} %get-tuple-element.75.meta_ref, ...), custom_call_target="tpu_custom_call" | custom-call | flops 33030144000 | bytes 6000000 | tf_op jit(solution)/shard_map/attend/pallas_call | solution.py:634
  126.7 7.1 %middle.1 = (f32[768,896]{1,0:T(8,128)}, bf16[768,896]{1,0:T(8,128)(2,1)}, bf16[768,128]{1,0:T(8,128)(2,1)}, bf16[896,1024]{1,0:T(8,128)(2,1)}) custom-call(s32[1]{0:T(128)} %bitcast.part_ref, bf16[768,896]{1,0:T(8,128)(2,1)} %get-tuple-element.81.o_ref, bf16[768,896]{1,0:T(8,128)(2,1)} %bitcast.38, s32[768,8]{1,0:T(8,128)} %get-tuple-element.66.meta_ref.refs_6_, ...), custom_call_target="tpu_custom_call" | custom-call | flops 1513881600 | bytes 12000000 | tf_op jit(solution)/shard_map/middle/pallas_call | solution.py:851
  133.8 1.8 constant_dynamic-slice_fusion.1
  135.7 83.3 %feed.1 = (f32[768,896]{1,0:T(8,128)}, f32[768,896]{1,0:T(8,128)}, bf16[1,256,896]{2,1,0:T(8,128)(2,1)}, bf16[3,256,896]{2,1,0:T(8,128)(2,1)}, bf16[2,256,896]{2,1,0:T(8,128)(2,1)}, /*index=5*/bf16[22976,128]{1,0:T(8,128)(2,1)}) custom-call(bf16[768,896]{1,0:T(8,128)(2,1)} %get-tuple-element.84.n_ref.n_hbm, bf16[768,896]{1,0:T(8,128)(2,1)} %get-tuple-element.84.n_ref.n_hbm, ...), custom_call_target="tpu_custom_call" | custom-call | flops 48771366912 | bytes 40000000 | tf_op jit(solution)/shard_map/feed/pallas_call | solution.py:1289
  219.1 14.2 %middle_back.1 = (f32[768,896]{1,0:T(8,128)}, bf16[768,896]{1,0:T(8,128)(2,1)}, bf16[1792,128]{1,0:T(8,128)(2,1)}, f32[3,736,128]{2,1,0:T(8,128)}, bf16[3,736,12...) custom-call(f32[768,896]{1,0:T(8,128)} %get-tuple-element.90.da_ref, ...), custom_call_target="tpu_custom_call" | custom-call | flops 2064384000 | bytes 20000000 | tf_op jit(solution)/shard_map/middle_back/pallas_call | solution.py:1008
  233.3 0.8 collective-permute-start.2
  234.1 1.7 collective-permute-start.3
  235.8 0.3 collective-permute-start.4
  236.1 4.5 %collective-permute-done.1 = bf16[2,256,896]{2,1,0:T(8,128)(2,1)S(1)} collective-permute-done((bf16[2,256,896]{2,1,0:T(8,128)(2,1)}, bf16[2,256,896]{2,1,0:T(8,128)(2,1)S(1)}, u32[]{:S(2)}, u32[]{:S(2)}) %collective-permute-start.1) | collective-permute-done | bytes 917536 | tf_op jit(solution)/shard_map/ppermute | solution.py:1914
  240.6 0.1 pad_maximum_fusion
  240.7 0.6 fusion.1
  241.4 1.7 broadcast_in_dim.26
  243.1 9.4 %all-to-all-start.1 = ((bf16[32,48,896]{2,1,0:T(8,128)(2,1)}), bf16[32,48,896]{2,1,0:T(8,128)(2,1)S(1)}, u32[]{:S(2)}, u32[]{:S(2)}) async-start(bf16[32,48,896]{2,1,0:T(8,128)(2,1)} %bitcast.42), calls=%async_computation.1 | async-start | bytes 5505024 | tf_op jit(solution)/shard_map/all_to_all | solution.py:1995
  252.5 41.9 %attend_back.1 = (bf16[768,896]{1,0:T(8,128)(2,1)}, bf16[768,256]{1,0:T(8,128)(2,1)}, bf16[768,256]{1,0:T(8,128)(2,1)}) custom-call(s32[2,6]{1,0:T(2,128)} %get-tuple-element.63.bounds_ref, bf16[768,896]{1,0:T(8,128)(2,1)} %get-tuple-element.97.q_ref, bf16[768,896]{1,0:T(8,128)(2,1)} %get-tuple-element.98.all_ref, bf16[768,896]{1,0:T(8,128)(2,1)} %get-tuple-element.99.o_ref, ...), custom_call_target="tpu_custom_call" | custom-call | flops 49545216000 | bytes 9000000 | tf_op jit(solution)/shard_map/attend_back/pallas_call | solution.py:775
  294.5 76.2 %tail.1 = (bf16[16,2,48,896]{3,2,1,0:T(8,128)(2,1)}, f32[736,128]{1,0:T(8,128)}) custom-call(bf16[768,896]{1,0:T(8,128)(2,1)} %get-tuple-element.103.refs_0_, bf16[768,256]{1,0:T(8,128)(2,1)} %get-tuple-element.104.refs_1_, bf16[768,896]{1,0:T(8,128)(2,1)} %bitcast.39, bf16[768,896]{1,0:T(8,128)(2,1)} %get-tuple-element.105.refs_3_, ...), custom_call_target="tpu_custom_call" | custom-call | flops 3991142400 | bytes 200000000 | tf_op jit(solution)/shard_map/tail/pallas_call | solution.py:1752
  370.6 2.3 fusion.3
  372.9 0.9 broadcast_multiply_fusion
  373.8 1.5 copy.28
  375.4 1.2 copy-done.2
  376.6 1.5 copy.29
  (26 shorter events, 0.1 us)
Async XLA Ops:
  69.2 11.9 %copy-start.8 = (bf16[2,896]{1,0:T(2,128)(2,1)S(1)}, bf16[2,896]{1,0:T(2,128)(2,1)}, u32[]{:S(2)}) copy-start(bf16[2,896]{1,0:T(2,128)(2,1)} %param.24) | copy-start | bytes 10756
  69.2 64.6 %all-to-all-start = ((bf16[16,96,896]{2,1,0:T(8,128)(2,1)}), bf16[16,96,896]{2,1,0:T(8,128)(2,1)S(1)}, u32[]{:S(2)}, u32[]{:S(2)}) async-start(bf16[16,96,896]{2,1,0:T(8,128)(2,1)} %bitcast.49), calls=%async_computation | async-start | bytes 5505024 | tf_op jit(solution)/shard_map/all_to_all | solution.py:1943
  82.3 16.4 %copy-start.6 = (bf16[448,896]{1,0:T(8,128)(2,1)S(1)}, bf16[448,896]{1,0:T(8,128)(2,1)}, u32[]{:S(2)}) copy-start(bf16[448,896]{1,0:T(8,128)(2,1)} %mine_ref) | copy-start | bytes 2408452
  98.7 28.0 %collective-permute-start = (bf16[448,896]{1,0:T(8,128)(2,1)S(1)}, bf16[448,896]{1,0:T(8,128)(2,1)}, u32[]{:S(2)}, u32[]{:S(2)}) collective-permute-start(bf16[448,896]{1,0:T(8,128)(2,1)S(1)} %copy-done.6), channel_id=1, source_target_pairs={{0,1},{1,0},{2,3},{3,2},{4,5},{5,4},{6,7},{7,6},{8,9},{9,8},{10,11... | collective-permute-start | bytes 2408456 | tf_op jit(solution)/shard_map/ppermute | solution.py:1914
  219.0 21.6 %collective-permute-start.1 = (bf16[2,256,896]{2,1,0:T(8,128)(2,1)}, bf16[2,256,896]{2,1,0:T(8,128)(2,1)S(1)}, u32[]{:S(2)}, u32[]{:S(2)}) collective-permute-start(bf16[2,256,896]{2,1,0:T(8,128)(2,1)} %get-tuple-element.89), channel_id=1, source_target_pairs={{0,1},{1,0},{2,3},{3,2},{4,5},{5,4},{6,7},{7,6},{8,9},{9,8},{10,11... | collective-permute-start | bytes 2752520 | tf_op jit(solution)/shard_map/ppermute | solution.py:1914
  219.1 21.5 %copy-start.7 = (bf16[1,256,896]{2,1,0:T(8,128)(2,1)S(1)}, bf16[1,256,896]{2,1,0:T(8,128)(2,1)}, u32[]{:S(2)}) copy-start(bf16[1,256,896]{2,1,0:T(8,128)(2,1)} %get-tuple-element.88) | copy-start | bytes 1376260
  219.1 21.6 %copy-start.1 = (f32[768,896]{1,0:T(8,128)S(1)}, f32[768,896]{1,0:T(8,128)}, u32[]{:S(2)}) copy-start(f32[768,896]{1,0:T(8,128)} %get-tuple-element.87) | copy-start | bytes 8257540
  233.3 7.4 %copy-start = (f32[768,896]{1,0:T(8,128)S(1)}, f32[768,896]{1,0:T(8,128)}, u32[]{:S(2)}) copy-start(f32[768,896]{1,0:T(8,128)} %get-tuple-element.83.y1_ref) | copy-start | bytes 8257540
  233.3 61.1 %collective-permute-start.2 = (bf16[3,736,128]{2,1,0:T(8,128)(2,1)}, bf16[3,736,128]{2,1,0:T(8,128)(2,1)}, u32[]{:S(2)}, u32[]{:S(2)}) collective-permute-start(bf16[3,736,128]{2,1,0:T(8,128)(2,1)} %get-tuple-element.114), channel_id=1, source_target_pairs={{0,4},{1,5},{2,6},{3,7},{4,0},{5,1},{6,2},{7,3},{8,12},{9,13},{10,... | collective-permute-start | bytes 1695752 | tf_op jit(solution)/shard_map/ppermute | solution.py:1991
  234.1 60.3 %collective-permute-start.3 = (bf16[3,736,128]{2,1,0:T(8,128)(2,1)}, bf16[3,736,128]{2,1,0:T(8,128)(2,1)}, u32[]{:S(2)}, u32[]{:S(2)}) collective-permute-start(bf16[3,736,128]{2,1,0:T(8,128)(2,1)} %get-tuple-element.115), channel_id=1, source_target_pairs={{0,1},{1,0},{2,3},{3,2},{4,5},{5,4},{6,7},{7,6},{8,9},{9,8},{10,11... | collective-permute-start | bytes 1695752 | tf_op jit(solution)/shard_map/ppermute | solution.py:1991
  235.8 58.6 %collective-permute-start.4 = (bf16[3,736,128]{2,1,0:T(8,128)(2,1)}, bf16[3,736,128]{2,1,0:T(8,128)(2,1)}, u32[]{:S(2)}, u32[]{:S(2)}) collective-permute-start(bf16[3,736,128]{2,1,0:T(8,128)(2,1)} %get-tuple-element.116), channel_id=1, source_target_pairs={{0,5},{1,4},{2,7},{3,6},{4,1},{5,0},{6,3},{7,2},{8,13},{9,12},{10,... | collective-permute-start | bytes 1695752 | tf_op jit(solution)/shard_map/ppermute | solution.py:1991
  243.1 130.7 %all-to-all-start.1 = ((bf16[32,48,896]{2,1,0:T(8,128)(2,1)}), bf16[32,48,896]{2,1,0:T(8,128)(2,1)S(1)}, u32[]{:S(2)}, u32[]{:S(2)}) async-start(bf16[32,48,896]{2,1,0:T(8,128)(2,1)} %bitcast.42), calls=%async_computation.1 | async-start | bytes 5505024 | tf_op jit(solution)/shard_map/all_to_all | solution.py:1995
  294.4 76.2 %copy-start.3 = (f32[716,128]{1,0:T(8,128)S(1)}, f32[716,128]{1,0:T(8,128)}, u32[]{:S(2)}) copy-start(f32[716,128]{1,0:T(8,128)} %param.35) | copy-start | bytes 1099780
  294.4 76.2 %copy-start.4 = (f32[716,128]{1,0:T(8,128)S(1)}, f32[716,128]{1,0:T(8,128)}, u32[]{:S(2)}) copy-start(f32[716,128]{1,0:T(8,128)} %param.36) | copy-start | bytes 1099780
  372.9 2.4 copy-start.5
  373.8 2.8 copy-start.2

commit v3 on v2

--- a/solution.py
+++ b/solution.py
@@ -147,11 +147,108 @@
     return place, part
 
 
+def whole_part(values, size):
+    return jnp.floor((values + 0.5) * (1.0 / size))
+
+
+def fill_tables(
+    parts, each, part, lengths_ref, ids_ref, order_ref, freq_ref,
+    turns_ref, sines_ref, own_ref, other_ref, sorted_ref, rows_ref, column_ref, column_row_ref,
+    bounds_ref,
+):
+    total = order_ref.shape[1]
+    local = total // parts
+    piece = each // parts
+    block = 256
+    order = jnp.broadcast_to(order_ref[0:1, :].astype(F32), (8, total))
+    group = whole_part(order, each)
+    rest = order - group * each
+    part_at = whole_part(rest, piece)
+    own = part_at == part.astype(F32)
+    slot = group * piece + (rest - part_at * piece)
+    column = jnp.where(own, slot, slot + local)
+    lanes = lane_iota((8, total))
+    upto = jnp.where(own, 1.0, 0.0)
+    shift = 1
+    while shift < total:
+        upto = upto + jnp.where(lanes >= shift, pltpu.roll(upto, shift, 1), 0.0)
+        shift *= 2
+    rank = jnp.where(own, upto - 1.0, 2.0 * total)
+    place = lanes.astype(F32)
+    number = row_iota((8, total))
+    column_row_ref[...] = column.astype(I32)
+    turned = jnp.transpose(jnp.where(number == 0, column, rank))
+    column_ref[...] = turned.astype(I32)
+
+    def halves(values):
+        high = whole_part(values, 256)
+        return high, values - high * 256
+
+    place_high, place_low = halves(place)
+    slot_high, slot_low = halves(slot)
+    left = jnp.where(
+        number == 0, place_high, jnp.where(number == 1, place_low, jnp.where(number == 2, slot_high, slot_low))
+    ).astype(BF16)
+
+    def chosen_by(keys, start):
+        hit = keys == (start + lane_iota((total, block))).astype(F32)
+        found = nn(left, jnp.where(hit, 1.0, 0.0).astype(BF16))
+        return found[0:1] * 256 + found[1:2], found[2:3] * 256 + found[3:4]
+
+    def sequence(places):
+        first = jnp.zeros_like(places)
+        adapter = jnp.zeros_like(places) + ids_ref[0, 0].astype(F32)
+        start = lengths_ref[0, 0].astype(F32)
+        for at in range(1, lengths_ref.shape[1]):
+            inside = places >= start
+            first = jnp.where(inside, start, first)
+            adapter = jnp.where(inside, ids_ref[0, at].astype(F32), adapter)
+            start = start + lengths_ref[0, at].astype(F32)
+        return first, adapter
+
+    def rope(position, at):
+        angles = jnp.broadcast_to(position, freq_ref.shape[:1] + position.shape[1:]) * freq_ref[:, 0:1]
+        turns_ref[:, at : at + block] = jnp.cos(angles)
+        sines_ref[:, at : at + block] = jnp.sin(angles)
+
+    def as_columns(*rows):
+        index = row_iota((8, block))
+        out = jnp.zeros((8, block), F32)
+        for at, row in enumerate(rows):
+            out = jnp.where(index == at, jnp.broadcast_to(row, (8, block)), out)
+        return out
+
+    for start in range(0, total, block):
+        places, _ = chosen_by(turned[:, 0:1], start)
+        first, adapter = sequence(places)
+        columns = jnp.transpose(as_columns(adapter)).astype(I32)
+        if start < local:
+            rope(places - first, start)
+            own_ref[start : start + block, :] = columns
+        else:
+            other_ref[start - local : start - local + block, :] = columns
+    for start in range(0, local, block):
+        places, slots = chosen_by(turned[:, 1:2], start)
+        first, _ = sequence(places)
+        rope(places - first, local + start)
+        rows = as_columns(slots, first, places)
+        rows_ref[:, start : start + block] = rows.astype(I32)
+        sorted_ref[start : start + block, :] = jnp.transpose(rows).astype(I32)
+        at_lane = lane_iota((1, block))
+        for tile in range(0, block, QUERY_TILE):
+            low = jnp.max(jnp.where(at_lane == tile, first, 0.0))
+            high = jnp.max(jnp.where(at_lane == tile + QUERY_TILE - 1, places, 0.0))
+            number_at = (start + tile) // QUERY_TILE
+            bounds_ref[0, number_at] = low.astype(I32) // KEY_TILE
+            bounds_ref[1, number_at] = high.astype(I32) // KEY_TILE + 1
+
+
 def front_kernel(
-    devices, rows_ref, chunk_ref, wq_ref, wk_ref, wv_ref, bias_ref,
-    got_ref, copies_ref, wq_out, wk_out, wv_out, bias_out,
-    local_sem, tsend, trecv, csend, crecv, wsend, wrecv,
+    devices, each, rows_ref, chunk_ref, wq_ref, wk_ref, wv_ref, bias_ref, lengths_ref, ids_ref,
+    order_ref, freq_ref,
+    got_ref, copies_ref, wq_out, wk_out, wv_out, bias_out, *rest,
 ):
+    tables, (local_sem, tsend, trecv, csend, crecv, wsend, wrecv) = rest[:9], rest[9:]
     place, part = lax.axis_index("dp"), lax.axis_index("tensor")
     plane = devices // PLANES
     depth, inside = place // plane, lax.rem(place, plane)
@@ -297,6 +394,7 @@
                 copy = weight_copy(out, out, 3 + number, core, partner)
                 copy.start()
                 relayed.append(copy)
+            fill_tables(2, each, part, lengths_ref, ids_ref, order_ref, freq_ref, *tables)
     for hop in range(PLANES):
         order = orders[hop % 2]
         origin = layer(hop) * plane + inside
@@ -333,18 +431,36 @@
         copy.wait()
 
 
-def front(rows, chunk, wq, wk, wv, bias, devices):
+def front(rows, chunk, wq, wk, wv, bias, order, lengths, adapter_ids, devices):
     _, _, piece, width = rows.shape
+    total = order.shape[1]
+    local = total // 2
+    freq_index = jnp.arange(HEAD // 2, dtype=F32)
+    freq = jnp.power(jnp.float32(ROPE_BASE), -2.0 * freq_index / HEAD)
+    freq = jnp.broadcast_to(freq[:, None], (HEAD // 2, LANES))
     anywhere = pl.BlockSpec(memory_space=pl.ANY)
     outs = [
         jax.ShapeDtypeStruct((devices, piece, width), BF16),
         jax.ShapeDtypeStruct((2 * devices * chunk.shape[0],) + chunk.shape[1:], BF16),
     ] + [jax.ShapeDtypeStruct(a.shape, BF16) for a in (wq, wk, wv, bias)]
+    shapes = [
+        ((HEAD // 2, total), F32),
+        ((HEAD // 2, total), F32),
+        ((local, 8), I32),
+        ((local, 8), I32),
+        ((local, 8), I32),
+        ((8, local), I32),
+        ((total, 8), I32),
+        ((8, total), I32),
+        ((2, local // QUERY_TILE), I32),
+    ]
+    outs += [jax.ShapeDtypeStruct(shape, kind) for shape, kind in shapes]
     dma = pltpu.SemaphoreType.DMA
+    near, scalar = pl.BlockSpec(memory_space=pltpu.VMEM), pl.BlockSpec(memory_space=pltpu.SMEM)
     return pl.pallas_call(
-        functools.partial(front_kernel, devices),
-        in_specs=[anywhere] * 6,
-        out_specs=[anywhere] * 6,
+        functools.partial(front_kernel, devices, 2 * piece),
+        in_specs=[anywhere] * 6 + [scalar, scalar, near, near],
+        out_specs=[anywhere] * 6 + [near] * 8 + [scalar],
         out_shape=outs,
         scratch_shapes=[
             dma((2,)),
@@ -355,10 +471,10 @@
             dma((8,)),
             dma((8,)),
         ],
-        compiler_params=pltpu.CompilerParams(collective_id=0, has_side_effects=True),
+        compiler_params=params(collective_id=0, has_side_effects=True),
         cost_estimate=cost(0, 100e6),
         name="front",
-    )(rows, chunk, wq, wk, wv, bias)
+    )(rows, chunk, wq, wk, wv, bias, lengths, adapter_ids, order, freq)
 
 
 def in_order(part, mine, theirs, place):
@@ -1764,135 +1880,6 @@
     )(*rows_in, other, w_cat, b_rows, gain, flat, grad_out, kept, *gots)
 
 
-def whole_part(values, size):
-    return jnp.floor((values + 0.5) * (1.0 / size))
-
-
-def tables_kernel(
-    parts, each, part_ref, lengths_ref, ids_ref, order_ref, freq_ref,
-    turns_ref, sines_ref, own_ref, other_ref, sorted_ref, rows_ref, column_ref, column_row_ref,
-    bounds_ref,
-):
-    total = order_ref.shape[1]
-    local = total // parts
-    piece = each // parts
-    block = 256
-    order = jnp.broadcast_to(order_ref[0:1, :].astype(F32), (8, total))
-    group = whole_part(order, each)
-    rest = order - group * each
-    part_at = whole_part(rest, piece)
-    own = part_at == part_ref[0].astype(F32)
-    slot = group * piece + (rest - part_at * piece)
-    column = jnp.where(own, slot, slot + local)
-    lanes = lane_iota((8, total))
-    upto = jnp.where(own, 1.0, 0.0)
-    shift = 1
-    while shift < total:
-        upto = upto + jnp.where(lanes >= shift, pltpu.roll(upto, shift, 1), 0.0)
-        shift *= 2
-    rank = jnp.where(own, upto - 1.0, 2.0 * total)
-    place = lanes.astype(F32)
-    number = row_iota((8, total))
-    column_row_ref[...] = column.astype(I32)
-    turned = jnp.transpose(jnp.where(number == 0, column, rank))
-    column_ref[...] = turned.astype(I32)
-
-    def halves(values):
-        high = whole_part(values, 256)
-        return high, values - high * 256
-
-    place_high, place_low = halves(place)
-    slot_high, slot_low = halves(slot)
-    left = jnp.where(
-        number == 0, place_high, jnp.where(number == 1, place_low, jnp.where(number == 2, slot_high, slot_low))
-    ).astype(BF16)
-
-    def chosen_by(keys, start):
-        hit = keys == (start + lane_iota((total, block))).astype(F32)
-        found = nn(left, jnp.where(hit, 1.0, 0.0).astype(BF16))
-        return found[0:1] * 256 + found[1:2], found[2:3] * 256 + found[3:4]
-
-    def sequence(places):
-        first = jnp.zeros_like(places)
-        adapter = jnp.zeros_like(places) + ids_ref[0].astype(F32)
-        start = lengths_ref[0].astype(F32)
-        for at in range(1, lengths_ref.shape[0]):
-            inside = places >= start
-            first = jnp.where(inside, start, first)
-            adapter = jnp.where(inside, ids_ref[at].astype(F32), adapter)
-            start = start + lengths_ref[at].astype(F32)
-        return first, adapter
-
-    def rope(position, at):
-        angles = jnp.broadcast_to(position, freq_ref.shape[:1] + position.shape[1:]) * freq_ref[:, 0:1]
-        turns_ref[:, at : at + block] = jnp.cos(angles)
-        sines_ref[:, at : at + block] = jnp.sin(angles)
-
-    def as_columns(*rows):
-        index = row_iota((8, block))
-        out = jnp.zeros((8, block), F32)
-        for at, row in enumerate(rows):
-            out = jnp.where(index == at, jnp.broadcast_to(row, (8, block)), out)
-        return out
-
-    for start in range(0, total, block):
-        places, _ = chosen_by(turned[:, 0:1], start)
-        first, adapter = sequence(places)
-        columns = jnp.transpose(as_columns(adapter)).astype(I32)
-        if start < local:
-            rope(places - first, start)
-            own_ref[start : start + block, :] = columns
-        else:
-            other_ref[start - local : start - local + block, :] = columns
-    for start in range(0, local, block):
-        places, slots = chosen_by(turned[:, 1:2], start)
-        first, _ = sequence(places)
-        rope(places - first, local + start)
-        rows = as_columns(slots, first, places)
-        rows_ref[:, start : start + block] = rows.astype(I32)
-        sorted_ref[start : start + block, :] = jnp.transpose(rows).astype(I32)
-        at_lane = lane_iota((1, block))
-        for tile in range(0, block, QUERY_TILE):
-            low = jnp.max(jnp.where(at_lane == tile, first, 0.0))
-            high = jnp.max(jnp.where(at_lane == tile + QUERY_TILE - 1, places, 0.0))
-            number_at = (start + tile) // QUERY_TILE
-            bounds_ref[0, number_at] = low.astype(I32) // KEY_TILE
-            bounds_ref[1, number_at] = high.astype(I32) // KEY_TILE + 1
-
-
-def row_tables(order, lengths, adapter_ids, part, parts, each):
-    total = order.shape[1]
-    local = total // parts
-    freq_index = jnp.arange(HEAD // 2, dtype=F32)
-    freq = jnp.power(jnp.float32(ROPE_BASE), -2.0 * freq_index / HEAD)
-    freq = jnp.broadcast_to(freq[:, None], (HEAD // 2, LANES))
-    shapes = [
-        ((HEAD // 2, total), F32),
-        ((HEAD // 2, total), F32),
-        ((local, 8), I32),
-        ((local, 8), I32),
-        ((local, 8), I32),
-        ((8, local), I32),
-        ((total, 8), I32),
-        ((8, total), I32),
-        ((2, local // QUERY_TILE), I32),
-    ]
-    outs = [jax.ShapeDtypeStruct(shape, kind) for shape, kind in shapes]
-    return pl.pallas_call(
-        functools.partial(tables_kernel, parts, each),
-        grid_spec=pltpu.PrefetchScalarGridSpec(
-            num_scalar_prefetch=3,
-            grid=(1,),
-            in_specs=[whole(order), whole(freq)],
-            out_specs=[whole(o) for o in outs[:-1]] + [pl.BlockSpec(memory_space=pltpu.SMEM)],
-        ),
-        out_shape=outs,
-        compiler_params=params(),
-        cost_estimate=cost(1e8, 4e6),
-        name="tables",
-    )(jnp.reshape(part, (1,)).astype(I32), lengths[0], adapter_ids[0], order, freq)
-
-
 def per_device(
     tokens, cotangent, order, lengths, adapter_ids, norm_gains, w_query, w_key, w_value,
     b_query, b_key, b_value, w_out, w_gate, w_up, w_down, adapters, first_moment, second_moment,
@@ -1931,13 +1918,14 @@
     unit = 4 if own_rows % 4 == 0 else 1
     bias = jnp.concatenate([b_query, b_key, b_value, jnp.zeros((width - qh - 2 * kh,), BF16)])
     mine = (w_query.T, w_key.T, w_value.T, jnp.broadcast_to(bias[None], (16, width)))
-    moved, copies, *theirs = front(
+    moved, copies, *rest = front(
         tokens.reshape(devices, parts, piece, width),
         adapters.astype(BF16).reshape(own_rows // unit, unit, rank),
         *[a.reshape(2, a.shape[0] // 2, width) for a in mine],
-        devices,
+        order, lengths, adapter_ids, devices,
     )
-    theirs = [a.reshape(b.shape) for a, b in zip(theirs, mine)]
+    theirs = [a.reshape(b.shape) for a, b in zip(rest[:4], mine)]
+    turns, sines, meta_own, meta_other, meta_sorted, meta_rows, column, column_row, bounds = rest[4:]
     cotangent, moved = lax.optimization_barrier((cotangent, moved))
     moved = moved.reshape(local, width)
     dy_all = lax.all_to_all(
@@ -1952,9 +1940,6 @@
 
     early = 3 * width + qw + 2 * kw
     flat = copies.reshape(2 * devices * own_rows, rank)
-    (
-        turns, sines, meta_own, meta_other, meta_sorted, meta_rows, column, column_row, bounds,
-    ) = row_tables(order, lengths, adapter_ids, part, parts, each)
     gain_one = norm_gains[0:1].astype(F32)
     gain_two = norm_gains[1:2].astype(F32)
     side = jnp.reshape(part, (1,)).astype(I32)

time: 379 us -> 381 us (level)
  starting transfers between devices: 18.8 us -> 27.5 us
  Pallas kernels: 337 us -> 331 us
    all_to_all x1, starting transfers between devices: 9.42 us -> 14.4 us  [per_device(): lax.all_to_all(layer_rows.reshape(devices * parts, piece, width), ('dp',...]
    pallas_call x2 -> x1, Pallas kernels: 70.9 us -> 67.8 us  [front(): pl.pallas_call(functools.partial(front_kernel, devices, 2 * piece), in_sp...]
  transfers between devices with their start and end apart: 7 -> 7, of which waited for: 1 -> 2; matrix products, arithmetic and copies ran while one was open for 2% -> 2% of each run, Pallas kernels for 50% -> 47%
where the time goes in v3:
time: 381 us
  Pallas kernels  331 us (87%)
  starting transfers between devices  27.5 us (7%)
  local copies, waits for them, and re-layouts  10.6 us (3%)
  other arithmetic  6.34 us (2%)
  waiting for transfers between devices  4.57 us (1%)
    pallas_call x1, Pallas kernels, feed(): pl.pallas_call(feed_kernel, grid=(2 * count,), in_specs=[own_rows(n2), an...  83.3 us
    pallas_call x1, Pallas kernels, tail(): pl.pallas_call(functools.partial(tail_kernel, plan, early, key_width, dir...  79.5 us
    pallas_call x1, Pallas kernels, front(): pl.pallas_call(functools.partial(front_kernel, devices, 2 * piece), in_sp...  67.8 us
    pallas_call x1, Pallas kernels, attend_back(): pl.pallas_call(functools.partial(attend_back_kernel, heads, kv_heads), gr...  38.6 us
    pallas_call x1, Pallas kernels, attend(): pl.pallas_call(functools.partial(attend_kernel, heads, kv_heads), grid_sp...  25.3 us
    pallas_call x1, Pallas kernels, project(): pl.pallas_call(project_kernel, grid=(rows // tile,), in_specs=[row_blocks...  16.3 us
    all_to_all x1, starting transfers between devices, per_device(): lax.all_to_all(layer_rows.reshape(devices * parts, piece, width), ('dp',...  14.4 us
    pallas_call x1, Pallas kernels, middle_back(): pl.pallas_call(functools.partial(middle_back_kernel, plan, start), grid=(...  13 us
  transfers between devices with their start and end apart: 7, of which 2 were waited for; matrix products, arithmetic and copies ran while one was open for 2% of the time, Pallas kernels for 47%

profile of v3, /device:TPU:1, one launch (start us, length us, event | category | flops | bytes accessed | tf_op | source)
XLA Modules:
  0.0 380.8 jit_solution(382974948411354892)
XLA Ops:
  0.6 1.0 convert_element_type.21
  1.7 0.8 reshape.95.chunk_ref
  2.4 0.8 pad_maximum_fusion.1
  3.2 0.7 broadcast_in_dim.11.freq_ref
  3.9 0.6 reshape.99.bias_ref
  4.5 67.8 %front.1 = (bf16[16,48,896]{2,1,0:T(8,128)(2,1)}, bf16[5728,4,128]{2,1,0:T(4,128)(2,1)}, bf16[2,224,896]{2,1,0:T(8,128)(2,1)}, bf16[2,32,896]{2,1,0:T(8,128)(2,1...) custom-call(bf16[16,2,48,896]{3,2,1,0:T(8,128)(2,1)} %bitcast.48, ...), custom_call_target="tpu_custom_call" | custom-call | bytes 100000000 | tf_op jit(solution)/shard_map/front/pallas_call | solution.py:460
  72.3 5.5 %all-to-all-start = ((bf16[16,96,896]{2,1,0:T(8,128)(2,1)}), bf16[16,96,896]{2,1,0:T(8,128)(2,1)S(1)}, u32[]{:S(2)}, u32[]{:S(2)}) async-start(bf16[16,96,896]{2,1,0:T(8,128)(2,1)} %bitcast.46), calls=%async_computation | async-start | bytes 5505024 | tf_op jit(solution)/shard_map/all_to_all | solution.py:1931
  77.8 0.6 slice_convert_fusion
  78.4 0.6 broadcast_in_dim.24.mb_ref
  79.0 16.3 %project.1 = (bf16[768,896]{1,0:T(8,128)(2,1)}, bf16[768,896]{1,0:T(8,128)(2,1)}, bf16[768,256]{1,0:T(8,128)(2,1)}, bf16[768,384]{1,0:T(8,128)(2,1)}, f32[768,12...) custom-call(bf16[768,896]{1,0:T(8,128)(2,1)} %bitcast.35, ...), custom_call_target="tpu_custom_call" | custom-call | flops 2202009600 | bytes 9000000 | tf_op jit(solution)/shard_map/project/pallas_call | solution.py:610
  95.3 1.0 collective-permute-start
  96.3 25.3 %attend.1 = (bf16[768,896]{1,0:T(8,128)(2,1)}, bf16[768,896]{1,0:T(8,128)(2,1)}, f32[16,768]{1,0:T(8,128)}, bf16[1536,256]{1,0:T(8,128)(2,1)}, bf16[768,896]{1,0:T(8,128)(2,1)}) custom-call(s32[2,6]{1,0:T(2,128)} %get-tuple-element.63.bounds_ref, bf16[768,896]{1,0:T(8,128)(2,1)} %get-tuple-element.74.all_ref, s32[768,8]{1,0:T(8,128)} %get-tuple-element.75.meta_ref, ...), custom_call_target="tpu_custom_call" | custom-call | flops 33030144000 | bytes 6000000 | tf_op jit(solution)/shard_map/attend/pallas_call | solution.py:750
  121.6 7.1 %middle.1 = (f32[768,896]{1,0:T(8,128)}, bf16[768,896]{1,0:T(8,128)(2,1)}, bf16[768,128]{1,0:T(8,128)(2,1)}, bf16[896,1024]{1,0:T(8,128)(2,1)}) custom-call(s32[1]{0:T(128)} %bitcast.part_ref, bf16[768,896]{1,0:T(8,128)(2,1)} %get-tuple-element.81.o_ref, bf16[768,896]{1,0:T(8,128)(2,1)} %bitcast.36, s32[768,8]{1,0:T(8,128)} %get-tuple-element.66.meta_ref.refs_6_, ...), custom_call_target="tpu_custom_call" | custom-call | flops 1513881600 | bytes 12000000 | tf_op jit(solution)/shard_map/middle/pallas_call | solution.py:967
  128.7 1.9 all-to-all-done
  130.7 1.8 constant_dynamic-slice_fusion.1
  132.5 83.3 %feed.1 = (f32[768,896]{1,0:T(8,128)}, f32[768,896]{1,0:T(8,128)}, bf16[1,256,896]{2,1,0:T(8,128)(2,1)}, bf16[3,256,896]{2,1,0:T(8,128)(2,1)}, bf16[2,256,896]{2,1,0:T(8,128)(2,1)}, /*index=5*/bf16[22976,128]{1,0:T(8,128)(2,1)}) custom-call(bf16[768,896]{1,0:T(8,128)(2,1)} %get-tuple-element.84.n_ref.n_hbm, bf16[768,896]{1,0:T(8,128)(2,1)} %get-tuple-element.84.n_ref.n_hbm, ...), custom_call_target="tpu_custom_call" | custom-call | flops 48771366912 | bytes 40000000 | tf_op jit(solution)/shard_map/feed/pallas_call | solution.py:1405
  215.8 1.4 collective-permute-start.1
  217.2 13.0 %middle_back.1 = (f32[768,896]{1,0:T(8,128)}, bf16[768,896]{1,0:T(8,128)(2,1)}, bf16[1792,128]{1,0:T(8,128)(2,1)}, f32[3,736,128]{2,1,0:T(8,128)}, bf16[3,736,12...) custom-call(f32[768,896]{1,0:T(8,128)} %get-tuple-element.90.da_ref, ...), custom_call_target="tpu_custom_call" | custom-call | flops 2064384000 | bytes 20000000 | tf_op jit(solution)/shard_map/middle_back/pallas_call | solution.py:1124
  230.2 4.0 %collective-permute-start.2 = (bf16[3,736,128]{2,1,0:T(8,128)(2,1)}, bf16[3,736,128]{2,1,0:T(8,128)(2,1)}, u32[]{:S(2)}, u32[]{:S(2)}) collective-permute-start(bf16[3,736,128]{2,1,0:T(8,128)(2,1)} %get-tuple-element.114), channel_id=1, source_target_pairs={{0,4},{1,5},{2,6},{3,7},{4,0},{5,1},{6,2},{7,3},{8,12},{9,13},{10,... | collective-permute-start | bytes 1695752 | tf_op jit(solution)/shard_map/ppermute | solution.py:1976
  234.2 0.9 collective-permute-start.3
  235.1 0.4 collective-permute-start.4
  235.5 2.6 collective-permute-done.1
  238.3 0.6 fusion.1
  238.9 1.7 broadcast_in_dim.26
  240.7 14.4 %all-to-all-start.1 = ((bf16[32,48,896]{2,1,0:T(8,128)(2,1)}), bf16[32,48,896]{2,1,0:T(8,128)(2,1)S(1)}, u32[]{:S(2)}, u32[]{:S(2)}) async-start(bf16[32,48,896]{2,1,0:T(8,128)(2,1)} %bitcast.40), calls=%async_computation.1 | async-start | bytes 5505024 | tf_op jit(solution)/shard_map/all_to_all | solution.py:1980
  255.1 38.6 %attend_back.1 = (bf16[768,896]{1,0:T(8,128)(2,1)}, bf16[768,256]{1,0:T(8,128)(2,1)}, bf16[768,256]{1,0:T(8,128)(2,1)}) custom-call(s32[2,6]{1,0:T(2,128)} %get-tuple-element.63.bounds_ref, bf16[768,896]{1,0:T(8,128)(2,1)} %get-tuple-element.97.q_ref, bf16[768,896]{1,0:T(8,128)(2,1)} %get-tuple-element.98.all_ref, bf16[768,896]{1,0:T(8,128)(2,1)} %get-tuple-element.99.o_ref, ...), custom_call_target="tpu_custom_call" | custom-call | flops 49545216000 | bytes 9000000 | tf_op jit(solution)/shard_map/attend_back/pallas_call | solution.py:891
  293.7 79.5 %tail.1 = (bf16[16,2,48,896]{3,2,1,0:T(8,128)(2,1)}, f32[736,128]{1,0:T(8,128)}) custom-call(bf16[768,896]{1,0:T(8,128)(2,1)} %get-tuple-element.103.refs_0_, bf16[768,256]{1,0:T(8,128)(2,1)} %get-tuple-element.104.refs_1_, bf16[768,896]{1,0:T(8,128)(2,1)} %bitcast.37, bf16[768,896]{1,0:T(8,128)(2,1)} %get-tuple-element.105.refs_3_, ...), custom_call_target="tpu_custom_call" | custom-call | flops 3991142400 | bytes 200000000 | tf_op jit(solution)/shard_map/tail/pallas_call | solution.py:1868
  373.3 2.3 fusion.3
  375.6 0.9 broadcast_multiply_fusion
  376.5 1.5 copy.28
  378.0 1.2 copy-done.2
  379.2 1.5 copy.29
  (25 shorter events, 0.2 us)
Async XLA Ops:
  72.3 5.5 %copy-start.8 = (bf16[2,896]{1,0:T(2,128)(2,1)S(1)}, bf16[2,896]{1,0:T(2,128)(2,1)}, u32[]{:S(2)}) copy-start(bf16[2,896]{1,0:T(2,128)(2,1)} %param.24) | copy-start | bytes 10756
  72.3 58.4 %all-to-all-start = ((bf16[16,96,896]{2,1,0:T(8,128)(2,1)}), bf16[16,96,896]{2,1,0:T(8,128)(2,1)S(1)}, u32[]{:S(2)}, u32[]{:S(2)}) async-start(bf16[16,96,896]{2,1,0:T(8,128)(2,1)} %bitcast.46), calls=%async_computation | async-start | bytes 5505024 | tf_op jit(solution)/shard_map/all_to_all | solution.py:1931
  79.0 16.3 %copy-start.6 = (bf16[448,896]{1,0:T(8,128)(2,1)S(1)}, bf16[448,896]{1,0:T(8,128)(2,1)}, u32[]{:S(2)}) copy-start(bf16[448,896]{1,0:T(8,128)(2,1)} %mine_ref) | copy-start | bytes 2408452
  95.3 26.3 %collective-permute-start = (bf16[448,896]{1,0:T(8,128)(2,1)S(1)}, bf16[448,896]{1,0:T(8,128)(2,1)}, u32[]{:S(2)}, u32[]{:S(2)}) collective-permute-start(bf16[448,896]{1,0:T(8,128)(2,1)S(1)} %copy-done.6), channel_id=1, source_target_pairs={{0,1},{1,0},{2,3},{3,2},{4,5},{5,4},{6,7},{7,6},{8,9},{9,8},{10,11... | collective-permute-start | bytes 2408456 | tf_op jit(solution)/shard_map/ppermute | solution.py:1901
  215.8 22.3 %collective-permute-start.1 = (bf16[2,256,896]{2,1,0:T(8,128)(2,1)}, bf16[2,256,896]{2,1,0:T(8,128)(2,1)S(1)}, u32[]{:S(2)}, u32[]{:S(2)}) collective-permute-start(bf16[2,256,896]{2,1,0:T(8,128)(2,1)} %get-tuple-element.89), channel_id=1, source_target_pairs={{0,1},{1,0},{2,3},{3,2},{4,5},{5,4},{6,7},{7,6},{8,9},{9,8},{10,11... | collective-permute-start | bytes 2752520 | tf_op jit(solution)/shard_map/ppermute | solution.py:1901
  217.2 20.9 %copy-start.7 = (bf16[1,256,896]{2,1,0:T(8,128)(2,1)S(1)}, bf16[1,256,896]{2,1,0:T(8,128)(2,1)}, u32[]{:S(2)}) copy-start(bf16[1,256,896]{2,1,0:T(8,128)(2,1)} %get-tuple-element.88) | copy-start | bytes 1376260
  217.2 21.1 %copy-start.1 = (f32[768,896]{1,0:T(8,128)S(1)}, f32[768,896]{1,0:T(8,128)}, u32[]{:S(2)}) copy-start(f32[768,896]{1,0:T(8,128)} %get-tuple-element.87) | copy-start | bytes 8257540
  230.2 8.0 %copy-start = (f32[768,896]{1,0:T(8,128)S(1)}, f32[768,896]{1,0:T(8,128)}, u32[]{:S(2)}) copy-start(f32[768,896]{1,0:T(8,128)} %get-tuple-element.83.y1_ref) | copy-start | bytes 8257540
  230.2 63.4 %collective-permute-start.2 = (bf16[3,736,128]{2,1,0:T(8,128)(2,1)}, bf16[3,736,128]{2,1,0:T(8,128)(2,1)}, u32[]{:S(2)}, u32[]{:S(2)}) collective-permute-start(bf16[3,736,128]{2,1,0:T(8,128)(2,1)} %get-tuple-element.114), channel_id=1, source_target_pairs={{0,4},{1,5},{2,6},{3,7},{4,0},{5,1},{6,2},{7,3},{8,12},{9,13},{10,... | collective-permute-start | bytes 1695752 | tf_op jit(solution)/shard_map/ppermute | solution.py:1976
  234.2 59.5 %collective-permute-start.3 = (bf16[3,736,128]{2,1,0:T(8,128)(2,1)}, bf16[3,736,128]{2,1,0:T(8,128)(2,1)}, u32[]{:S(2)}, u32[]{:S(2)}) collective-permute-start(bf16[3,736,128]{2,1,0:T(8,128)(2,1)} %get-tuple-element.115), channel_id=1, source_target_pairs={{0,1},{1,0},{2,3},{3,2},{4,5},{5,4},{6,7},{7,6},{8,9},{9,8},{10,11... | collective-permute-start | bytes 1695752 | tf_op jit(solution)/shard_map/ppermute | solution.py:1976
  235.1 58.6 %collective-permute-start.4 = (bf16[3,736,128]{2,1,0:T(8,128)(2,1)}, bf16[3,736,128]{2,1,0:T(8,128)(2,1)}, u32[]{:S(2)}, u32[]{:S(2)}) collective-permute-start(bf16[3,736,128]{2,1,0:T(8,128)(2,1)} %get-tuple-element.116), channel_id=1, source_target_pairs={{0,5},{1,4},{2,7},{3,6},{4,1},{5,0},{6,3},{7,2},{8,13},{9,12},{10,... | collective-permute-start | bytes 1695752 | tf_op jit(solution)/shard_map/ppermute | solution.py:1976
  240.7 135.8 %all-to-all-start.1 = ((bf16[32,48,896]{2,1,0:T(8,128)(2,1)}), bf16[32,48,896]{2,1,0:T(8,128)(2,1)S(1)}, u32[]{:S(2)}, u32[]{:S(2)}) async-start(bf16[32,48,896]{2,1,0:T(8,128)(2,1)} %bitcast.40), calls=%async_computation.1 | async-start | bytes 5505024 | tf_op jit(solution)/shard_map/all_to_all | solution.py:1980
  293.7 79.6 %copy-start.3 = (f32[716,128]{1,0:T(8,128)S(1)}, f32[716,128]{1,0:T(8,128)}, u32[]{:S(2)}) copy-start(f32[716,128]{1,0:T(8,128)} %param.35) | copy-start | bytes 1099780
  293.7 79.6 %copy-start.4 = (f32[716,128]{1,0:T(8,128)S(1)}, f32[716,128]{1,0:T(8,128)}, u32[]{:S(2)}) copy-start(f32[716,128]{1,0:T(8,128)} %param.36) | copy-start | bytes 1099780
  375.6 2.4 copy-start.5
  376.5 2.8 copy-start.2
